TPU v7x, 32 devices: a whole 2x2x4 slice. The times are simulated.
32 devices in a mesh: dp: 8 (over z, x), outer: 4 (over y, core).
Axes of the slice: x: 2, y: 2, z: 4, core: 2. Of those that a mesh axis runs over, the one named last changes fastest.
Arguments:
- text_rows: bfloat16 [32, 512, 768], P(('dp', 'outer')), may hold values from -6 to 6
- text_segments: int32 [32, 512], P(('dp', 'outer')), may hold values from 0 to 3, never falling along the last dimension, each value on 1 to 256 neighbouring positions
- positives: int32 [64], replicated, may hold values from 0 to 63
- w_mix: bfloat16 [768, 4608], P('dp'), may hold values from -0.21875 to 0.21875
- w_proj: bfloat16 [768, 1536], P('dp'), may hold values from -0.875 to 0.875
- w_up: bfloat16 [768, 6144], P('dp'), may hold values from -0.21875 to 0.21875
- w_down: bfloat16 [3072, 1536], P('dp'), may hold values from -0.109375 to 0.109375
- b_up: bfloat16 [3072, 2], P('dp'), may hold values from -1 to 1
- b_rows: bfloat16 [768, 12], P('dp'), may hold values from -1 to 1
- g_rows: bfloat16 [768, 4], P('dp'), may hold values from 0.5 to 1.5
Outputs:
- encoded: bfloat16 [32, 512, 768], P(('dp', 'outer'))
- row_grads: float32 [32, 512, 768], P(('dp', 'outer'))
- grad_mix: float32 [768, 4608], P('dp')
- grad_proj: float32 [768, 1536], P('dp')
- grad_up: float32 [768, 6144], P('dp')
- grad_down: float32 [3072, 1536], P('dp')
- grad_up_bias: float32 [3072, 2], P('dp')
- grad_biases: float32 [768, 12], P('dp')
- grad_gains: float32 [768, 4], P('dp')
Inputs may be any that keep to these rules, and one draw needn't show every extreme that they name: `text_segments`: within each row segment numbers never fall, every number 0 to 3 occurs, and no segment has more than 256 tokens.
All inputs are finite; a program needn't handle non-finite values.
Results may differ from a plain program's by a relative error of at most 0.023.
Values may be sent and summed in bfloat16 or wider, within the bound.
A program may use at most 256 MiB of HBM per device.

v0:
```python
import jax
import jax.numpy as jnp
from jax import lax
from jax.sharding import PartitionSpec as P

D = 768
HEADS = 12
HEAD_DIM = 64
FF = 3072
SEGS = 4


masked_score = -1e30
layer_eps = 1e-05


def norm_rows(inputs, gain_row, offset):
    center = inputs - jnp.mean(inputs, axis=-1, keepdims=True)
    spread = jnp.mean(center * center, axis=-1, keepdims=True)
    return center * lax.rsqrt(spread + layer_eps) * gain_row + offset


def gelu_exact(inputs):
    return jax.nn.gelu(inputs, approximate=False)


def dot_plain(left_mat, right_mat):
    return jnp.dot(left_mat, right_mat, preferred_element_type=jnp.float32)


def dot_over_rows(left_mat, right_mat):
    return lax.dot_general(
        left_mat, right_mat, (((0,), (0,)), ((), ())), preferred_element_type=jnp.float32
    )


def dot_over_columns(left_mat, right_mat):
    return lax.dot_general(
        left_mat, right_mat, (((1,), (1,)), ((), ())), preferred_element_type=jnp.float32
    )


def cls_starts(segments):
    levels = jnp.arange(SEGS, dtype=jnp.int32)
    return jnp.sum((segments[None, :] < levels[:, None]).astype(jnp.int32), axis=1)


def split_tower(gathered, tower_index):
    w_mix, w_proj, w_up, w_down, b_up, b_rows, g_rows = gathered
    model_width = w_mix.shape[0]
    hidden = w_down.shape[0]
    return (
        lax.dynamic_slice_in_dim(w_mix, 3 * tower_index * model_width, 3 * model_width, 1),
        lax.dynamic_slice_in_dim(w_proj, tower_index * model_width, model_width, 1),
        lax.dynamic_slice_in_dim(w_up, tower_index * hidden, hidden, 1),
        lax.dynamic_slice_in_dim(w_down, tower_index * model_width, model_width, 1),
        lax.dynamic_slice_in_dim(b_up, tower_index, 1, 1)[:, 0].astype(jnp.float32),
        lax.dynamic_slice_in_dim(b_rows, 6 * tower_index, 6, 1).T.astype(jnp.float32),
        lax.dynamic_slice_in_dim(g_rows, 2 * tower_index, 2, 1).T.astype(jnp.float32),
    )


def encode_row(rows_in, segments, weights_one):
    w_mix, w_proj, w_up, w_down, b_up, b_rows, g_rows = weights_one
    row_len = rows_in.shape[0]
    model_width = rows_in.shape[1]
    scaled = HEAD_DIM ** (-0.5)
    mixed_rows = dot_plain(rows_in, w_mix) + jnp.concatenate(
        [b_rows[0], jnp.zeros_like(b_rows[0]), b_rows[1]]
    )
    mixed_low = mixed_rows.astype(jnp.bfloat16)
    queries = mixed_low[:, :model_width].reshape(row_len, HEADS, HEAD_DIM)
    key_rows = mixed_low[:, model_width : 2 * model_width].reshape(row_len, HEADS, HEAD_DIM)
    values = mixed_low[:, 2 * model_width :].reshape(row_len, HEADS, HEAD_DIM)
    allowed = segments[:, None] == segments[None, :]
    scores = (
        jnp.einsum("qhe,khe->hqk", queries, key_rows, preferred_element_type=jnp.float32) * scaled
    )
    scores = jnp.where(allowed[None], scores, masked_score)
    top_score = jnp.max(scores, axis=-1, keepdims=True)
    log_total = top_score + jnp.log(jnp.sum(jnp.exp(scores - top_score), axis=-1, keepdims=True))
    chances_low = jnp.exp(scores - log_total).astype(jnp.bfloat16)
    attended = jnp.einsum("hqk,khe->qhe", chances_low, values, preferred_element_type=jnp.float32)
    attended_low = attended.reshape(row_len, model_width).astype(jnp.bfloat16)
    before_one = rows_in.astype(jnp.float32) + dot_plain(attended_low, w_proj) + b_rows[2]
    normed_one = norm_rows(before_one, g_rows[0], b_rows[3])
    normed_low = normed_one.astype(jnp.bfloat16)
    up_pre = dot_plain(normed_low, w_up) + b_up
    gelu_low = gelu_exact(up_pre).astype(jnp.bfloat16)
    before_two = normed_one + dot_plain(gelu_low, w_down) + b_rows[4]
    encoded = norm_rows(before_two, g_rows[1], b_rows[5])
    return (
        encoded,
        (mixed_low, log_total, attended_low, before_one, normed_low, up_pre, gelu_low, before_two),
    )


def attention_back(mixed_low, log_total, segments, d_attended):
    model_width = d_attended.shape[1]
    row_len = d_attended.shape[0]
    scaled = HEAD_DIM ** (-0.5)
    pair_width = 2 * HEAD_DIM
    allowed = segments[:, None] == segments[None, :]

    def one_pair(pair_index):
        col_start = pair_index * pair_width
        queries = lax.dynamic_slice_in_dim(mixed_low, col_start, pair_width, 1).reshape(
            row_len, 2, HEAD_DIM
        )
        key_rows = lax.dynamic_slice_in_dim(
            mixed_low, model_width + col_start, pair_width, 1
        ).reshape(row_len, 2, HEAD_DIM)
        values = lax.dynamic_slice_in_dim(
            mixed_low, 2 * model_width + col_start, pair_width, 1
        ).reshape(row_len, 2, HEAD_DIM)
        d_out_pair = lax.dynamic_slice_in_dim(d_attended, col_start, pair_width, 1).reshape(
            row_len, 2, HEAD_DIM
        )
        pair_total = lax.dynamic_slice_in_dim(log_total, pair_index * 2, 2, 0)
        scores = (
            jnp.einsum("qhe,khe->hqk", queries, key_rows, preferred_element_type=jnp.float32)
            * scaled
        )
        scores = jnp.where(allowed[None], scores, masked_score)
        chances = jnp.exp(scores - pair_total)
        chances_low = chances.astype(jnp.bfloat16)
        d_values = jnp.einsum(
            "hqk,qhe->khe", chances_low, d_out_pair, preferred_element_type=jnp.float32
        )
        d_chances = jnp.einsum(
            "qhe,khe->hqk", d_out_pair, values, preferred_element_type=jnp.float32
        )
        d_scores = chances * (d_chances - jnp.sum(chances * d_chances, axis=-1, keepdims=True))
        d_scores = d_scores.astype(jnp.bfloat16)
        d_queries = (
            jnp.einsum("hqk,khe->qhe", d_scores, key_rows, preferred_element_type=jnp.float32)
            * scaled
        )
        d_keys = (
            jnp.einsum("hqk,qhe->khe", d_scores, queries, preferred_element_type=jnp.float32)
            * scaled
        )
        return (
            d_queries.reshape(row_len, pair_width).astype(jnp.bfloat16),
            d_keys.reshape(row_len, pair_width).astype(jnp.bfloat16),
            d_values.reshape(row_len, pair_width).astype(jnp.bfloat16),
        )

    pieces = lax.map(one_pair, jnp.arange(HEADS // 2, dtype=jnp.int32))

    def to_rows(stacked):
        return jnp.moveaxis(stacked, 0, 1).reshape(row_len, model_width)

    return jnp.concatenate([to_rows(pieces[0]), to_rows(pieces[1]), to_rows(pieces[2])], axis=1)


def backprop(rows_in, segments, weights_one, row_state, grad_out):
    w_mix, w_proj, w_up, w_down, b_up, b_rows, g_rows = weights_one
    mixed_low, log_total, attended_low, before_one, normed_low, up_pre, gelu_low, before_two = (
        row_state
    )
    model_width = rows_in.shape[1]
    second_norm, second_back = jax.vjp(norm_rows, before_two, g_rows[1], b_rows[5])
    d_before_two, d_gain_two, d_offset_two = second_back(grad_out)
    ffn_low = d_before_two.astype(jnp.bfloat16)
    d_down = dot_over_rows(gelu_low, ffn_low)
    d_down_bias = jnp.sum(ffn_low.astype(jnp.float32), axis=0)
    d_gelu = dot_over_columns(ffn_low, w_down)
    gelu_out, gelu_back = jax.vjp(gelu_exact, up_pre)
    up_low = gelu_back(d_gelu)[0].astype(jnp.bfloat16)
    d_up = dot_over_rows(normed_low, up_low)
    d_up_bias = jnp.sum(up_low.astype(jnp.float32), axis=0)
    d_normed = d_before_two + dot_over_columns(up_low, w_up)
    first_norm, first_back = jax.vjp(norm_rows, before_one, g_rows[0], b_rows[3])
    d_before_one, d_gain_one, d_offset_one = first_back(d_normed)
    proj_low = d_before_one.astype(jnp.bfloat16)
    d_proj = dot_over_rows(attended_low, proj_low)
    d_proj_bias = jnp.sum(proj_low.astype(jnp.float32), axis=0)
    d_attended = dot_over_columns(proj_low, w_proj).astype(jnp.bfloat16)
    d_mixed = attention_back(mixed_low, log_total, segments, d_attended)
    d_mix = dot_over_rows(rows_in, d_mixed)
    d_mixed_wide = d_mixed.astype(jnp.float32)
    d_query_bias = jnp.sum(d_mixed_wide[:, :model_width], axis=0)
    d_value_bias = jnp.sum(d_mixed_wide[:, 2 * model_width :], axis=0)
    d_rows = d_before_one + dot_over_columns(d_mixed, w_mix)
    d_biases = jnp.stack(
        [d_query_bias, d_value_bias, d_proj_bias, d_offset_one, d_down_bias, d_offset_two], axis=1
    )
    d_gains = jnp.stack([d_gain_one, d_gain_two], axis=1)
    return (d_rows, (d_mix, d_proj, d_up, d_down, d_up_bias[:, None], d_biases, d_gains))


def softmax_minus(logits, targets):
    top_logit = jnp.max(logits, axis=1, keepdims=True)
    raised = jnp.exp(logits - top_logit)
    chances = raised / jnp.sum(raised, axis=1, keepdims=True)
    columns = jnp.arange(logits.shape[1], dtype=jnp.int32)
    target_hits = (targets[:, None] == columns[None, :]).astype(jnp.float32)
    return (chances - target_hits).astype(jnp.bfloat16)


def place_tower(whole_shape, term, begin):
    return lax.dynamic_update_slice_in_dim(jnp.zeros(whole_shape, jnp.float32), term, begin, 1)


def per_device(
    text_rows, text_segments, positives, w_mix, w_proj, w_up, w_down, b_up, b_rows, g_rows
):
    gathered = (
        lax.all_gather(w_mix, "dp", axis=0, tiled=True),
        lax.all_gather(w_proj, "dp", axis=0, tiled=True),
        lax.all_gather(w_up, "dp", axis=0, tiled=True),
        lax.all_gather(w_down, "dp", axis=0, tiled=True),
        lax.all_gather(b_up, "dp", axis=0, tiled=True),
        lax.all_gather(b_rows, "dp", axis=0, tiled=True),
        lax.all_gather(g_rows, "dp", axis=0, tiled=True),
    )
    own_index = lax.axis_index(("dp", "outer"))
    tower_index = own_index * 2 // lax.axis_size(("dp", "outer"))
    weights_one = split_tower(gathered, tower_index)
    row_index = 0
    result, saved_state = encode_row(text_rows[row_index], text_segments[row_index], weights_one)
    starts = cls_starts(text_segments[row_index])
    encoded_rows = [result.astype(jnp.bfloat16)]
    kept_rows = [saved_state]
    starts_rows = [starts]
    vectors = jnp.take(result, starts, axis=0).astype(jnp.bfloat16)
    local_count = vectors.shape[0]
    pair_scale = 2.0 * D ** (-0.5)
    all_cls = lax.all_gather(vectors, ("dp", "outer"), axis=0, tiled=True)
    texts = all_cls.shape[0] // 2
    all_queries = all_cls[:texts]
    all_passages = all_cls[texts:]
    logits = dot_over_columns(all_queries, all_passages) * pair_scale
    d_logits = softmax_minus(logits, positives)
    position = own_index * local_count - tower_index * texts
    own_rows = lax.dynamic_slice_in_dim(d_logits, position, local_count, 0)
    own_columns = lax.dynamic_slice_in_dim(d_logits, position, local_count, 1)
    d_query_cls = dot_plain(own_rows, all_passages)
    d_passage_cls = dot_over_rows(own_columns, all_queries)
    d_own_cls = jnp.where(tower_index == 0, d_query_cls, d_passage_cls) * pair_scale
    row_index = 0
    rows_in = text_rows[row_index]
    segments = text_segments[row_index]
    row_state = kept_rows[row_index]
    row_len = rows_in.shape[0]
    grad_out = jnp.zeros((row_len, D), jnp.float32).at[starts_rows[row_index]].set(d_own_cls)
    d_rows, row_terms = backprop(rows_in, segments, weights_one, row_state, grad_out)
    input_grads = [d_rows]
    g_all = (
        place_tower(gathered[0].shape, row_terms[0], 3 * tower_index * D),
        place_tower(gathered[1].shape, row_terms[1], tower_index * D),
        place_tower(gathered[2].shape, row_terms[2], tower_index * FF),
        place_tower(gathered[3].shape, row_terms[3], tower_index * D),
        place_tower(gathered[4].shape, row_terms[4], tower_index),
        place_tower(gathered[5].shape, row_terms[5], 6 * tower_index),
        place_tower(gathered[6].shape, row_terms[6], 2 * tower_index),
    )
    s_mix, s_proj, s_up, s_down, s_up_bias, s_biases, s_gains = (
        lax.psum_scatter(
            g_all[0].astype(jnp.bfloat16), "dp", scatter_dimension=0, tiled=True
        ).astype(jnp.float32),
        lax.psum_scatter(
            g_all[1].astype(jnp.bfloat16), "dp", scatter_dimension=0, tiled=True
        ).astype(jnp.float32),
        lax.psum_scatter(
            g_all[2].astype(jnp.bfloat16), "dp", scatter_dimension=0, tiled=True
        ).astype(jnp.float32),
        lax.psum_scatter(
            g_all[3].astype(jnp.bfloat16), "dp", scatter_dimension=0, tiled=True
        ).astype(jnp.float32),
        lax.psum_scatter(
            g_all[4].astype(jnp.bfloat16), "dp", scatter_dimension=0, tiled=True
        ).astype(jnp.float32),
        lax.psum_scatter(
            g_all[5].astype(jnp.bfloat16), "dp", scatter_dimension=0, tiled=True
        ).astype(jnp.float32),
        lax.psum_scatter(
            g_all[6].astype(jnp.bfloat16), "dp", scatter_dimension=0, tiled=True
        ).astype(jnp.float32),
    )
    totals = (
        lax.psum(s_mix.astype(jnp.bfloat16), "outer").astype(jnp.float32),
        lax.psum(s_proj.astype(jnp.bfloat16), "outer").astype(jnp.float32),
        lax.psum(s_up.astype(jnp.bfloat16), "outer").astype(jnp.float32),
        lax.psum(s_down.astype(jnp.bfloat16), "outer").astype(jnp.float32),
        lax.psum(s_up_bias.astype(jnp.bfloat16), "outer").astype(jnp.float32),
        lax.psum(s_biases.astype(jnp.bfloat16), "outer").astype(jnp.float32),
        lax.psum(s_gains.astype(jnp.bfloat16), "outer").astype(jnp.float32),
    )
    return (
        jnp.stack(encoded_rows),
        jnp.stack(input_grads),
        totals[0],
        totals[1],
        totals[2],
        totals[3],
        totals[4],
        totals[5],
        totals[6],
    )


def solution(mesh):
    return jax.shard_map(
        per_device,
        mesh=mesh,
        in_specs=(
            P(("dp", "outer"), None, None),
            P(("dp", "outer"), None),
            P(),
            P("dp", None),
            P("dp", None),
            P("dp", None),
            P("dp", None),
            P("dp", None),
            P("dp", None),
            P("dp", None),
        ),
        out_specs=(
            P(("dp", "outer"), None, None),
            P(("dp", "outer"), None, None),
            P("dp", None),
            P("dp", None),
            P("dp", None),
            P("dp", None),
            P("dp", None),
            P("dp", None),
            P("dp", None),
        ),
        check_vma=False,
    )
```

profile of v0, /device:TPU:1, one launch (start us, length us, event | category | flops | bytes accessed | tf_op | source)
XLA Modules:
  0.0 1347.6 jit_solution(744836415622316761)
XLA Ops:
  10.1 25.4 %all-gather = bf16[8,96,12]{1,2,0:T(8,128)(2,1)S(1)} all-gather(bf16[1,96,12]{1,2,0:T(8,128)(2,1)S(1)} %bitcast.166), channel_id=1, replica_groups=mesh['dp'=8,'outer'=4] {'dp'}, dimensions={0}, use_global_device_ids=true | all-gather | bytes 20736 | tf_op jit(solution)/shard_map/all_gather | solution.py:215
  35.7 17.3 %all-gather.1 = bf16[8,96,4]{1,2,0:T(4,128)(2,1)S(1)} all-gather(bf16[1,96,4]{1,2,0:T(4,128)(2,1)S(1)} %bitcast.167), channel_id=1, replica_groups=mesh['dp'=8,'outer'=4] {'dp'}, dimensions={0}, use_global_device_ids=true | all-gather | bytes 6912 | tf_op jit(solution)/shard_map/all_gather | solution.py:216
  53.1 22.3 %all_gather.29 = bf16[3072,2]{0,1:T(2,128)(2,1)S(1)} all-gather(bf16[384,2]{0,1:T(2,128)(2,1)S(1)} %copy-done.40), channel_id=1, replica_groups=mesh['dp'=8,'outer'=4] {'dp'}, dimensions={0}, use_global_device_ids=true | all-gather | bytes 13824 | tf_op jit(solution)/shard_map/all_gather | solution.py:214
  76.0 45.1 %all-gather.8.cloned.1.call-done = bf16[768,4608]{1,0:T(8,128)(2,1)} async-done(((bf16[96,4608]{1,0:T(8,128)(2,1)}), bf16[768,4608]{1,0:T(8,128)(2,1)}) %all-gather.8.cloned.1.call-update) | async-done | bytes 7077904 | tf_op jit(solution)/shard_map/all_gather | solution.py:210
  121.2 4.3 fusion.23
  125.7 1.2 copy-done.3
  126.9 2.1 fusion.5
  129.0 2.6 exponential_reduce_fusion
  131.6 4.2 fusion.29
  135.8 37.0 %all-gather.10.cloned.1.call-done = bf16[768,1536]{1,0:T(8,128)(2,1)} async-done(((bf16[96,1536]{1,0:T(8,128)(2,1)}), bf16[768,1536]{1,0:T(8,128)(2,1)}) %all-gather.10.cloned.1.call-update) | async-done | bytes 2359312 | tf_op jit(solution)/shard_map/all_gather | solution.py:211
  172.8 2.6 fusion.70
  175.8 136.6 %all-gather.12.cloned.1.call-done = bf16[768,6144]{1,0:T(8,128)(2,1)} async-done(((bf16[96,6144]{1,0:T(8,128)(2,1)}), bf16[768,6144]{1,0:T(8,128)(2,1)}) %all-gather.12.cloned.1.call-update) | async-done | bytes 9437200 | tf_op jit(solution)/shard_map/all_gather | solution.py:212
  312.4 19.7 %multiply_convert_fusion.1 = (bf16[512,3072]{1,0:T(8,128)(2,1)}, f32[512,3072]{1,0:T(8,128)}, f32[512,3072]{1,0:T(8,128)}) fusion(f32[3072]{0:T(1024)S(1)} %bitcast.164, bf16[768,6144]{1,0:T(8,128)(2,1)} %all-gather.12.cloned.1.call-done, s32[]{:T(128)S(6)} %select_n.111, f32[512,768]{1,0:T(8,128)S(1)} %get-tuple-element.251, ...), kind=kOutput, calls=%fused_computation.31 | convolution fusion | flops 2521694208 | bytes 22042628 | tf_op jit(solution)/shard_map/dot_general | solution.py:28
  332.1 118.6 %all-gather.14.cloned.1.call-done = bf16[3072,1536]{1,0:T(8,128)(2,1)} async-done(((bf16[384,1536]{1,0:T(8,128)(2,1)}), bf16[3072,1536]{1,0:T(8,128)(2,1)}) %all-gather.14.cloned.1.call-update) | async-done | bytes 9437200 | tf_op jit(solution)/shard_map/all_gather | solution.py:213
  450.7 6.0 fusion.71
  458.1 40.0 %all-gather.2 = bf16[32,4,768]{2,1,0:T(4,128)(2,1)S(1)} all-gather(bf16[1,4,768]{2,1,0:T(4,128)(2,1)S(1)} %fusion.47), channel_id=1, replica_groups=mesh['dp'=8,'outer'=4] {'dp','outer'}, dimensions={0}, use_global_device_ids=true | all-gather | bytes 202752 | tf_op jit(solution)/shard_map/all_gather | solution.py:230
  498.9 1.0 scatter_custom_fusion
  499.9 1.1 multiply_reduce_fusion.1
  502.4 21.9 %convert_reduce_fusion = (f32[3072]{0:T(1024)}, bf16[512,3072]{1,0:T(8,128)(2,1)S(1)}) fusion(f32[512,3072]{1,0:T(8,128)} %get-tuple-element.235, bf16[512,768]{1,0:T(8,128)(2,1)S(1)} %get-tuple-element.227, bf16[3072,1536]{1,0:T(8,128)(2,1)} %all-gather.14.cloned.1.call-done, s32[]{:T(128)S(6)} %select_n.109, f32[512,3072]{1,0:T(8,128)} %get-tuple-element.252, ...), kind=kOutput, calls=%fused_computation.29 | convolution fusion | flops 2442654720 | bytes 21258244 | tf_op jit(solution)/shard_map/dot_general | solution.py:38
  524.4 3.7 multiply_reduce_fusion.2
  531.4 1.4 copy-done.2
  532.8 2.1 convolution_convert_fusion.1
  535.0 43.2 %while.17 = (s32[]{:T(128)}, bf16[6,512,128]{1,2,0:T(8,128)(2,1)S(1)}, bf16[6,512,128]{1,2,0:T(8,128)(2,1)}, bf16[6,512,128]{1,2,0:T(8,128)(2,1)}, s32[6]{0:T(12...) while((s32[]{:T(128)}, ...), condition=%wide.region_16.17_spmd.clone, body=%wide.region_14.16_spmd.clone.sunk | while | flops 340851712 | bytes 25975256 | solution.py:149
  536.3 1.1 constant_dynamic-slice_fusion.9
  538.8 0.9 multiply_reduce_fusion.8
  543.5 1.1 constant_dynamic-slice_fusion.9
  546.1 0.9 multiply_reduce_fusion.8
  550.7 1.1 constant_dynamic-slice_fusion.9
  553.2 0.9 multiply_reduce_fusion.8
  557.9 1.1 constant_dynamic-slice_fusion.9
  560.5 0.9 multiply_reduce_fusion.8
  565.1 1.1 constant_dynamic-slice_fusion.9
  567.6 0.9 multiply_reduce_fusion.8
  572.3 1.1 constant_dynamic-slice_fusion.9
  574.8 0.9 multiply_reduce_fusion.8
  578.2 0.9 copy-done.12
  579.1 5.4 convolution_bitcast_fusion
  584.5 4.3 copy.48
  588.8 3.3 broadcast_in_dim.117
  592.1 2.1 constant_dynamic-update-slice_fusion.3
  594.3 4.8 broadcast_in_dim.119
  599.2 4.9 convolution_dynamic-update-slice_fusion.1
  604.2 5.0 broadcast_in_dim.120
  609.1 4.4 convolution_dynamic-update-slice_fusion
  614.2 0.8 copy.57
  615.2 2.9 fusion.62
  618.2 1.2 copy.53
  619.5 2.3 slice_reduce_fusion
  622.2 0.8 copy.55
  623.4 105.2 %reduce-scatter.14.cloned.1.call-done = bf16[96,4608]{1,0:T(8,128)(2,1)} async-done(((bf16[768,4608]{1,0:T(8,128)(2,1)}), bf16[96,4608]{1,0:T(8,128)(2,1)}) %reduce-scatter.14.cloned.1.call-update) | async-done | bytes 884752 | tf_op jit(solution)/shard_map/reduce_scatter | solution.py:260
  728.5 167.6 %reduce-scatter.18.cloned.1.call-done = bf16[96,6144]{1,0:T(8,128)(2,1)} async-done(((bf16[768,6144]{1,0:T(8,128)(2,1)}), bf16[96,6144]{1,0:T(8,128)(2,1)}) %reduce-scatter.18.cloned.1.call-update) | async-done | bytes 1179664 | tf_op jit(solution)/shard_map/reduce_scatter | solution.py:266
  896.1 166.5 %reduce-scatter.20.cloned.1.call-done = bf16[384,1536]{1,0:T(8,128)(2,1)} async-done(((bf16[3072,1536]{1,0:T(8,128)(2,1)}), bf16[384,1536]{1,0:T(8,128)(2,1)}) %reduce-scatter.20.cloned.1.call-update) | async-done | bytes 1179664 | tf_op jit(solution)/shard_map/reduce_scatter | solution.py:269
  1062.6 1.2 fusion.100
  1063.8 5.9 add_bitcast_fusion
  1069.8 54.7 %reduce-scatter.26.cloned.1.call-done = bf16[96,4]{1,0:T(8,128)(2,1)} async-done(((bf16[768,4]{1,0:T(8,128)(2,1)}), bf16[96,4]{1,0:T(8,128)(2,1)}) %reduce-scatter.26.cloned.1.call-update) | async-done | bytes 784
  1125.2 65.0 %reduce-scatter.22.cloned.1.call-done = bf16[384,2]{1,0:T(8,128)(2,1)} async-done(((bf16[3072,2]{1,0:T(8,128)(2,1)}), bf16[384,2]{1,0:T(8,128)(2,1)}) %reduce-scatter.22.cloned.1.call-update) | async-done | bytes 1552
  1190.2 1.0 copy.54
  1191.2 62.8 %reduce-scatter.24.cloned.1.call-done = bf16[96,12]{1,0:T(8,128)(2,1)} async-done(((bf16[768,12]{1,0:T(8,128)(2,1)}), bf16[96,12]{1,0:T(8,128)(2,1)}) %reduce-scatter.24.cloned.1.call-update) | async-done | bytes 2320
  1254.8 7.7 all-reduce
  1264.2 68.4 %all-reduce.4.cloned.1.call-done = (bf16[96,4608]{1,0:T(8,128)(2,1)}, bf16[96,1536]{1,0:T(8,128)(2,1)}, bf16[96,6144]{1,0:T(8,128)(2,1)}, bf16[384,1536]{1,0:T(8,128)(2,1)}) async-done(((bf16[96,4608]{1,0:T(8,128)(2,1)}, bf16[96,1536]{1,0:T(8,128)(2,1)}, bf16[96,6144]{1,0:T(8,128)(2,1)}, bf16[384,1536]{1,0:T(8,128)(2,1)}), (bf16[96,4608]{1,0:T(8,128)(2,1)}, bf16[96,1536]{1,0:T(8,128)(2,1)}, ...) | async-done | bytes 3538960 | tf_op jit(solution)/shard_map/psum | solution.py:283
  1332.7 2.7 convert_element_type.238
  1335.3 1.8 convert_element_type.240
  1337.2 1.6 convert_element_type.242
  1338.8 1.7 convert_element_type.244
  (284 shorter events, 39.7 us)
Async XLA Ops:
  7.2 3.0 copy-start.35
  7.2 28.5 %copy-start.41 = (bf16[96,4]{0,1:T(4,128)(2,1)S(1)}, bf16[96,4]{0,1:T(4,128)(2,1)}, u32[]{:S(2)}) copy-start(bf16[96,4]{0,1:T(4,128)(2,1)} %param.21) | copy-start | bytes 2308
  7.2 45.9 %copy-start.40 = (bf16[384,2]{0,1:T(2,128)(2,1)S(1)}, bf16[384,2]{0,1:T(2,128)(2,1)}, u32[]{:S(2)}) copy-start(bf16[384,2]{0,1:T(2,128)(2,1)} %param.19) | copy-start | bytes 4612
  7.2 68.2 %copy-start.21 = (s32[1,512]{1,0:T(1,128)S(1)}, s32[1,512]{1,0:T(1,128)}, u32[]{:S(2)}) copy-start(s32[1,512]{1,0:T(1,128)} %param.13) | copy-start | bytes 6148
  7.2 114.0 %copy-start.43 = (bf16[1,512,768]{2,1,0:T(8,128)(2,1)S(1)}, bf16[1,512,768]{2,1,0:T(8,128)(2,1)}, u32[]{:S(2)}) copy-start(bf16[1,512,768]{2,1,0:T(8,128)(2,1)} %param.12) | copy-start | bytes 2359300
  7.2 113.9 %all-gather.8.cloned.1.call-start = ((), (), s32[]{:S(2)}) async-start(), calls=%async_computation.7 | async-start | bytes 7962624 | tf_op jit(solution)/shard_map/all_gather | solution.py:210
  8.0 164.9 %all-gather.10.cloned.1.call-start = ((), (), s32[]{:S(2)}) async-start(), calls=%async_computation.8 | async-start | bytes 2654208 | tf_op jit(solution)/shard_map/all_gather | solution.py:211
  8.7 303.7 %all-gather.12.cloned.1.call-start = ((), (), s32[]{:S(2)}) async-start(), calls=%async_computation.9 | async-start | bytes 10616832 | tf_op jit(solution)/shard_map/all_gather | solution.py:212
  9.4 441.3 %all-gather.14.cloned.1.call-start = ((), (), s32[]{:S(2)}) async-start(), calls=%async_computation.10 | async-start | bytes 10616832 | tf_op jit(solution)/shard_map/all_gather | solution.py:213
  10.0 613.3 %reduce-scatter.16.cloned.1.call-start = ((), (), s32[]{:S(2)}) async-start(), calls=%async_computation.12 | async-start | bytes 2654208 | tf_op jit(solution)/shard_map/reduce_scatter | solution.py:263
  75.7 375.0 %copy-start.36 = (f32[768]{0:T(1024)}, f32[768]{0:T(1024)S(1)}, u32[]{:S(2)}) copy-start(f32[768]{0:T(1024)S(1)} %get-tuple-element.195) | copy-start | bytes 9220
  75.8 452.4 %copy-start.24 = (f32[768]{0:T(1024)}, f32[768]{0:T(1024)S(1)}, u32[]{:S(2)}) copy-start(f32[768]{0:T(1024)S(1)} %get-tuple-element.200) | copy-start | bytes 9220
  175.5 275.3 %copy-start.6 = (f32[512,768]{1,0:T(8,128)}, f32[512,768]{1,0:T(8,128)S(1)}, u32[]{:S(2)}) copy-start(f32[512,768]{1,0:T(8,128)S(1)} %get-tuple-element.251) | copy-start | bytes 4718596
  175.5 352.7 %copy-start.22 = (f32[512]{0:T(512)}, f32[512]{0:T(512)S(1)}, u32[]{:S(2)}) copy-start(f32[512]{0:T(512)S(1)} %broadcast_multiply_fusion.1) | copy-start | bytes 6148
  175.8 352.4 %copy-start.30 = (f32[512]{0:T(512)}, f32[512]{0:T(512)S(1)}, u32[]{:S(2)}) copy-start(f32[512]{0:T(512)S(1)} %fusion.57) | copy-start | bytes 6148
  456.8 44.2 %copy-start = (f32[512,768]{1,0:T(8,128)}, f32[512,768]{1,0:T(8,128)S(1)}, u32[]{:S(2)}) copy-start(f32[512,768]{1,0:T(8,128)S(1)} %get-tuple-element.254) | copy-start | bytes 4718596
  456.8 41.7 %copy-start.42 = (s32[64]{0:T(128)S(1)}, s32[64]{0:T(128)}, u32[]{:S(2)}) copy-start(s32[64]{0:T(128)} %param.14) | copy-start | bytes 772
  501.6 22.8 %slice-start = ((s8[9437184]{0:T(1024)(128)(4,1)}), s8[4194304]{0:T(1024)(128)(4,1)S(1)}, s32[]{:S(2)}) async-start(s8[9437184]{0:T(1024)(128)(4,1)} %bitcast.168), calls=%async_computation.19 | async-start | bytes 8388608
  502.4 21.9 %copy-start.16 = (bf16[512,768]{1,0:T(8,128)(2,1)}, bf16[512,768]{1,0:T(8,128)(2,1)S(1)}, u32[]{:S(2)}) copy-start(bf16[512,768]{1,0:T(8,128)(2,1)S(1)} %get-tuple-element.227) | copy-start | bytes 2359300
  502.4 22.0 %copy-start.7 = (f32[512,768]{1,0:T(8,128)S(1)}, f32[512,768]{1,0:T(8,128)}, u32[]{:S(2)}) copy-start(f32[512,768]{1,0:T(8,128)} %copy-done.6) | copy-start | bytes 4718596
  502.4 22.0 %slice-start.1 = ((s8[9437184]{0:T(1024)(128)(4,1)}), s8[4194304]{0:T(1024)(128)(4,1)S(1)}, s32[]{:S(2)}) async-start(s8[9437184]{0:T(1024)(128)(4,1)} %bitcast.168), calls=%async_computation.20 | async-start | bytes 8388608
  502.4 22.0 %slice-start.2 = ((s8[9437184]{0:T(1024)(128)(4,1)}), s8[1048576]{0:T(1024)(128)(4,1)S(1)}, s32[]{:S(2)}) async-start(s8[9437184]{0:T(1024)(128)(4,1)} %bitcast.168), calls=%async_computation.21 | async-start | bytes 2097152
  524.4 3.8 copy-start.45
  528.8 1.7 copy-start.18
  528.9 2.5 copy-start.27
  532.8 2.2 copy-start.11
  532.8 195.8 %reduce-scatter.14.cloned.1.call-start = ((), (), s32[]{:S(2)}) async-start(), calls=%async_computation.11 | async-start | bytes 7962624 | tf_op jit(solution)/shard_map/reduce_scatter | solution.py:260
  535.0 2.5 copy-start.19
  540.3 2.0 copy-start.20
  542.3 2.5 copy-start.19
  547.5 1.9 copy-start.20
  549.5 2.5 copy-start.19
  554.7 2.0 copy-start.20
  556.7 2.5 copy-start.19
  561.9 1.9 copy-start.20
  563.8 2.5 copy-start.19
  569.1 2.0 copy-start.20
  571.0 2.5 copy-start.19
  576.3 1.9 copy-start.20
  594.2 4.9 copy-start.8
  594.2 4.9 copy-start.23
  594.2 4.9 copy-start.25
  594.3 4.9 copy-start.31
  594.3 4.9 copy-start.37
  594.3 301.8 %reduce-scatter.18.cloned.1.call-start = ((), (), s32[]{:S(2)}) async-start(), calls=%async_computation.13 | async-start | bytes 10616832 | tf_op jit(solution)/shard_map/reduce_scatter | solution.py:266
  594.3 4.8 copy-start.46
  604.1 5.0 copy-start.17
  604.1 458.5 %reduce-scatter.20.cloned.1.call-start = ((), (), s32[]{:S(2)}) async-start(), calls=%async_computation.14 | async-start | bytes 10616832 | tf_op jit(solution)/shard_map/reduce_scatter | solution.py:269
  604.2 5.0 copy-start.44
  613.5 1.7 copy-start.15
  613.5 510.9 %reduce-scatter.26.cloned.1.call-start = ((), (), s32[]{:S(2)}) async-start(), calls=%async_computation.17 | async-start | bytes 221184
  615.1 3.0 copy-start.26
  615.1 575.1 %reduce-scatter.22.cloned.1.call-start = ((), (), s32[]{:S(2)}) async-start(), calls=%async_computation.15 | async-start | bytes 884736
  618.1 3.8 copy-start.32
  618.1 3.8 copy-start.38
  618.1 3.8 copy-start.29
  618.1 3.8 copy-start.33
  619.4 443.2 %copy-start.1 = (f32[512,768]{1,0:T(8,128)S(1)}, f32[512,768]{1,0:T(8,128)}, u32[]{:S(2)}) copy-start(f32[512,768]{1,0:T(8,128)} %copy-done) | copy-start | bytes 4718596
  619.5 634.5 %reduce-scatter.24.cloned.1.call-start = ((), (), s32[]{:S(2)}) async-start(), calls=%async_computation.16 | async-start | bytes 221184
  622.2 441.6 %copy-start.5 = (f32[512,768]{1,0:T(8,128)S(1)}, f32[512,768]{1,0:T(8,128)}, u32[]{:S(2)}) copy-start(f32[512,768]{1,0:T(8,128)} %copy-done.4) | copy-start | bytes 4718596
  622.2 441.6 %copy-start.28 = (f32[512]{0:T(512)S(1)}, f32[512]{0:T(512)}, u32[]{:S(2)}) copy-start(f32[512]{0:T(512)} %copy-done.27) | copy-start | bytes 6148
  623.1 709.6 %all-reduce.4.cloned.1.call-start = ((), (), s32[]{:S(2)}) async-start(), calls=%async_computation.18 | async-start | bytes 7077888 | tf_op jit(solution)/shard_map/psum | solution.py:283
  1332.7 4.5 copy-start.10
  1332.7 6.1 copy-start.9
  (8 other events, 9.5 us)
Sparse Core Ops, SparseCore 0:
  10.3 110.8 all-gather.7
  123.4 49.4 all-gather.9
  175.0 137.3 all-gather.11
  314.5 136.2 all-gather.13
  532.9 63.8 reduce-scatter.15
  600.3 128.1 reduce-scatter.13
  732.6 163.5 reduce-scatter.17
  900.1 162.4 reduce-scatter.19
  1066.2 58.1 reduce-scatter.25
  1128.5 61.6 reduce-scatter.21
  1194.1 59.8 reduce-scatter.23
  1256.4 76.1 all-reduce.3
where the time goes:
time: 1350 us
  waiting for transfers between devices  1030 us (76%)
  blocking collectives  113 us (8%)
  matrix products  104 us (8%)
  local copies, waits for them, and re-layouts  48.5 us (4%)
  other arithmetic  28.6 us (2%)
  between operations  15.3 us (1%)
    unnamed x15, waiting for transfers between devices  185 us
    reduce_scatter x1, waiting for transfers between devices, per_device(): lax.psum_scatter(g_all[2].astype(jnp.bfloat16), 'dp', scatter_dimension=0...  168 us
    reduce_scatter x1, waiting for transfers between devices, per_device(): lax.psum_scatter(g_all[3].astype(jnp.bfloat16), 'dp', scatter_dimension=0...  166 us
    all_gather x1, waiting for transfers between devices, per_device(): lax.all_gather(w_up, 'dp', axis=0, tiled=True)  137 us
    all_gather x1, waiting for transfers between devices, per_device(): lax.all_gather(w_down, 'dp', axis=0, tiled=True)  119 us
    reduce_scatter x1, waiting for transfers between devices, per_device(): lax.psum_scatter(g_all[0].astype(jnp.bfloat16), 'dp', scatter_dimension=0...  105 us
    psum x1, waiting for transfers between devices, per_device(): lax.psum(s_mix.astype(jnp.bfloat16), 'outer').astype(jnp.float32)  68.4 us
    all_gather x1, waiting for transfers between devices, per_device(): lax.all_gather(w_mix, 'dp', axis=0, tiled=True)  45.1 us
  transfers between devices with their start and end apart: 12, of which 11 were waited for; matrix products, arithmetic and copies ran while one was open for 10% of the time, Pallas kernels for 0%

commit v1 on v0

v1 whole, which is shorter than its diff:
```python
import functools

import jax
import jax.numpy as jnp
from jax import lax
from jax.experimental import pallas as pl
from jax.experimental.pallas import tpu as pltpu
from jax.sharding import PartitionSpec as P

D = 768
HEADS = 12
HEAD_DIM = 64
FF = 3072
SEGS = 4
BF = jnp.bfloat16
F32 = jnp.float32
MESH = pl.DeviceIdType.MESH

masked_score = -1e30
layer_eps = 1e-05


def dot_plain(left, right):
    return jnp.dot(left, right, preferred_element_type=F32)


def dot_over_rows(left, right):
    return lax.dot_general(left, right, (((0,), (0,)), ((), ())), preferred_element_type=F32)


def dot_over_columns(left, right):
    return lax.dot_general(left, right, (((1,), (1,)), ((), ())), preferred_element_type=F32)


def gelu_exact(inputs):
    return jax.nn.gelu(inputs, approximate=False)


def norm_parts(inputs):
    center = inputs - jnp.mean(inputs, axis=-1, keepdims=True)
    inverse = lax.rsqrt(jnp.mean(center * center, axis=-1, keepdims=True) + layer_eps)
    return center * inverse, inverse


def norm_back(unit, inverse, gain, grad):
    scaled = gain * grad
    return inverse * (
        scaled
        - jnp.mean(scaled, axis=-1, keepdims=True)
        - unit * jnp.mean(scaled * unit, axis=-1, keepdims=True)
    )


def gather_kernel(widths, *refs):
    kinds = len(widths)
    sources, results = refs[:kinds], refs[kinds : 2 * kinds]
    local, far_s, far_r, near_s, near_r, pass_s, pass_r, x_s, x_r, y_s, y_r, c_s, c_r = refs[2 * kinds :]
    place = lax.axis_index("dp")
    other = lax.axis_index("outer")
    z, x = place // 2, place % 2
    y, c = other // 2, other % 2
    z_near = z + 1 - 2 * (z % 2)
    z_far = 3 - z
    z_last = 3 - z_near
    tower = z // 2

    def device(zz, xx, yy, cc):
        return (zz * 2 + xx, yy * 2 + cc)

    to_far = device(z_far, x, y, c)
    to_near = device(z_near, x, y, c)
    to_x = device(z, 1 - x, y, c)
    to_y = device(z, x, 1 - y, c)
    to_core = device(z, x, y, 1 - c)
    barrier = pltpu.get_barrier_semaphore()
    for peer in (to_far, to_near, to_x, to_y, to_core):
        pl.semaphore_signal(barrier, inc=1, device_id=peer, device_id_type=MESH)
    pl.semaphore_wait(barrier, 5)

    def rows_of(k):
        return sources[k].shape[0]

    def own(k, which, half_row, half_col):
        n, r = widths[k], rows_of(k)
        row, rows = (half_row * (r // 2), r // 2)
        col, cols = which * n, n
        if half_col is not None:
            col, cols = col + half_col * (n // 2), n // 2
        return sources[k].at[
            pl.ds(pl.multiple_of(row, 16), rows), pl.ds(pl.multiple_of(col, 128), cols)
        ]

    def full(k, zz, xx, half_row, half_col):
        n, r = widths[k], rows_of(k)
        row, rows = (zz * 2 + xx) * r + half_row * (r // 2), r // 2
        col, cols = 0, n
        if half_col is not None:
            col, cols = half_col * (n // 2), n // 2
            col = pl.multiple_of(col, 128)
        return results[k].at[pl.ds(pl.multiple_of(row, 16), rows), pl.ds(col, cols)]

    def remote(src, dst, s, r, peer):
        return pltpu.make_async_remote_copy(
            src_ref=src, dst_ref=dst, send_sem=s, recv_sem=r, device_id=peer, device_id_type=MESH
        )

    planes = (z, z_near, z_far, z_last)
    sent = []

    def go(copy):
        copy.start()
        sent.append(copy)

    def x_copy(k, j):
        src = own(k, tower, c, y) if j == 0 else full(k, planes[j], x, c, y)
        return remote(src, full(k, planes[j], x, c, y), x_s.at[k, j], x_r.at[k, j], to_x)

    def y_copy(k, j):
        ref = full(k, planes[j], 1 - x, c, y)
        return remote(ref, ref, y_s.at[k, j], y_r.at[k, j], to_y)

    def c_copy(k, j):
        ref = full(k, planes[j % 4], x if j < 4 else 1 - x, c, None)
        return remote(ref, ref, c_s.at[k, j], c_r.at[k, j], to_core)

    locals_ = []
    for k in range(kinds):
        go(remote(own(k, 1 - tower, c, None), full(k, z, x, c, None), far_s.at[k], far_r.at[k], to_far))
        go(remote(own(k, tower, c, None), full(k, z, x, c, None), near_s.at[k], near_r.at[k], to_near))
        go(x_copy(k, 0))
        n, r = widths[k], rows_of(k)
        copy = pltpu.make_async_copy(
            sources[k].at[:, pl.ds(pl.multiple_of(tower * n, 128), n)],
            results[k].at[pl.ds(pl.multiple_of((z * 2 + x) * r, 16), r), :],
            local.at[k],
        )
        copy.start()
        locals_.append(copy)

    def wait_far(k):
        ref = full(k, z_far, x, c, None)
        remote(ref, ref, far_s.at[k], far_r.at[k], to_far).wait_recv()

    def wait_near(k):
        ref = full(k, z_near, x, c, None)
        remote(ref, ref, near_s.at[k], near_r.at[k], to_near).wait_recv()

    def wait_pass(k):
        ref = full(k, z_last, x, c, None)
        remote(ref, ref, pass_s.at[k], pass_r.at[k], to_near).wait_recv()

    def wait_x(k, j):
        ref = full(k, planes[j], 1 - x, c, y)
        remote(ref, ref, x_s.at[k, j], x_r.at[k, j], to_x).wait_recv()

    def wait_y(k, j):
        ref = full(k, planes[j], 1 - x, c, 1 - y)
        remote(ref, ref, y_s.at[k, j], y_r.at[k, j], to_y).wait_recv()

    def wait_c(k, j):
        ref = full(k, planes[j % 4], x if j < 4 else 1 - x, 1 - c, None)
        remote(ref, ref, c_s.at[k, j], c_r.at[k, j], to_core).wait_recv()

    def first(k):
        wait_far(k)
        ref = full(k, z_far, x, c, None)
        go(remote(ref, ref, pass_s.at[k], pass_r.at[k], to_near))
        go(x_copy(k, 2))
        go(c_copy(k, 2))
        wait_near(k)
        go(x_copy(k, 1))
        go(c_copy(k, 1))
        wait_x(k, 0)
        go(y_copy(k, 0))

    def second(k):
        wait_pass(k)
        go(x_copy(k, 3))
        go(c_copy(k, 3))
        for j in (2, 1):
            wait_x(k, j)
            go(y_copy(k, j))

    def third(k):
        wait_x(k, 3)
        go(y_copy(k, 3))
        for j in (0, 2, 1, 3):
            wait_y(k, j)
            go(c_copy(k, 4 + j))

    for step in range(kinds + 2):
        if step < kinds:
            first(step)
        if 0 <= step - 1 < kinds:
            second(step - 1)
        if 0 <= step - 2 < kinds:
            third(step - 2)
    for k in range(kinds):
        for j in range(1, 8):
            wait_c(k, j)
    for copy in sent:
        copy.wait_send()
    for copy in locals_:
        copy.wait()


def gather_weights(weights, widths, n_dp, n_outer):
    if (n_dp, n_outer) != (8, 4):
        tower = lax.axis_index("dp") * 2 // n_dp
        whole = [lax.all_gather(w, "dp", axis=0, tiled=True) for w in weights]
        return [lax.dynamic_slice_in_dim(w, tower * n, n, 1) for w, n in zip(whole, widths)]
    kinds = len(weights)
    sem = pltpu.SemaphoreType.DMA
    return pl.pallas_call(
        functools.partial(gather_kernel, widths),
        out_shape=[jax.ShapeDtypeStruct((w.shape[0] * n_dp, n), w.dtype) for w, n in zip(weights, widths)],
        in_specs=[pl.BlockSpec(memory_space=pl.ANY)] * kinds,
        out_specs=[pl.BlockSpec(memory_space=pl.ANY)] * kinds,
        scratch_shapes=[sem((kinds,))] * 7
        + [sem((kinds, 4))] * 4
        + [sem((kinds, 8))] * 2,
        compiler_params=pltpu.CompilerParams(collective_id=1, has_side_effects=True),
        name="gather_weights",
    )(*weights)


def spread_kernel(n_outer, total, whole_ref, parts_ref, all_ref, sliced_ref, local, s_one, r_one, s_two, r_two):
    dp, outer = lax.axis_index("dp"), lax.axis_index("outer")
    me = dp * n_outer + outer
    barrier = pltpu.get_barrier_semaphore()

    def greet(i, carry):
        peer = lax.rem(me + i, total)
        pl.semaphore_signal(barrier, inc=1, device_id=(peer // n_outer, lax.rem(peer, n_outer)), device_id_type=MESH)
        return carry

    lax.fori_loop(1, total, greet, 0)
    pl.semaphore_wait(barrier, total - 1)

    def copies(i):
        peer = lax.rem(me + i, total)
        there = peer // n_outer
        device = (there, lax.rem(peer, n_outer))
        one = pltpu.make_async_remote_copy(
            src_ref=whole_ref, dst_ref=all_ref.at[me], send_sem=s_one.at[i], recv_sem=r_one.at[i],
            device_id=device, device_id_type=MESH,
        )
        if parts_ref is None:
            return (one,)
        two = pltpu.make_async_remote_copy(
            src_ref=parts_ref.at[there], dst_ref=sliced_ref.at[me], send_sem=s_two.at[i], recv_sem=r_two.at[i],
            device_id=device, device_id_type=MESH,
        )
        return (one, two)

    def send(i, carry):
        for copy in copies(i):
            copy.start()
        return carry

    lax.fori_loop(1, total, send, 0)
    own = [pltpu.make_async_copy(whole_ref, all_ref.at[me], local.at[0])]
    if parts_ref is not None:
        own.append(pltpu.make_async_copy(parts_ref.at[dp], sliced_ref.at[me], local.at[1]))
    for copy in own:
        copy.start()

    def settle(i, carry):
        for copy in copies(i):
            copy.wait()
        return carry

    lax.fori_loop(1, total, settle, 0)
    for copy in own:
        copy.wait()


def spread(whole, parts, n_dp, n_outer, identity):
    total = n_dp * n_outer
    sem = pltpu.SemaphoreType.DMA
    out_shape = [jax.ShapeDtypeStruct((total,) + whole.shape, whole.dtype)]
    operands = [whole]
    if parts is not None:
        out_shape.append(jax.ShapeDtypeStruct((total,) + parts.shape[1:], parts.dtype))
        operands.append(parts)
        kernel = functools.partial(spread_kernel, n_outer, total)
        scratch = [sem((2,))] + [sem((total,))] * 4
    else:
        def kernel(w, a, local, s, r):
            spread_kernel(n_outer, total, w, None, a, None, local, s, r, None, None)
        scratch = [sem((2,))] + [sem((total,))] * 2
    return pl.pallas_call(
        kernel,
        out_shape=out_shape,
        in_specs=[pl.BlockSpec(memory_space=pltpu.VMEM)] * len(operands),
        out_specs=[pl.BlockSpec(memory_space=pltpu.VMEM)] * len(out_shape),
        scratch_shapes=scratch,
        compiler_params=pltpu.CompilerParams(
            collective_id=identity, has_side_effects=True, vmem_limit_bytes=48 << 20
        ),
        name="spread%d" % identity,
    )(*operands)


def expand_heads(rows):
    head_of = jnp.arange(D, dtype=jnp.int32) // HEAD_DIM
    keep = head_of[None, :] == jnp.arange(HEADS, dtype=jnp.int32)[:, None]
    return jnp.where(keep[:, None, :], rows[None], 0).reshape(HEADS * rows.shape[0], D)


def per_device(text_rows, text_segments, positives, w_mix, w_proj, w_up, w_down, b_up, b_rows, g_rows):
    n_dp, n_outer = lax.axis_size("dp"), lax.axis_size("outer")
    total = n_dp * n_outer
    own_index = lax.axis_index(("dp", "outer"))
    tower = own_index * 2 // total
    rows_in, segments = text_rows[0], text_segments[0]
    row_len = rows_in.shape[0]
    widths = (3 * D, D, FF, D)
    wm, wp, wu, wd = gather_weights((w_mix, w_proj, w_up, w_down), widths, n_dp, n_outer)
    part_f, part_d = b_up.shape[0], b_rows.shape[0]
    small = jnp.concatenate([b_up.reshape(part_f // part_d, part_d, 2).transpose(0, 2, 1).reshape(-1, part_d), b_rows.T, g_rows.T], axis=0)
    small = lax.all_gather(small, "dp", axis=0)
    split = 2 * (part_f // part_d)
    up_b = small[:, :split].reshape(n_dp, part_f // part_d, 2, part_d).transpose(2, 0, 1, 3).reshape(2, FF)
    row_b = small[:, split : split + 12].transpose(1, 0, 2).reshape(2, 6, D)
    gain_b = small[:, split + 12 :].transpose(1, 0, 2).reshape(2, 2, D)
    pick = lambda both_towers: jnp.where(tower == 0, both_towers[0], both_towers[1]).astype(F32)
    c_up, biases, gains = pick(up_b), pick(row_b), pick(gain_b)
    bq, bv, bo, o1, bd, o2 = (biases[i] for i in range(6))
    g1, g2 = gains[0], gains[1]

    scaled = HEAD_DIM ** (-0.5)
    mixed = (dot_plain(rows_in, wm) + jnp.concatenate([bq, jnp.zeros_like(bq), bv])).astype(BF)
    q, k, v = mixed[:, :D], mixed[:, D : 2 * D], mixed[:, 2 * D :]
    allowed = segments[:, None] == segments[None, :]
    heads = lambda m: m.reshape(row_len, HEADS, HEAD_DIM)
    scores = jnp.einsum("qhe,khe->hqk", heads(q), heads(k), preferred_element_type=F32) * scaled
    scores = jnp.where(allowed[None], scores, masked_score)
    top = jnp.max(scores, axis=-1, keepdims=True)
    raised = jnp.exp(scores - top)
    chances = (raised / jnp.sum(raised, axis=-1, keepdims=True)).astype(BF)
    attended = jnp.einsum("hqk,khe->qhe", chances, heads(v), preferred_element_type=F32).reshape(row_len, D).astype(BF)
    before_one = rows_in.astype(F32) + dot_plain(attended, wp) + bo
    unit_one, inv_one = norm_parts(before_one)
    h1 = unit_one * g1 + o1
    h1_low = h1.astype(BF)
    up_pre = dot_plain(h1_low, wu) + c_up
    gelu_low = gelu_exact(up_pre).astype(BF)
    before_two = h1 + dot_plain(gelu_low, wd) + bd
    unit_two, inv_two = norm_parts(before_two)
    encoded = unit_two * g2 + o2

    levels = jnp.arange(SEGS, dtype=jnp.int32)
    starts = jnp.sum((segments[None, :] < levels[:, None]).astype(jnp.int32), axis=1)
    at = lambda m: jnp.take(m, starts, axis=0)
    vectors = at(encoded).astype(BF)
    all_cls = spread(vectors, None, n_dp, n_outer, 2)[0].reshape(total * SEGS, D)
    texts = total * SEGS // 2
    all_q, all_p = all_cls[:texts], all_cls[texts:]
    pair_scale = 2.0 * D ** (-0.5)
    logits = dot_over_columns(all_q, all_p) * pair_scale
    raised_l = jnp.exp(logits - jnp.max(logits, axis=1, keepdims=True))
    hit = (positives[:, None] == jnp.arange(texts, dtype=jnp.int32)[None, :]).astype(F32)
    d_logits = (raised_l / jnp.sum(raised_l, axis=1, keepdims=True) - hit).astype(BF)
    position = own_index * SEGS - tower * texts
    d_q = dot_plain(lax.dynamic_slice_in_dim(d_logits, position, SEGS, 0), all_p)
    d_p = dot_over_rows(lax.dynamic_slice_in_dim(d_logits, position, SEGS, 1), all_q)
    d_cls = jnp.where(tower == 0, d_q, d_p) * pair_scale

    ut, it = at(unit_two), at(inv_two)
    dg2, do2 = jnp.sum(d_cls * ut, axis=0), jnp.sum(d_cls, axis=0)
    dz2 = norm_back(ut, it, g2, d_cls)
    df = dz2.astype(BF)
    dg = dot_over_columns(df, wd)
    u_r = at(up_pre)
    _, gelu_back = jax.vjp(gelu_exact, u_r)
    du = gelu_back(dg)[0].astype(BF)
    dh1 = dz2 + dot_over_columns(du, wu)
    uo, io = at(unit_one), at(inv_one)
    dg1, do1 = jnp.sum(dh1 * uo, axis=0), jnp.sum(dh1, axis=0)
    dz1 = norm_back(uo, io, g1, dh1)
    db = dz1.astype(BF)
    da = dot_over_columns(db, wp).astype(BF)
    q_r = at(q)
    q_wide, a_wide = expand_heads(q_r), expand_heads(da)
    own_segment = jnp.tile(levels, HEADS)
    open_keys = own_segment[:, None] == segments[None, :]
    s_r = jnp.where(open_keys, dot_over_columns(q_wide, k) * scaled, masked_score)
    e_r = jnp.exp(s_r - jnp.max(s_r, axis=-1, keepdims=True))
    p_r = e_r / jnp.sum(e_r, axis=-1, keepdims=True)
    pl_r = p_r.astype(BF)
    dp_r = dot_over_columns(a_wide, v)
    ds_r = (p_r * (dp_r - jnp.sum(p_r * dp_r, axis=-1, keepdims=True))).astype(BF)
    dq_wide = dot_plain(ds_r, k).reshape(HEADS, SEGS, HEADS, HEAD_DIM)
    dq = (jnp.einsum("hshe->she", dq_wide).reshape(SEGS, D) * scaled).astype(BF)
    y_r = (dot_plain(ds_r, rows_in) * scaled).astype(BF)
    z_r = dot_plain(pl_r, rows_in).astype(BF)
    weight_sum = jnp.sum(pl_r.astype(F32), axis=1, keepdims=True)
    dbv = jnp.sum(weight_sum * a_wide.astype(F32), axis=0)
    t_k = (dot_over_columns(q_wide, wm[:, D : 2 * D]) * scaled).astype(BF)
    t_v = dot_over_columns(a_wide, wm[:, 2 * D :]).astype(BF)
    d_rows = dot_over_rows(jnp.concatenate([ds_r, pl_r], axis=0), jnp.concatenate([t_k, t_v], axis=0))
    d_rows_at = dz1 + dot_over_columns(dq, wm[:, :D])
    spot = (starts[:, None] == jnp.arange(row_len, dtype=jnp.int32)[None, :])
    for s in range(SEGS):
        d_rows = d_rows + jnp.where(spot[s][:, None], d_rows_at[s][None, :], 0.0)

    ff_rows = SEGS * FF // D
    whole = jnp.concatenate(
        [df, db, dq, q_r, da, du.reshape(ff_rows, D), jnp.stack([dbv, do1, do2, dg1, dg2]).astype(BF), jnp.zeros((3, D), BF)],
        axis=0,
    )
    g_r, h_r, at_r, x_r = at(gelu_low), at(h1_low), at(attended), at(rows_in)
    by_part = lambda m: m.reshape(m.shape[0], n_dp, m.shape[1] // n_dp).transpose(1, 0, 2)
    parts = jnp.concatenate(
        [by_part(h_r), by_part(at_r), by_part(x_r), by_part(y_r), by_part(z_r),
         by_part(g_r).reshape(n_dp, -1, part_d)],
        axis=1,
    )
    all_w, all_s = spread(whole, parts, n_dp, n_outer, 3)
    half = total // 2
    tw = all_w.reshape(2, half, -1, D)
    ts = all_s.reshape(2, half, -1, part_d)
    rank = lambda m: m.reshape(half * SEGS, -1)
    grads = []
    outs = [[], [], [], []]
    vec_b, vec_g, vec_u = [], [], []
    mine = lax.axis_index("dp")
    for t in range(2):
        w, s = tw[t], ts[t]
        df_a, db_a, dq_a, q_a, da_a = (rank(w[:, 4 * i : 4 * i + 4]) for i in range(5))
        du_a = w[:, 20 : 20 + ff_rows].reshape(half * SEGS, FF)
        vec = jnp.sum(w[:, 20 + ff_rows : 25 + ff_rows].astype(F32), axis=0)
        h_a, at_a, x_a = (rank(s[:, 4 * i : 4 * i + 4]) for i in range(3))
        y_a = s[:, 12:60].reshape(half, HEADS, SEGS, part_d)
        z_a = s[:, 60:108].reshape(half, HEADS, SEGS, part_d)
        g_a = s[:, 108:].reshape(half * SEGS, part_f)
        by_head = lambda m: m.reshape(half, SEGS, HEADS, HEAD_DIM)
        gk = jnp.einsum("rhsa,rshe->ahe", y_a, by_head(q_a), preferred_element_type=F32).reshape(part_d, D)
        gv = jnp.einsum("rhsa,rshe->ahe", z_a, by_head(da_a), preferred_element_type=F32).reshape(part_d, D)
        outs[0] += [dot_over_rows(x_a, dq_a), gk, gv]
        outs[1].append(dot_over_rows(at_a, db_a))
        outs[2].append(dot_over_rows(h_a, du_a))
        outs[3].append(dot_over_rows(g_a, df_a))
        col = lambda m, n: lax.dynamic_slice_in_dim(m, mine * n, n, 0)
        summed = lambda m: jnp.sum(m.astype(F32), axis=0)
        vec_b += [col(m, part_d) for m in (summed(dq_a), vec[0], summed(db_a), vec[1], summed(df_a), vec[2])]
        vec_g += [col(m, part_d) for m in (vec[3], vec[4])]
        vec_u.append(col(summed(du_a), part_f))
    return (
        encoded.astype(BF)[None],
        d_rows[None],
        jnp.concatenate(outs[0], axis=1),
        jnp.concatenate(outs[1], axis=1),
        jnp.concatenate(outs[2], axis=1),
        jnp.concatenate(outs[3], axis=1),
        jnp.stack(vec_u, axis=1),
        jnp.stack(vec_b, axis=1),
        jnp.stack(vec_g, axis=1),
    )


def solution(mesh):
    rows, cols = P(("dp", "outer"), None, None), P("dp", None)
    return jax.shard_map(
        per_device,
        mesh=mesh,
        in_specs=(rows, P(("dp", "outer"), None), P(), cols, cols, cols, cols, cols, cols, cols),
        out_specs=(rows, rows, cols, cols, cols, cols, cols, cols, cols),
        check_vma=False,
    )
```

time: 1350 us -> 356 us (0.26)
  the two profiles are of different devices: /device:TPU:1 before, /device:TPU:15 now
where the time goes in v1:
time: 356 us; the launch traced here: 355 us
  Pallas kernels  199 us (56%)
  matrix products  67.8 us (19%)
  local copies, waits for them, and re-layouts  47.8 us (13%)
  blocking collectives  21.8 us (6%)
  other arithmetic  16.9 us (5%)
    pallas_call x2, Pallas kernels, spread(): pl.pallas_call(kernel, out_shape=out_shape, in_specs=[pl.BlockSpec(memory...  100 us
    pallas_call x1, Pallas kernels, gather_weights(): pl.pallas_call(functools.partial(gather_kernel, widths), out_shape=[jax.S...  98.8 us
    dot_general x8, matrix products, dot_plain(): return jnp.dot(left, right, preferred_element_type=F32)  32.9 us
    all_gather x1, blocking collectives, per_device(): small = lax.all_gather(small, 'dp', axis=0)  21.8 us
    gather x11, local copies, waits for them, and re-layouts, per_device(): at = lambda m: jnp.take(m, starts, axis=0)  16.9 us
    dot_general x9, matrix products, dot_over_columns(): lax.dot_general(left, right, (((1,), (1,)), ((), ())), preferred_element_...  14.3 us
    sub x1, matrix products, per_device(): raised = jnp.exp(scores - top)  7.79 us

profile of v1, /device:TPU:15, one launch (start us, length us, event | category | flops | bytes accessed | tf_op | source)
XLA Modules:
  0.0 355.0 jit_solution(13029617712969637258)
XLA Ops:
  0.7 0.8 reshape.409
  1.5 0.7 pad_maximum_fusion.4
  2.2 21.8 %all-gather = bf16[192,96]{1,0:T(8,128)(2,1)S(1)} all-gather(bf16[24,96]{1,0:T(8,128)(2,1)S(1)} %pad_maximum_fusion.4), channel_id=2, replica_groups=mesh['dp'=8,'outer'=4] {'dp'}, dimensions={0}, use_global_device_ids=true | all-gather | bytes 41472 | tf_op jit(solution)/shard_map/all_gather | solution.py:322
  24.4 98.8 %gather_weights.1 = (bf16[768,2304]{1,0:T(8,128)(2,1)}, bf16[768,768]{1,0:T(8,128)(2,1)}, bf16[768,3072]{1,0:T(8,128)(2,1)}, bf16[3072,768]{1,0:T(8,128)(2,1)}) custom-call(bf16[96,4608]{1,0:T(8,128)(2,1)} %refs_0_.1, bf16[96,1536]{1,0:T(8,128)(2,1)} %refs_1_.1, bf16[96,6144]{1,0:T(8,128)(2,1)} %refs_2_.1, bf16[384,1536]{1,0:T(8,128)(2,1)} %refs_3_.1), custom_call_target="tpu_custom_call" | custom-call | tf_op jit(solution)/shard_map/gather_weights/pallas_call | solution.py:214
  123.2 4.3 %fusion.17 = bf16[512,2304]{0,1:T(8,128)(2,1)S(1)} fusion(bf16[768,2304]{1,0:T(8,128)(2,1)} %get-tuple-element.18, f32[2304]{0:T(1024)S(1)} %pad_maximum_fusion.3, bf16[1,512,768]{2,1,0:T(8,128)(2,1)S(1)} %copy-done.6), kind=kOutput, calls=%fused_computation.42 | convolution fusion | flops 1814298624 | bytes 6693888 | tf_op jit(solution)/shard_map/dot_general | solution.py:24
  127.5 1.4 copy-done.2
  129.1 0.5 copy-done.32
  129.8 7.8 %fusion.129 = (f32[12,512]{1,0:T(8,128)S(1)}, f32[12,512,512]{1,2,0:T(8,128)}) fusion(pred[512,512]{0,1:T(8,128)(4,1)S(1)} %broadcast_compare_fusion, bf16[512,12,64]{0,2,1:T(8,128)(2,1)S(1)} %bitcast.176, bf16[512,12,64]{0,2,1:T(8,128)(2,1)S(1)} %bitcast.183), kind=kOutput, calls=%fused_computation.290 | convolution fusion | flops 415236608 | bytes 14442496 | tf_op jit(solution)/shard_map/sub | solution.py:340
  137.6 6.7 %fusion.18 = bf16[12,64,512]{2,1,0:T(8,128)(2,1)} fusion(bf16[512,12,64]{0,2,1:T(8,128)(2,1)S(1)} %bitcast.182, f32[12,512,512]{1,2,0:T(8,128)} %get-tuple-element.116, f32[12,512]{1,0:T(8,128)S(1)} %get-tuple-element.115), kind=kOutput, calls=%fused_computation.54 | convolution fusion | flops 409337856 | bytes 14180352 | tf_op jit(solution)/shard_map/hqk,khe->qhe/dot_general | solution.py:342
  144.4 2.5 fusion.130
  147.3 1.8 fusion.19
  149.2 18.6 %fusion.4 = (bf16[512,3072]{1,0:T(8,128)(2,1)}, f32[512,3072]{1,0:T(8,128)}) fusion(f32[3072]{0:T(1024)S(1)} %reshape.439, bf16[512,768]{1,0:T(8,128)(2,1)} %get-tuple-element.66, bf16[768,3072]{1,0:T(8,128)(2,1)} %get-tuple-element.20), kind=kOutput, calls=%fused_computation.19 | convolution fusion | flops 2519728128 | bytes 14954496 | tf_op jit(solution)/shard_map/dot_general | solution.py:24
  168.0 2.9 gather_fusion.1
  170.9 0.6 gather_fusion.3
  171.7 0.7 reshape.422
  172.4 6.4 %fusion.131 = (f32[512]{0:T(512)S(1)}, f32[512,768]{1,0:T(8,128)S(1)}) fusion(f32[768]{0:T(1024)S(1)} %add.182, bf16[512,3072]{1,0:T(8,128)(2,1)} %get-tuple-element.119, bf16[3072,768]{1,0:T(8,128)(2,1)} %get-tuple-element.21, f32[768]{0:T(1024)S(1)} %add.176, f32[512,768]{1,0:T(8,128)} %get-tuple-element.67, f32[768]{0:T(1024)S(1)} %mul.247), kind=kOutput, calls=%fused_computation.292 | convolution fusion | flops 2417884672 | bytes 11021312 | tf_op jit(solution)/shard_map/dot_general | solution.py:24
  179.2 0.6 gather_fusion.4
  180.0 1.7 multiply_add_fusion
  181.7 1.8 gather_fusion.5
  183.6 1.8 gather_fusion.8
  185.4 1.4 copy.82
  186.8 0.6 gather_fusion.9
  187.6 0.6 gather_fusion.2
  188.2 0.6 gather_fusion.10
  188.8 0.7 broadcast_select_fusion.4
  189.4 9.4 %spread2.1 = bf16[32,4,768]{2,1,0:T(4,128)(2,1)S(1)} custom-call(bf16[4,768]{1,0:T(4,128)(2,1)S(1)} %get-tuple-element.113.w), custom_call_target="tpu_custom_call" | custom-call | tf_op jit(solution)/shard_map/spread2/pallas_call | solution.py:292
  199.5 2.0 gather_fusion.6
  201.5 0.7 multiply_reduce_fusion.4
  202.4 3.4 gather_fusion
  205.7 3.7 %fusion.73 = bf16[4,3072]{1,0:T(4,128)(2,1)S(1)} fusion(f32[4,3072]{1,0:T(4,128)S(1)} %gather_fusion, pred[4]{0:T(512)(128)(4,1)S(1)} %get-tuple-element.61, bf16[4,768]{1,0:T(4,128)(2,1)S(1)} %get-tuple-element.62, bf16[3072,768]{1,0:T(8,128)(2,1)} %get-tuple-element.21), kind=kOutput, calls=%fused_computation.136 | convolution fusion | flops 19771392 | bytes 4798468 | tf_op jit(solution)/shard_map/dot_general | solution.py:32
  209.4 2.0 gather_fusion.7
  211.4 4.4 %multiply_reduce_fusion.5 = (bf16[768]{0:T(1024)(128)(2,1)}, f32[4]{0:T(128)S(1)}, f32[4]{0:T(128)S(1)}, bf16[768]{0:T(1024)(128)(2,1)}, f32[4,768]{1,0:T(4,128)S(1)}) fusion(f32[4,768]{1,0:T(4,128)S(1)} %gather_fusion.7, pred[4]{0:T(512)(128)(4,1)S(1)} %get-tuple-element.61, f32[768]{0:T(1024)S(1)} %mul.247, f32[4,768]{1,0:T(4,128)S(1)} %get-tuple-element.63, ...), kind=kOutput, calls=%fused_computation.174 | convolution fusion | flops 18900472 | bytes 4786212 | tf_op jit(solution)/shard_map/dot_general | solution.py:32
  215.9 0.7 fusion.118
  216.5 1.7 convolution_convert_fusion.1
  220.2 0.7 convert_reduce_fusion.10
  221.8 0.8 reshape.419
  222.6 0.8 reshape.418
  223.3 0.8 reshape.417
  224.1 1.4 concatenate.36.parts_ref
  225.5 0.7 mul.299
  226.3 0.8 multiply_reduce_fusion.2
  227.8 0.8 reshape.416
  228.6 0.7 stack.86
  229.3 0.7 stack.88
  229.9 0.7 stack.87
  230.6 0.7 stack.89
  231.3 2.3 concatenate.35.whole_ref
  233.6 90.9 %spread3.1 = (bf16[32,44,768]{2,1,0:T(8,128)(2,1)S(1)}, bf16[32,124,96]{2,1,0:T(8,128)(2,1)S(1)}) custom-call(bf16[44,768]{1,0:T(8,128)(2,1)S(1)} %concatenate.35.whole_ref, bf16[8,124,96]{2,1,0:T(8,128)(2,1)S(1)} %concatenate.36.parts_ref), custom_call_target="tpu_custom_call" | custom-call | tf_op jit(solution)/shard_map/spread3/pallas_call | solution.py:292
  324.5 1.0 copy-done
  326.0 0.6 pad_maximum_fusion.6
  327.8 1.2 stack.105
  329.0 1.1 fusion.121
  330.1 2.0 reshape.432
  332.1 1.1 convert_reduce_fusion.1
  333.3 2.0 reshape.434
  335.2 1.1 convert_reduce_fusion
  336.4 0.6 pad_maximum_fusion.5
  337.0 1.1 fusion.120
  338.1 0.9 reshape.436
  340.1 1.7 pad_maximum_fusion.1
  342.6 1.6 pad_maximum_fusion
  344.6 0.9 pad_maximum_fusion.2
  349.2 2.7 fusion.36
  353.1 1.9 add_bitcast_fusion
  (203 shorter events, 15.1 us)
Async XLA Ops:
  0.6 122.6 %copy-start.6 = (bf16[1,512,768]{2,1,0:T(8,128)(2,1)S(1)}, bf16[1,512,768]{2,1,0:T(8,128)(2,1)}, u32[]{:S(2)}) copy-start(bf16[1,512,768]{2,1,0:T(8,128)(2,1)} %param.16) | copy-start | bytes 2359300
  127.5 1.4 copy-start.2
  128.9 0.7 copy-start.32
  168.0 10.9 %copy-start.33 = (s32[4]{0:T(128)}, s32[4]{0:T(128)S(1)}, u32[]{:S(2)}) copy-start(s32[4]{0:T(128)S(1)} %convert_reduce_fusion.11) | copy-start | bytes 52
  181.7 17.5 %copy-start.35 = (s32[64]{0:T(128)S(1)}, s32[64]{0:T(128)}, u32[]{:S(2)}) copy-start(s32[64]{0:T(128)} %param.18) | copy-start | bytes 772
  189.4 28.9 %copy-start.28 = (bf16[4,768]{1,0:T(4,128)(2,1)}, bf16[4,768]{1,0:T(4,128)(2,1)S(1)}, u32[]{:S(2)}) copy-start(bf16[4,768]{1,0:T(4,128)(2,1)S(1)} %get-tuple-element.114) | copy-start | bytes 18436
  202.3 13.5 %copy-start.31 = (bf16[4,768]{1,0:T(4,128)(2,1)}, bf16[4,768]{1,0:T(4,128)(2,1)S(1)}, u32[]{:S(2)}) copy-start(bf16[4,768]{1,0:T(4,128)(2,1)S(1)} %get-tuple-element.62) | copy-start | bytes 18436
  209.4 8.8 %copy-start.19 = (bf16[4,3072]{1,0:T(4,128)(2,1)}, bf16[4,3072]{1,0:T(4,128)(2,1)S(1)}, u32[]{:S(2)}) copy-start(bf16[4,3072]{1,0:T(4,128)(2,1)S(1)} %fusion.73) | copy-start | bytes 73732
  211.4 7.6 %copy-start.3 = (bf16[512,2304]{0,1:T(8,128)(2,1)S(1)}, bf16[512,2304]{0,1:T(8,128)(2,1)}, u32[]{:S(2)}) copy-start(bf16[512,2304]{0,1:T(8,128)(2,1)} %copy-done.2) | copy-start | bytes 7077892
  216.5 1.7 copy-start.25
  218.2 0.6 copy-start.20
  218.3 0.6 copy-start.18
  218.4 1.5 copy-start.21
  219.6 0.6 copy-start.23
  220.9 3.2 copy-start.16
  227.8 99.2 %copy-start.26 = (bf16[4,768]{1,0:T(4,128)(2,1)}, bf16[4,768]{1,0:T(4,128)(2,1)S(1)}, u32[]{:S(2)}) copy-start(bf16[4,768]{1,0:T(4,128)(2,1)S(1)} %convert_element_type.170) | copy-start | bytes 18436
  324.5 1.0 copy-start
  327.3 11.7 %copy-start.1 = (bf16[32,124,96]{2,1,0:T(8,128)(2,1)S(1)}, bf16[32,124,96]{2,1,0:T(8,128)(2,1)}, u32[]{:S(2)}) copy-start(bf16[32,124,96]{2,1,0:T(8,128)(2,1)} %copy-done) | copy-start | bytes 2285572
  339.7 2.1 copy-start.4
  340.0 2.1 copy-start.5
  342.2 1.9 copy-start.15
  342.2 2.1 copy-start.14
  342.5 2.9 copy-start.13
  344.1 2.3 copy-start.12
  344.6 2.6 copy-start.11
  345.7 2.2 copy-start.10
  346.3 2.3 copy-start.9
  347.0 1.9 copy-start.8
  347.4 1.8 copy-start.22
  347.9 4.1 %copy-start.24 = (bf16[48,768]{1,0:T(8,128)(2,1)S(1)}, bf16[48,768]{1,0:T(8,128)(2,1)}, u32[]{:S(2)}) copy-start(bf16[48,768]{1,0:T(8,128)(2,1)} %copy-done.23) | copy-start | bytes 221188
  348.4 4.1 %copy-start.27 = (bf16[4,768]{1,0:T(4,128)(2,1)S(1)}, bf16[4,768]{1,0:T(4,128)(2,1)}, u32[]{:S(2)}) copy-start(bf16[4,768]{1,0:T(4,128)(2,1)} %copy-done.26) | copy-start | bytes 18436
  348.4 4.1 %copy-start.29 = (f32[4,768]{1,0:T(4,128)S(1)}, f32[4,768]{1,0:T(4,128)}, u32[]{:S(2)}) copy-start(f32[4,768]{1,0:T(4,128)} %get-tuple-element.59) | copy-start | bytes 36868
  348.6 3.4 copy-start.7
  348.8 4.1 %copy-start.34 = (s32[4]{0:T(128)S(1)}, s32[4]{0:T(128)}, u32[]{:S(2)}) copy-start(s32[4]{0:T(128)} %copy-done.33) | copy-start | bytes 52
  348.9 4.2 %copy-start.17 = (bf16[48,512]{1,0:T(8,128)(2,1)S(1)}, bf16[48,512]{1,0:T(8,128)(2,1)}, u32[]{:S(2)}) copy-start(bf16[48,512]{1,0:T(8,128)(2,1)} %copy-done.16) | copy-start | bytes 147460
  349.2 5.8 %copy-start.30 = (f32[96,4608]{1,0:T(8,128)}, f32[96,4608]{1,0:T(8,128)S(1)}, u32[]{:S(2)}) copy-start(f32[96,4608]{1,0:T(8,128)S(1)} %constant_dynamic-update-slice_fusion) | copy-start | bytes 5308420

commit v2 on v1

--- a/solution.py
+++ b/solution.py
@@ -51,177 +51,10 @@
     )
 
 
-def gather_kernel(widths, *refs):
-    kinds = len(widths)
-    sources, results = refs[:kinds], refs[kinds : 2 * kinds]
-    local, far_s, far_r, near_s, near_r, pass_s, pass_r, x_s, x_r, y_s, y_r, c_s, c_r = refs[2 * kinds :]
-    place = lax.axis_index("dp")
-    other = lax.axis_index("outer")
-    z, x = place // 2, place % 2
-    y, c = other // 2, other % 2
-    z_near = z + 1 - 2 * (z % 2)
-    z_far = 3 - z
-    z_last = 3 - z_near
-    tower = z // 2
-
-    def device(zz, xx, yy, cc):
-        return (zz * 2 + xx, yy * 2 + cc)
-
-    to_far = device(z_far, x, y, c)
-    to_near = device(z_near, x, y, c)
-    to_x = device(z, 1 - x, y, c)
-    to_y = device(z, x, 1 - y, c)
-    to_core = device(z, x, y, 1 - c)
-    barrier = pltpu.get_barrier_semaphore()
-    for peer in (to_far, to_near, to_x, to_y, to_core):
-        pl.semaphore_signal(barrier, inc=1, device_id=peer, device_id_type=MESH)
-    pl.semaphore_wait(barrier, 5)
-
-    def rows_of(k):
-        return sources[k].shape[0]
-
-    def own(k, which, half_row, half_col):
-        n, r = widths[k], rows_of(k)
-        row, rows = (half_row * (r // 2), r // 2)
-        col, cols = which * n, n
-        if half_col is not None:
-            col, cols = col + half_col * (n // 2), n // 2
-        return sources[k].at[
-            pl.ds(pl.multiple_of(row, 16), rows), pl.ds(pl.multiple_of(col, 128), cols)
-        ]
-
-    def full(k, zz, xx, half_row, half_col):
-        n, r = widths[k], rows_of(k)
-        row, rows = (zz * 2 + xx) * r + half_row * (r // 2), r // 2
-        col, cols = 0, n
-        if half_col is not None:
-            col, cols = half_col * (n // 2), n // 2
-            col = pl.multiple_of(col, 128)
-        return results[k].at[pl.ds(pl.multiple_of(row, 16), rows), pl.ds(col, cols)]
-
-    def remote(src, dst, s, r, peer):
-        return pltpu.make_async_remote_copy(
-            src_ref=src, dst_ref=dst, send_sem=s, recv_sem=r, device_id=peer, device_id_type=MESH
-        )
-
-    planes = (z, z_near, z_far, z_last)
-    sent = []
-
-    def go(copy):
-        copy.start()
-        sent.append(copy)
-
-    def x_copy(k, j):
-        src = own(k, tower, c, y) if j == 0 else full(k, planes[j], x, c, y)
-        return remote(src, full(k, planes[j], x, c, y), x_s.at[k, j], x_r.at[k, j], to_x)
-
-    def y_copy(k, j):
-        ref = full(k, planes[j], 1 - x, c, y)
-        return remote(ref, ref, y_s.at[k, j], y_r.at[k, j], to_y)
-
-    def c_copy(k, j):
-        ref = full(k, planes[j % 4], x if j < 4 else 1 - x, c, None)
-        return remote(ref, ref, c_s.at[k, j], c_r.at[k, j], to_core)
-
-    locals_ = []
-    for k in range(kinds):
-        go(remote(own(k, 1 - tower, c, None), full(k, z, x, c, None), far_s.at[k], far_r.at[k], to_far))
-        go(remote(own(k, tower, c, None), full(k, z, x, c, None), near_s.at[k], near_r.at[k], to_near))
-        go(x_copy(k, 0))
-        n, r = widths[k], rows_of(k)
-        copy = pltpu.make_async_copy(
-            sources[k].at[:, pl.ds(pl.multiple_of(tower * n, 128), n)],
-            results[k].at[pl.ds(pl.multiple_of((z * 2 + x) * r, 16), r), :],
-            local.at[k],
-        )
-        copy.start()
-        locals_.append(copy)
-
-    def wait_far(k):
-        ref = full(k, z_far, x, c, None)
-        remote(ref, ref, far_s.at[k], far_r.at[k], to_far).wait_recv()
-
-    def wait_near(k):
-        ref = full(k, z_near, x, c, None)
-        remote(ref, ref, near_s.at[k], near_r.at[k], to_near).wait_recv()
-
-    def wait_pass(k):
-        ref = full(k, z_last, x, c, None)
-        remote(ref, ref, pass_s.at[k], pass_r.at[k], to_near).wait_recv()
-
-    def wait_x(k, j):
-        ref = full(k, planes[j], 1 - x, c, y)
-        remote(ref, ref, x_s.at[k, j], x_r.at[k, j], to_x).wait_recv()
-
-    def wait_y(k, j):
-        ref = full(k, planes[j], 1 - x, c, 1 - y)
-        remote(ref, ref, y_s.at[k, j], y_r.at[k, j], to_y).wait_recv()
-
-    def wait_c(k, j):
-        ref = full(k, planes[j % 4], x if j < 4 else 1 - x, 1 - c, None)
-        remote(ref, ref, c_s.at[k, j], c_r.at[k, j], to_core).wait_recv()
-
-    def first(k):
-        wait_far(k)
-        ref = full(k, z_far, x, c, None)
-        go(remote(ref, ref, pass_s.at[k], pass_r.at[k], to_near))
-        go(x_copy(k, 2))
-        go(c_copy(k, 2))
-        wait_near(k)
-        go(x_copy(k, 1))
-        go(c_copy(k, 1))
-        wait_x(k, 0)
-        go(y_copy(k, 0))
-
-    def second(k):
-        wait_pass(k)
-        go(x_copy(k, 3))
-        go(c_copy(k, 3))
-        for j in (2, 1):
-            wait_x(k, j)
-            go(y_copy(k, j))
-
-    def third(k):
-        wait_x(k, 3)
-        go(y_copy(k, 3))
-        for j in (0, 2, 1, 3):
-            wait_y(k, j)
-            go(c_copy(k, 4 + j))
-
-    for step in range(kinds + 2):
-        if step < kinds:
-            first(step)
-        if 0 <= step - 1 < kinds:
-            second(step - 1)
-        if 0 <= step - 2 < kinds:
-            third(step - 2)
-    for k in range(kinds):
-        for j in range(1, 8):
-            wait_c(k, j)
-    for copy in sent:
-        copy.wait_send()
-    for copy in locals_:
-        copy.wait()
-
-
-def gather_weights(weights, widths, n_dp, n_outer):
-    if (n_dp, n_outer) != (8, 4):
-        tower = lax.axis_index("dp") * 2 // n_dp
-        whole = [lax.all_gather(w, "dp", axis=0, tiled=True) for w in weights]
-        return [lax.dynamic_slice_in_dim(w, tower * n, n, 1) for w, n in zip(whole, widths)]
-    kinds = len(weights)
-    sem = pltpu.SemaphoreType.DMA
-    return pl.pallas_call(
-        functools.partial(gather_kernel, widths),
-        out_shape=[jax.ShapeDtypeStruct((w.shape[0] * n_dp, n), w.dtype) for w, n in zip(weights, widths)],
-        in_specs=[pl.BlockSpec(memory_space=pl.ANY)] * kinds,
-        out_specs=[pl.BlockSpec(memory_space=pl.ANY)] * kinds,
-        scratch_shapes=[sem((kinds,))] * 7
-        + [sem((kinds, 4))] * 4
-        + [sem((kinds, 8))] * 2,
-        compiler_params=pltpu.CompilerParams(collective_id=1, has_side_effects=True),
-        name="gather_weights",
-    )(*weights)
+def gather_weights(weights, widths, n_dp):
+    tower = lax.axis_index("dp") * 2 // n_dp
+    whole = [lax.all_gather(w, "dp", axis=0, tiled=True) for w in weights]
+    return [lax.dynamic_slice_in_dim(w, tower * n, n, 1) for w, n in zip(whole, widths)]
 
 
 def spread_kernel(n_outer, total, whole_ref, parts_ref, all_ref, sliced_ref, local, s_one, r_one, s_two, r_two):
@@ -316,7 +149,7 @@
     rows_in, segments = text_rows[0], text_segments[0]
     row_len = rows_in.shape[0]
     widths = (3 * D, D, FF, D)
-    wm, wp, wu, wd = gather_weights((w_mix, w_proj, w_up, w_down), widths, n_dp, n_outer)
+    wm, wp, wu, wd = gather_weights((w_mix, w_proj, w_up, w_down), widths, n_dp)
     part_f, part_d = b_up.shape[0], b_rows.shape[0]
     small = jnp.concatenate([b_up.reshape(part_f // part_d, part_d, 2).transpose(0, 2, 1).reshape(-1, part_d), b_rows.T, g_rows.T], axis=0)
     small = lax.all_gather(small, "dp", axis=0)
@@ -460,10 +293,673 @@
     )
 
 
+PIECES = (
+    [(0, D, D), (0, 2 * D, D), (0, 0, D), (1, 0, D)]
+    + [(2, D * i, D) for i in range(4)]
+    + [(3, 256 * i, 256) for i in range(3)]
+)
+WIDTHS = (3 * D, D, FF, D)
+ROW = 16
+BLOCK = 256
+
+
+def iota(shape, dim):
+    return lax.broadcasted_iota(jnp.int32, shape, dim)
+
+
+def gelu_erf(u):
+    return 0.5 * u * (1.0 + lax.erf(u * 0.7071067811865476))
+
+
+def gelu_slope(u):
+    return 0.5 * (1.0 + lax.erf(u * 0.7071067811865476)) + u * (0.3989422804014327 * jnp.exp(-0.5 * u * u))
+
+
+def main_kernel(
+    x_ref, seg_ref, pos_ref, sv_ref, w_mix, w_proj, w_up, w_down,
+    enc_ref, drow_ref, fq_ref, fu_ref, fa_ref, se_ref, sl_ref,
+    wa, wd, sv_all, q_s, k_s, v_s, a_s, mask_s, b_s, h_s, hl_s, g_s, sel_s,
+    cls_own, cls_all, cls_f, src_q, src_u, src_a, src_e, src_l,
+    ld, far_s, near_s, z_r, rel_s, x_s, x_r, y_s, y_r, c_s, c_r, sv_sem, sv_r, cls_sem, cls_r,
+    fl, fz_s, fz_r, ff_s, ff_r, fg_s, fg_r, fc_s, fc_r, s1_s, s1_r, s2_s, s2_r, s3_s, s3_r,
+):
+    sources = (w_mix, w_proj, w_up, w_down)
+    place, other = lax.axis_index("dp"), lax.axis_index("outer")
+    z, x = place // 2, place % 2
+    y, c = other // 2, other % 2
+    tower, zi = z // 2, z % 2
+    me = place * 4 + other
+    inner = zi * (1 - tower) + (1 - zi) * tower
+    zn = z + 1 - 2 * zi
+    z_a, z_b = 2 - tower, 3 - 3 * tower
+    scaled = HEAD_DIM ** (-0.5)
+    row_len = x_ref.shape[0]
+
+    def device(zz, xx, yy, cc):
+        return (zz * 2 + xx, yy * 2 + cc)
+
+    to_near, to_far = device(zn, x, y, c), device(z_a, x, y, c)
+    to_x, to_y, to_core = device(z, 1 - x, y, c), device(z, x, 1 - y, c), device(z, x, y, 1 - c)
+
+    barrier = pltpu.get_barrier_semaphore()
+
+    def peer_at(i):
+        p = lax.rem(me + i, 32)
+        return (p // 4, lax.rem(p, 4))
+
+    def greet(i, carry):
+        pl.semaphore_signal(barrier, inc=1, device_id=peer_at(i), device_id_type=MESH)
+        return carry
+
+    lax.fori_loop(1, 32, greet, 0)
+    pl.semaphore_wait(barrier, 31)
+
+    def remote(src, dst, s, r, peer):
+        return pltpu.make_async_remote_copy(
+            src_ref=src, dst_ref=dst, send_sem=s, recv_sem=r, device_id=peer, device_id_type=MESH
+        )
+
+    def arrived(ref, s, r):
+        remote(ref, ref, s, r, to_x).wait_recv()
+
+    sent = []
+
+    def go(copy):
+        copy.start()
+        sent.append(copy)
+
+    def dims(k):
+        tensor, first, cols = PIECES[k]
+        return tensor, sources[tensor].shape[0], first, cols
+
+    def own(k, which, half_row, half_col):
+        tensor, r, first, n = dims(k)
+        row, rows = (0, r) if half_row is None else (half_row * (r // 2), r // 2)
+        col, cols = which * WIDTHS[tensor] + first, n
+        if half_col is not None:
+            col, cols = col + half_col * (n // 2), n // 2
+        return sources[tensor].at[
+            pl.ds(pl.multiple_of(row, 16), rows), pl.ds(pl.multiple_of(col, 128), cols)
+        ]
+
+    def held(k):
+        return wa.at[k] if k < 8 else wd.at[k - 8]
+
+    def full(k, zz, xx, half_row, half_col):
+        tensor, r, first, n = dims(k)
+        row, rows = (zz * 2 + xx) * r, r
+        if half_row is not None:
+            row, rows = row + half_row * (r // 2), r // 2
+        col, cols = (0, n) if half_col is None else (pl.multiple_of(half_col * (n // 2), 128), n // 2)
+        return held(k).at[pl.ds(pl.multiple_of(row, 16), rows), pl.ds(col, cols)]
+
+    planes = (z, zn, z_a, z_b)
+    kinds = len(PIECES)
+    local = []
+
+    def stage0(k):
+        go(remote(own(k, 1 - tower, None, c), full(k, z, x, None, c), far_s.at[k], z_r.at[k, 2 - inner], to_far))
+        go(remote(own(k, tower, y, c), full(k, z, x, y, c), near_s.at[k], z_r.at[k, 0], to_near))
+        go(remote(own(k, tower, None, c), full(k, z, x, None, c), x_s.at[k, 0], x_r.at[k, 0], to_x))
+        copy = pltpu.make_async_copy(own(k, tower, None, c), full(k, z, x, None, c), ld.at[k])
+        copy.start()
+        local.append(copy)
+
+    def stage1(k):
+        ref = full(k, zn, x, y, c)
+        arrived(ref, near_s.at[k], z_r.at[k, 0])
+        go(remote(ref, ref, x_s.at[k, 1], x_r.at[k, 1], to_x))
+        go(remote(ref, ref, y_s.at[k, 0], y_r.at[k, 0], to_y))
+        for j, zz in ((1, z_a), (2, z_b)):
+            whole = full(k, zz, x, None, c)
+            arrived(whole, near_s.at[k], z_r.at[k, j])
+
+            @pl.when(inner == 1)
+            def _():
+                remote(whole, whole, rel_s.at[k, j - 1], z_r.at[k, j], to_near).start()
+
+            ref = full(k, zz, x, y, c)
+            go(remote(ref, ref, x_s.at[k, 1 + j], x_r.at[k, 1 + j], to_x))
+
+    def stage2(k):
+        arrived(full(k, z, 1 - x, None, c), x_s.at[k, 0], x_r.at[k, 0])
+        for j in (1, 2, 3):
+            ref = full(k, planes[j], 1 - x, y, c)
+            arrived(ref, x_s.at[k, j], x_r.at[k, j])
+            go(remote(ref, ref, y_s.at[k, j], y_r.at[k, j], to_y))
+
+    def stage3(k):
+        arrived(full(k, zn, x, 1 - y, c), y_s.at[k, 0], y_r.at[k, 0])
+        for j in (1, 2, 3):
+            arrived(full(k, planes[j], 1 - x, 1 - y, c), y_s.at[k, j], y_r.at[k, j])
+        local[k].wait()
+        n = dims(k)[3]
+        ref = held(k).at[:, pl.ds(pl.multiple_of(c * (n // 2), 128), n // 2)]
+        go(remote(ref, ref, c_s.at[k], c_r.at[k], to_core))
+
+    def stage4(k):
+        n = dims(k)[3]
+        ref = held(k).at[:, pl.ds(pl.multiple_of((1 - c) * (n // 2), 128), n // 2)]
+        arrived(ref, c_s.at[k], c_r.at[k])
+
+    def sv_copy(i):
+        there = lax.rem(place + i, 8)
+        return remote(sv_ref.at[there // 4], sv_all.at[place], sv_sem.at[i], sv_r.at[i], (there, other))
+
+    WINDOW = 2
+    for k in range(WINDOW):
+        stage0(k)
+    for i in range(1, 8):
+        sv_copy(i).start()
+    sv_all[place] = sv_ref[tower]
+
+    sel_row, sel_col = iota((D, 1024), 0), iota((D, 1024), 1)
+    lane = sel_col % 128
+    sel_s[...] = jnp.where((sel_row == (sel_col // 128) * 96 + lane) & (lane < 96), 1.0, 0.0).astype(BF)
+    segments = seg_ref[...]
+    level = iota((ROW, row_len), 0)
+    begin = jnp.sum(jnp.where(segments < level, 1.0, 0.0), axis=1, keepdims=True).astype(jnp.int32)
+    spot = jnp.where((iota((ROW, row_len), 1) == begin) & (level < SEGS), 1.0, 0.0).astype(BF)
+    belongs = jnp.where((segments == level) & (level < SEGS), 1.0, 0.0).astype(BF)
+    mask_s[...] = (dot_over_rows(belongs, belongs) - 1.0) * -masked_score
+    wide_row, wide_col = iota((48, D), 0), iota((48, D), 1)
+    own_head = (wide_row // SEGS) == (wide_col // HEAD_DIM)
+    repeat = jnp.where(iota((48, ROW), 0) % SEGS == iota((48, ROW), 1), 1.0, 0.0).astype(BF)
+    open_keys = (iota((48, row_len), 0) % SEGS) == segments
+    row16 = iota((ROW, D), 0)
+    x_r_rows = dot_plain(spot, x_ref[...])
+    x_low = x_r_rows.astype(BF)
+
+    def widen(rows):
+        return jnp.where(own_head, dot_plain(repeat, rows), 0.0)
+
+    def narrow(wide):
+        return dot_over_rows(repeat, jnp.where(own_head, wide, 0.0).astype(BF))
+
+    state = {}
+
+    def small_vectors():
+        for i in range(1, 8):
+            sv_copy(i).wait_recv()
+        rows = jnp.zeros((ROW, D), F32)
+        for m in range(8):
+            put = jnp.where((iota((128, D), 1) == iota((128, D), 0) + 96 * m) & (iota((128, D), 0) < 96), 1.0, 0.0)
+            rows = rows + dot_plain(sv_all[m][:, :128], put.astype(BF))
+        names = ("bq", "bv", "bo", "o1", "bd", "o2", "g1", "g2")
+        for i, name in enumerate(names):
+            state[name] = rows[1 + i : 2 + i, :]
+        state["cu"] = [
+            jnp.concatenate([sv_all[2 * j][0:1, :], sv_all[2 * j + 1][0:1, :]], axis=1).astype(F32) for j in range(4)
+        ]
+
+    def mix(k, out, bias, factor):
+        for n in range(0, D, BLOCK):
+            m = dot_plain(x_ref[...], wa[k, :, n : n + BLOCK])
+            if bias is not None:
+                m = m + state[bias][:, n : n + BLOCK]
+            m = m.astype(BF)
+            if factor is not None:
+                m = m * jnp.asarray(factor, BF)
+            out[:, n : n + BLOCK] = m
+
+    def attend(low, high):
+        rows = 256
+        per = row_len // rows
+
+        def body(i, carry):
+            pair, part = i // per, lax.rem(i, per)
+            cols = pl.ds(pl.multiple_of(pair * 128, 128), 128)
+            at = pl.ds(pl.multiple_of(part * rows, rows), rows)
+            qp, kp, vp = q_s[at, cols], k_s[:, cols], v_s[:, cols]
+            left = iota((rows, 128), 1) < HEAD_DIM
+            found = []
+            for keep in (left, jnp.logical_not(left)):
+                s = dot_over_columns(jnp.where(keep, qp, jnp.zeros((), BF)), kp) + mask_s[at, :]
+                e = jnp.exp(s - jnp.max(s, axis=1, keepdims=True))
+                p = (e * (1.0 / jnp.sum(e, axis=1, keepdims=True))).astype(BF)
+                found.append(dot_plain(p, vp))
+            a_s[at, cols] = jnp.where(left, found[0], found[1]).astype(BF)
+            return carry
+
+        lax.fori_loop(low * per, high * per, body, 0)
+
+    def project():
+        for n in range(0, D, BLOCK):
+            b_s[:, n : n + BLOCK] = (
+                x_ref[:, n : n + BLOCK].astype(F32)
+                + dot_plain(a_s[...], wa[3, :, n : n + BLOCK])
+                + state["bo"][:, n : n + BLOCK]
+            )
+
+        def body(i, carry):
+            at = pl.ds(pl.multiple_of(i * 128, 128), 128)
+            unit, _ = norm_parts(b_s[at, :])
+            h = unit * state["g1"] + state["o1"]
+            h_s[at, :] = h
+            hl_s[at, :] = h.astype(BF)
+            return carry
+
+        lax.fori_loop(0, row_len // 128, body, 0)
+
+    def up(j):
+        for n in range(0, D, BLOCK):
+            u = dot_plain(hl_s[...], wa[4 + j, :, n : n + BLOCK]) + state["cu"][j][:, n : n + BLOCK]
+            g_s[j, :, n : n + BLOCK] = gelu_erf(u).astype(BF)
+
+    def down(j):
+        cols = slice(256 * j, 256 * j + 256)
+        total = h_s[:, cols] + state["bd"][:, cols]
+        for i in range(4):
+            total = total + dot_plain(g_s[i], wd[j, D * i : D * i + D, :])
+        b_s[:, cols] = total
+
+    def finish():
+        def body(i, carry):
+            at = pl.ds(pl.multiple_of(i * 128, 128), 128)
+            unit, _ = norm_parts(b_s[at, :])
+            enc_ref[at, :] = (unit * state["g2"] + state["o2"]).astype(BF)
+            return carry
+
+        lax.fori_loop(0, row_len // 128, body, 0)
+
+    def rows_attention():
+        q_r = (dot_plain(x_low, wa[2]) + state["bq"]).astype(BF)
+        state["q_r"] = q_r
+        q_wide = (widen(q_r) * scaled).astype(BF)
+        state["q_wide"] = q_wide
+        s = jnp.where(open_keys, dot_over_columns(q_wide, k_s[...]), masked_score)
+        e = jnp.exp(s - jnp.max(s, axis=1, keepdims=True))
+        p = e * (1.0 / jnp.sum(e, axis=1, keepdims=True))
+        state["p"] = p
+        state["p_low"] = p.astype(BF)
+        state["a_r"] = narrow(dot_plain(state["p_low"], v_s[...])).astype(BF)
+
+    def rows_project():
+        before = x_r_rows + dot_plain(state["a_r"], wa[3]) + state["bo"]
+        unit, inverse = norm_parts(before)
+        state["unit1"], state["inv1"] = unit, inverse
+        state["h_r"] = unit * state["g1"] + state["o1"]
+        state["hl_r"] = state["h_r"].astype(BF)
+        state["u_r"], state["g_r"], state["f_r"] = [], [], []
+
+    def rows_up(j):
+        u = dot_plain(state["hl_r"], wa[4 + j]) + state["cu"][j]
+        state["u_r"].append(u)
+        state["g_r"].append(gelu_erf(u).astype(BF))
+
+    def rows_down(j):
+        f = jnp.zeros((ROW, 256), F32)
+        for i in range(4):
+            f = f + dot_plain(state["g_r"][i], wd[j, D * i : D * i + D, :])
+        state["f_r"].append(f)
+
+    def rows_finish():
+        before = state["h_r"] + jnp.concatenate(state["f_r"], axis=1) + state["bd"]
+        unit, inverse = norm_parts(before)
+        state["unit2"], state["inv2"] = unit, inverse
+        e = (unit * state["g2"] + state["o2"]).astype(BF)
+        cls_own[...] = e[:SEGS, :]
+        cls_all[me] = e[:SEGS, :]
+
+    after = {
+        0: [lambda: small_vectors(), lambda: mix(0, k_s, None, None)],
+        1: [lambda: mix(1, v_s, "bv", None)],
+        2: [lambda: mix(2, q_s, "bq", scaled), rows_attention, lambda: attend(0, 2)],
+        3: [rows_project, lambda: attend(2, 4)],
+        4: [lambda: rows_up(0), lambda: attend(4, 6)],
+        5: [lambda: rows_up(1), project, lambda: up(0)],
+        6: [lambda: rows_up(2), lambda: up(1)],
+        7: [lambda: rows_up(3), lambda: up(2)],
+        8: [lambda: rows_down(0), lambda: up(3)],
+        9: [lambda: rows_down(1), lambda: down(0)],
+        10: [lambda: rows_down(2), rows_finish],
+    }
+    for i in range(kinds + 3):
+        if i + WINDOW < kinds:
+            stage0(i + WINDOW)
+        if i < kinds:
+            stage1(i)
+        if 0 <= i - 1 < kinds:
+            stage2(i - 1)
+        if 0 <= i - 2 < kinds:
+            stage3(i - 2)
+        if 0 <= i - 3 < kinds:
+            stage4(i - 3)
+            for unit in after[i - 3]:
+                unit()
+
+    def cls_copy(i):
+        return remote(cls_own, cls_all.at[me], cls_sem.at[i], cls_r.at[i], peer_at(i))
+
+    def cls_send(i, carry):
+        cls_copy(i).start()
+        return carry
+
+    lax.fori_loop(1, 32, cls_send, 0)
+
+    xf, yf = x + (1 - c) * (1 - 2 * x), y + c * (1 - 2 * y)
+    xg, yg = x + c * (1 - 2 * x), y + (1 - c) * (1 - 2 * y)
+    to_f, to_g = device(z, xf, yf, c), device(z, xg, yg, c)
+    wholes = ((src_q, fq_ref), (src_u, fu_ref), (src_a, fa_ref))
+    sliced = ((src_e, se_ref), (src_l, sl_ref))
+
+    def slot(ref):
+        return ref.at[tower, c, x, y, zi]
+
+    def whole_z(i):
+        src, dst = wholes[i]
+        for r in (1, 2, 3):
+            go(remote(src, slot(dst), fz_s.at[i, r], fz_r.at[i, r], device(lax.rem(z + r, 4), x, y, c)))
+        copy = pltpu.make_async_copy(src, slot(dst), fl.at[i])
+        copy.start()
+        copy.wait()
+
+    def whole_f(i):
+        src, dst = wholes[i]
+        for r in (1, 2, 3):
+            arrived(slot(dst), fz_s.at[i, r], fz_r.at[i, r])
+        ref = dst.at[:, c, x, y]
+        go(remote(ref, ref, ff_s.at[i], ff_r.at[i], to_f))
+        go(remote(ref, ref, fg_s.at[i, 0], fg_r.at[i, 0], to_g))
+
+    def whole_g(i):
+        dst = wholes[i][1]
+        ref = dst.at[:, c, xf, yf]
+        arrived(ref, ff_s.at[i], ff_r.at[i])
+        go(remote(ref, ref, fg_s.at[i, 1], fg_r.at[i, 1], to_g))
+
+    def whole_c(i):
+        dst = wholes[i][1]
+        for j in (0, 1):
+            arrived(dst.at[:, c, xg, yg], fg_s.at[i, j], fg_r.at[i, j])
+        ref = dst.at[:, c]
+        go(remote(ref, ref, fc_s.at[i], fc_r.at[i], to_core))
+
+    def whole_end(i):
+        arrived(wholes[i][1].at[:, c], fc_s.at[i], fc_r.at[i])
+
+    def slice_1(i):
+        src, dst = sliced[i]
+        for r in range(1, 8):
+            there = lax.rem(place + r, 8)
+            go(remote(src.at[there], slot(dst), s1_s.at[i, r], s1_r.at[i, r], (there, other)))
+        copy = pltpu.make_async_copy(src.at[place], slot(dst), fl.at[3 + i])
+        copy.start()
+        copy.wait()
+
+    def slice_2(i):
+        dst = sliced[i][1]
+        for r in range(1, 8):
+            arrived(slot(dst), s1_s.at[i, r], s1_r.at[i, r])
+        ref = dst.at[:, c, :, y]
+        go(remote(ref, ref, s2_s.at[i], s2_r.at[i], to_y))
+
+    def slice_3(i):
+        dst = sliced[i][1]
+        arrived(dst.at[:, c, :, y], s2_s.at[i], s2_r.at[i])
+        ref = dst.at[:, c]
+        go(remote(ref, ref, s3_s.at[i], s3_r.at[i], to_core))
+
+    def slice_end(i):
+        arrived(sliced[i][1].at[:, c], s3_s.at[i], s3_r.at[i])
+
+    first_rows = row16 < SEGS
+
+    def top(rows):
+        return jnp.where(row16[:, : rows.shape[1]] < SEGS, rows, 0.0)
+
+    q_f32 = top(state["q_r"].astype(F32))
+    src_q[...] = q_f32.astype(BF)
+    whole_z(0)
+    hl_f32, a_f32, x_f32 = (top(m.astype(F32)) for m in (state["hl_r"], state["a_r"], x_low))
+    four = hl_f32
+    for r in (4, 8, 12):
+        four = four + pltpu.roll(hl_f32, r, 0)
+    pair = pltpu.roll(a_f32, 4, 0) + pltpu.roll(x_f32, 8, 0)
+    z_rows = dot_plain(state["p_low"], x_ref[...])
+    early = jnp.concatenate([four, pair, z_rows], axis=0).astype(BF)
+    early = dot_plain(early, sel_s[...]).astype(BF)
+    for d in range(8):
+        src_e[d, :80, :] = early[:, 128 * d : 128 * d + 128]
+        for b in range(3):
+            first = 384 * d + 128 * b
+            g = state["g_r"][first // D][:, first % D : first % D + 128]
+            src_e[d, 80 + 16 * b : 96 + 16 * b, :] = top(g.astype(F32)).astype(BF)
+    slice_1(0)
+
+    down(1)
+    down(2)
+    finish()
+
+    def cls_wait(i, carry):
+        cls_copy(i).wait_recv()
+        return carry
+
+    lax.fori_loop(1, 32, cls_wait, 0)
+    for i in range(32):
+        cls_f[SEGS * i : SEGS * i + SEGS, :] = cls_all[i].astype(F32)
+    all_q, all_p = cls_f[:64, :].astype(BF), cls_f[64:, :].astype(BF)
+    pair_scale = 2.0 * D ** (-0.5)
+    logits = dot_over_columns(all_p, all_q) * pair_scale
+    raised = jnp.exp(logits - jnp.max(logits, axis=0, keepdims=True))
+    hit = jnp.where(iota((64, 64), 0) == pos_ref[...], 1.0, 0.0)
+    d_logits = (raised / jnp.sum(raised, axis=0, keepdims=True) - hit).astype(BF)
+    position = me * SEGS - tower * 64
+    take = jnp.where((iota((ROW, 64), 1) == iota((ROW, 64), 0) + position) & (iota((ROW, 64), 0) < SEGS), 1.0, 0.0)
+    take = take.astype(BF)
+    d_q = dot_plain(dot_over_columns(take, d_logits).astype(BF), all_p)
+    d_p = dot_plain(dot_plain(take, d_logits).astype(BF), all_q)
+    d_cls = jnp.where(tower == 0, d_q, d_p) * pair_scale
+
+    def total(rows):
+        return jnp.sum(rows, axis=0, keepdims=True)
+
+    vec_g2, vec_o2 = total(d_cls * state["unit2"]), total(d_cls)
+    dz2 = norm_back(state["unit2"], state["inv2"], state["g2"], d_cls)
+    df = dz2.astype(BF)
+    whole_f(0)
+    dh = dz2
+    du_rows = []
+    for j in range(4):
+        dg = jnp.zeros((ROW, D), F32)
+        for i in range(3):
+            dg = dg + dot_over_columns(df[:, 256 * i : 256 * i + 256], wd[i, D * j : D * j + D, :])
+        du = (dg * gelu_slope(state["u_r"][j])).astype(BF)
+        du_rows.append(du.astype(F32))
+    packed = du_rows[0]
+    for j in (1, 2, 3):
+        packed = packed + pltpu.roll(du_rows[j], 4 * j, 0)
+    src_u[...] = packed.astype(BF)
+    whole_z(1)
+    slice_2(0)
+    whole_g(0)
+    for j in range(4):
+        dh = dh + dot_over_columns(du_rows[j].astype(BF), wa[4 + j])
+    vec_g1, vec_o1 = total(dh * state["unit1"]), total(dh)
+    dz1 = norm_back(state["unit1"], state["inv1"], state["g1"], dh)
+    db = dz1.astype(BF)
+    whole_f(1)
+    slice_3(0)
+    whole_c(0)
+    da = dot_over_columns(db, wa[3]).astype(BF)
+    a_wide = widen(da).astype(BF)
+    d_p_rows = dot_over_columns(a_wide, v_s[...])
+    p = state["p"]
+    ds = (p * (d_p_rows - jnp.sum(p * d_p_rows, axis=1, keepdims=True))).astype(BF)
+    dq = narrow(dot_plain(ds, k_s[...]) * scaled).astype(BF)
+    df_f, db_f, da_f, dq_f = (m.astype(F32) for m in (df, db, da, dq))
+    src_a[...] = (df_f + pltpu.roll(db_f, 4, 0) + pltpu.roll(dq_f, 8, 0) + pltpu.roll(da_f, 12, 0)).astype(BF)
+    whole_z(2)
+    whole_g(1)
+    y_rows = dot_plain(ds, x_ref[...]) * scaled
+    weight_sum = jnp.sum(state["p_low"].astype(F32), axis=1, keepdims=True)
+    vec_bv = total(weight_sum * a_wide.astype(F32))
+    vectors = jnp.concatenate(
+        [total(dq_f), vec_bv, total(db_f), vec_o1, total(df_f), vec_o2, vec_g1, vec_g2, jnp.zeros((8, D), F32)], axis=0
+    )
+    late = jnp.concatenate([y_rows, vectors], axis=0).astype(BF)
+    late = dot_plain(late, sel_s[...]).astype(BF)
+    for d in range(8):
+        src_l[d] = late[:, 128 * d : 128 * d + 128]
+    slice_1(1)
+    whole_f(2)
+    whole_c(1)
+
+    t_k = dot_over_columns(state["q_wide"], wa[0]).astype(BF)
+    t_v = dot_over_columns(a_wide, wa[1]).astype(BF)
+    at_rows = dz1 + dot_over_columns(dq, wa[2])
+    high = at_rows.astype(BF)
+    rest = (at_rows - high.astype(F32)).astype(BF)
+    left = jnp.concatenate([ds, state["p_low"], spot, spot], axis=0)
+    right = jnp.concatenate([t_k, t_v, high, rest], axis=0)
+    whole_g(2)
+    slice_2(1)
+    for n in range(0, D, BLOCK):
+        drow_ref[:, n : n + BLOCK] = dot_over_rows(left, right[:, n : n + BLOCK])
+    whole_c(2)
+    slice_3(1)
+    for i in range(3):
+        whole_end(i)
+    for i in range(2):
+        slice_end(i)
+
+    for copy in sent:
+        copy.wait_send()
+    for k in range(kinds):
+
+        @pl.when(inner == 1)
+        def _():
+            for j, zz in ((1, z_a), (2, z_b)):
+                ref = full(k, zz, x, None, c)
+                remote(ref, ref, rel_s.at[k, j - 1], z_r.at[k, j], to_near).wait_send()
+
+    for i in range(1, 8):
+        sv_copy(i).wait_send()
+
+    def cls_sent(i, carry):
+        cls_copy(i).wait_send()
+        return carry
+
+    lax.fori_loop(1, 32, cls_sent, 0)
+
+
+def grads_kernel(fq_ref, fu_ref, fa_ref, se_ref, sl_ref, mix_ref, proj_ref, up_ref, down_ref, upb_ref, rowb_ref, gain_ref):
+    place = lax.axis_index("dp")
+    kind = iota((256, 128), 0) % ROW
+    part = 96
+    pick = iota((192, 64), 0)
+    group, within = pick // 48, pick % SEGS
+    head_row, head_col = iota((192, D), 0), iota((192, D), 1)
+    own_head = (head_row % 48) // SEGS == head_col // HEAD_DIM
+    take_q = jnp.where(iota((192, 64), 1) == group * ROW + within, 1.0, 0.0).astype(BF)
+    take_a = jnp.where(iota((192, 64), 1) == group * ROW + within + 12, 1.0, 0.0).astype(BF)
+    kind16, col16 = iota((256, ROW), 0) % ROW, iota((256, ROW), 1)
+    biases = jnp.zeros((128, ROW), F32)
+    gains = jnp.zeros((128, ROW), F32)
+    up_bias = jnp.zeros((384, ROW), F32)
+    for t in range(2):
+        def keep(ref_rows, lo, hi):
+            return jnp.where((kind >= lo) & (kind < hi), ref_rows, jnp.zeros((), BF))
+
+        four = se_ref[t, :, 0:16, :].reshape(256, 128)
+        two = se_ref[t, :, 16:32, :].reshape(256, 128)
+        fa, fu = fa_ref[t], fu_ref[t]
+        mix_ref[:, 3 * D * t : 3 * D * t + D] = dot_over_rows(keep(two, 8, 12), fa)[:part]
+        proj_ref[:, D * t : D * t + D] = dot_over_rows(keep(two, 4, 8), fa)[:part]
+        for j in range(4):
+            first = FF * t + D * j
+            up_ref[:, first : first + D] = dot_over_rows(keep(four, 4 * j, 4 * j + 4), fu)[:part]
+        for b in range(3):
+            g = se_ref[t, :, 80 + 16 * b : 96 + 16 * b, :].reshape(256, 128)
+            down_ref[128 * b : 128 * b + 128, D * t : D * t + D] = dot_over_rows(g, fa)
+        gk = jnp.zeros((128, D), F32)
+        gv = jnp.zeros((128, D), F32)
+        for s in range(4):
+            q_wide = jnp.where(own_head, dot_plain(take_q, fq_ref[t, 64 * s : 64 * s + 64, :]), 0.0).astype(BF)
+            a_wide = jnp.where(own_head, dot_plain(take_a, fa[64 * s : 64 * s + 64, :]), 0.0).astype(BF)
+            y = sl_ref[t, 4 * s : 4 * s + 4, 0:48, :].reshape(192, 128)
+            z = se_ref[t, 4 * s : 4 * s + 4, 32:80, :].reshape(192, 128)
+            gk = gk + dot_over_rows(y, q_wide)
+            gv = gv + dot_over_rows(z, a_wide)
+        mix_ref[:, 3 * D * t + D : 3 * D * t + 2 * D] = gk[:part]
+        mix_ref[:, 3 * D * t + 2 * D : 3 * D * t + 3 * D] = gv[:part]
+        vec = sl_ref[t, :, 48:64, :].reshape(256, 128)
+        to_bias = jnp.where((kind16 < 6) & (col16 == kind16 + 6 * t), 1.0, 0.0).astype(BF)
+        to_gain = jnp.where((kind16 >= 6) & (kind16 < 8) & (col16 == kind16 - 6 + 2 * t), 1.0, 0.0).astype(BF)
+        biases = biases + dot_over_rows(vec, to_bias)
+        gains = gains + dot_over_rows(vec, to_gain)
+        mine = fu_ref[t, :, pl.ds(pl.multiple_of(place % 2 * 384, 128), 384)]
+        to_up = jnp.where((kind16 // 4 == place // 2) & (col16 == t), 1.0, 0.0).astype(BF)
+        up_bias = up_bias + dot_over_rows(mine, to_up)
+    rowb_ref[...] = biases[:part, :12]
+    gain_ref[...] = gains[:part, :4]
+    upb_ref[...] = up_bias[:, :2]
+
+
+def fast_device(text_rows, text_segments, positives, w_mix, w_proj, w_up, w_down, b_up, b_rows, g_rows):
+    sem = pltpu.SemaphoreType.DMA
+    vm = pltpu.VMEM
+    part = b_rows.shape[0]
+    towers = []
+    for t in range(2):
+        narrow = jnp.concatenate([b_rows[:, 6 * t : 6 * t + 6], g_rows[:, 2 * t : 2 * t + 2]], axis=1).T
+        narrow = jnp.pad(narrow, ((0, 7), (0, 4 * part - part)))
+        towers.append(jnp.concatenate([b_up[:, t][None, :], narrow], axis=0))
+    small = jnp.stack(towers)
+    kinds = len(PIECES)
+    fulls = jax.ShapeDtypeStruct((2, 2, 2, 2, 2, ROW, D), BF)
+    row_len = text_rows.shape[1]
+    here, there = pl.BlockSpec(memory_space=vm), pl.BlockSpec(memory_space=pl.ANY)
+    encoded, d_rows, fq, fu, fa, se, sl = pl.pallas_call(
+        main_kernel,
+        out_shape=[
+            jax.ShapeDtypeStruct((row_len, D), BF),
+            jax.ShapeDtypeStruct((row_len, D), F32),
+            fulls, fulls, fulls,
+            jax.ShapeDtypeStruct((2, 2, 2, 2, 2, 128, 128), BF),
+            jax.ShapeDtypeStruct((2, 2, 2, 2, 2, 64, 128), BF),
+        ],
+        in_specs=[here] * 4 + [there] * 4,
+        out_specs=[here] * 2 + [there] * 5,
+        scratch_shapes=[
+            vm((8, D, D), BF), vm((3, FF, 256), BF), vm((8, ROW, 384), BF),
+            vm((row_len, D), BF), vm((row_len, D), BF), vm((row_len, D), BF), vm((row_len, D), BF),
+            vm((row_len, row_len), F32), vm((row_len, D), F32), vm((row_len, D), F32), vm((row_len, D), BF),
+            vm((4, row_len, D), BF), vm((D, 1024), BF),
+            vm((SEGS, D), BF), vm((32, SEGS, D), BF), vm((128, D), F32),
+            vm((ROW, D), BF), vm((ROW, D), BF), vm((ROW, D), BF), vm((8, 128, 128), BF), vm((8, 64, 128), BF),
+            sem((kinds,)), sem((kinds,)), sem((kinds,)), sem((kinds, 3)), sem((kinds, 2)),
+            sem((kinds, 4)), sem((kinds, 4)), sem((kinds, 4)), sem((kinds, 4)), sem((kinds,)), sem((kinds,)),
+            sem((8,)), sem((8,)), sem((32,)), sem((32,)),
+            sem((5,)), sem((3, 4)), sem((3, 4)), sem((3,)), sem((3,)), sem((3, 2)), sem((3, 2)), sem((3,)), sem((3,)),
+            sem((2, 8)), sem((2, 8)), sem((2,)), sem((2,)), sem((2,)), sem((2,)),
+        ],
+        compiler_params=pltpu.CompilerParams(collective_id=5, has_side_effects=True, vmem_limit_bytes=60 << 20),
+        name="main_step",
+    )(text_rows[0], text_segments, positives[None, :], small, w_mix, w_proj, w_up, w_down)
+    shape = lambda r, n: jax.ShapeDtypeStruct((r, n), F32)
+    grads = pl.pallas_call(
+        grads_kernel,
+        out_shape=[
+            shape(part, 6 * D), shape(part, 2 * D), shape(part, 2 * FF), shape(4 * part, 2 * D),
+            shape(4 * part, 2), shape(part, 12), shape(part, 4),
+        ],
+        in_specs=[here] * 5,
+        out_specs=[here] * 7,
+        compiler_params=pltpu.CompilerParams(vmem_limit_bytes=60 << 20),
+        name="weight_grads",
+    )(
+        fq.reshape(2, 256, D), fu.reshape(2, 256, D), fa.reshape(2, 256, D),
+        se.reshape(2, 16, 128, 128), sl.reshape(2, 16, 64, 128),
+    )
+    return (encoded[None], d_rows[None], *grads)
+
+
 def solution(mesh):
     rows, cols = P(("dp", "outer"), None, None), P("dp", None)
+    sizes = (mesh.shape["dp"], mesh.shape["outer"])
     return jax.shard_map(
-        per_device,
+        fast_device if sizes == (8, 4) else per_device,
         mesh=mesh,
         in_specs=(rows, P(("dp", "outer"), None), P(), cols, cols, cols, cols, cols, cols, cols),
         out_specs=(rows, rows, cols, cols, cols, cols, cols, cols, cols),

time: 356 us -> 139 us (0.39)
  the two profiles are of different devices: /device:TPU:15 before, /device:TPU:1 now
where the time goes in v2:
time: 139 us
  Pallas kernels  128 us (92%)
  local copies, waits for them, and re-layouts  8.97 us (6%)
    pallas_call x1, Pallas kernels, fast_device(): pl.pallas_call(main_kernel, out_shape=[jax.ShapeDtypeStruct((row_len, D),...  121 us
    pallas_call x1, Pallas kernels, fast_device(): pl.pallas_call(grads_kernel, out_shape=[shape(part, 6 * D), shape(part, 2...  7.74 us
    unnamed x9, local copies, waits for them, and re-layouts  6.68 us

profile of v2, /device:TPU:1, one launch (start us, length us, event | category | flops | bytes accessed | tf_op | source)
XLA Modules:
  0.0 138.5 jit_solution(10341755278247911438)
XLA Ops:
  0.6 0.8 fusion.7
  1.4 0.8 slice_bitcast_fusion.1
  2.2 0.8 fusion.6
  3.0 0.6 pad_maximum_fusion.sv_ref
  3.6 120.5 %main_step.1 = (bf16[512,768]{1,0:T(8,128)(2,1)}, f32[512,768]{1,0:T(8,128)}, bf16[2,2,2,2,2,16,768]{6,5,4,3,2,1,0:T(8,128)(2,1)}, bf16[2,2,2,2,2,16,768]{6,5,4,...) custom-call(bf16[512,768]{1,0:T(8,128)(2,1)} %bitcast.24, ...), custom_call_target="tpu_custom_call" | custom-call | tf_op jit(solution)/shard_map/main_step/pallas_call | solution.py:913
  124.1 0.0 copy-start.1
  124.1 7.7 %weight_grads.1 = (f32[96,4608]{1,0:T(8,128)}, f32[96,1536]{1,0:T(8,128)}, f32[96,6144]{1,0:T(8,128)}, f32[384,1536]{1,0:T(8,128)}, f32[384,2]{1,0:T(8,128)}, /*index=5*/f32[96,12]{1,0:T(8,128)}, f32[96,4]{1,0:T(8,128)}) custom-call(bf16[2,256,768]{2,1,0:T(8,128)(2,1)} %bitcast.25, bf16[2,256,768]{2,1,0:T(8,128)(2,1)} %bitcast.26, ...), custom_call_target="tpu_custom_call" | custom-call | tf_op jit(solution)/shard_map/weight_grads/pallas_call | solution.py:941
  131.8 0.0 copy-start
  131.9 1.6 %copy.21 = f32[96,4]{0,1:T(4,128)} copy(f32[96,4]{1,0:T(8,128)} %get-tuple-element.45) | data formatting | bytes 3072
  133.4 1.6 %copy.19 = f32[384,2]{0,1:T(2,128)} copy(f32[384,2]{1,0:T(8,128)} %get-tuple-element.43) | data formatting | bytes 6144
  135.0 1.5 %copy.20 = f32[96,12]{0,1:T(8,128)} copy(f32[96,12]{1,0:T(8,128)} %get-tuple-element.44) | data formatting | bytes 9216
  136.5 0.0 copy-done.1
  136.5 0.9 copy.24
  137.4 0.0 copy-done
  137.4 1.1 copy.25
  (3 shorter events, 0.0 us)
Async XLA Ops:
  124.1 12.4 %copy-start.1 = (bf16[512,768]{1,0:T(8,128)(2,1)S(1)}, bf16[512,768]{1,0:T(8,128)(2,1)}, u32[]{:S(2)}) copy-start(bf16[512,768]{1,0:T(8,128)(2,1)} %get-tuple-element.23) | copy-start | bytes 2359300
  131.8 5.5 %copy-start = (f32[512,768]{1,0:T(8,128)S(1)}, f32[512,768]{1,0:T(8,128)}, u32[]{:S(2)}) copy-start(f32[512,768]{1,0:T(8,128)} %get-tuple-element.24) | copy-start | bytes 4718596

commit v3 on v2

--- a/solution.py
+++ b/solution.py
@@ -316,11 +316,11 @@
 
 
 def main_kernel(
-    x_ref, seg_ref, pos_ref, sv_ref, w_mix, w_proj, w_up, w_down,
-    enc_ref, drow_ref, fq_ref, fu_ref, fa_ref, se_ref, sl_ref,
-    wa, wd, sv_all, q_s, k_s, v_s, a_s, mask_s, b_s, h_s, hl_s, g_s, sel_s,
-    cls_own, cls_all, cls_f, src_q, src_u, src_a, src_e, src_l,
-    ld, far_s, near_s, z_r, rel_s, x_s, x_r, y_s, y_r, c_s, c_r, sv_sem, sv_r, cls_sem, cls_r,
+    x_ref, seg_ref, pos_ref, bu_ref, br_ref, gr_ref, w_mix, w_proj, w_up, w_down,
+    enc_out, drow_out, fq_ref, fu_ref, fa_ref, se_ref, sg_ref, sl_ref,
+    enc_ref, drow_ref, wa, wd, sv_f, sv_ref, sv_all, q_s, k_s, v_s, a_s, mask_s, b_s, h_s, hl_s, g_s, sel_s,
+    cls_own, cls_all, cls_f, src_q, src_u, src_a, src_e, src_g, src_l,
+    ld, far_s, near_s, z_r, rel_s, x_s, x_r, y_s, y_r, c_s, c_r, sv_sem, sv_r, cz_s, cz_r, cp_s, cp_r, done,
     fl, fz_s, fz_r, ff_s, ff_r, fg_s, fg_r, fc_s, fc_r, s1_s, s1_r, s2_s, s2_r, s3_s, s3_r,
 ):
     sources = (w_mix, w_proj, w_up, w_down)
@@ -338,6 +338,7 @@
     def device(zz, xx, yy, cc):
         return (zz * 2 + xx, yy * 2 + cc)
 
+    plane = x * 4 + other
     to_near, to_far = device(zn, x, y, c), device(z_a, x, y, c)
     to_x, to_y, to_core = device(z, 1 - x, y, c), device(z, x, 1 - y, c), device(z, x, y, 1 - c)
 
@@ -445,6 +446,13 @@
     def sv_copy(i):
         there = lax.rem(place + i, 8)
         return remote(sv_ref.at[there // 4], sv_all.at[place], sv_sem.at[i], sv_r.at[i], (there, other))
+
+    sv_f[...] = jnp.zeros_like(sv_f)
+    for t in range(2):
+        sv_f[t, 0:1, :] = bu_ref[...].astype(F32)[t : t + 1]
+        sv_f[t, 1:7, 0:96] = br_ref[...].astype(F32)[6 * t : 6 * t + 6]
+        sv_f[t, 7:9, 0:96] = gr_ref[...].astype(F32)[2 * t : 2 * t + 2]
+    sv_ref[...] = sv_f[...].astype(BF)
 
     WINDOW = 2
     for k in range(WINDOW):
@@ -466,7 +474,6 @@
     own_head = (wide_row // SEGS) == (wide_col // HEAD_DIM)
     repeat = jnp.where(iota((48, ROW), 0) % SEGS == iota((48, ROW), 1), 1.0, 0.0).astype(BF)
     open_keys = (iota((48, row_len), 0) % SEGS) == segments
-    row16 = iota((ROW, D), 0)
     x_r_rows = dot_plain(spot, x_ref[...])
     x_low = x_r_rows.astype(BF)
 
@@ -599,18 +606,117 @@
         state["unit2"], state["inv2"] = unit, inverse
         e = (unit * state["g2"] + state["o2"]).astype(BF)
         cls_own[...] = e[:SEGS, :]
-        cls_all[me] = e[:SEGS, :]
+        cls_all[z, plane] = e[:SEGS, :]
+
+    def cls_z(r):
+        peer = device(lax.rem(z + r, 4), x, y, c)
+        return remote(cls_own, cls_all.at[z, plane], cz_s.at[r], cz_r.at[r], peer)
+
+    def cls_plane(r):
+        to = lax.rem(plane + r, 8)
+        ref = cls_all.at[:, plane]
+        return remote(ref, ref, cp_s.at[r], cp_r.at[r], (z * 2 + to // 4, lax.rem(to, 4)))
+
+    xf, yf = x + (1 - c) * (1 - 2 * x), y + c * (1 - 2 * y)
+    xg, yg = x + c * (1 - 2 * x), y + (1 - c) * (1 - 2 * y)
+    to_f, to_g = device(z, xf, yf, c), device(z, xg, yg, c)
+    wholes = ((src_q, fq_ref), (src_u, fu_ref), (src_a, fa_ref))
+    sliced = ((src_e, se_ref), (src_g, sg_ref), (src_l, sl_ref))
+
+    def slot(ref):
+        return ref.at[tower, c, x, y, zi]
+
+    def whole_z(i):
+        src, dst = wholes[i]
+        for r in (1, 2, 3):
+            go(remote(src, slot(dst), fz_s.at[i, r], fz_r.at[i, r], device(lax.rem(z + r, 4), x, y, c)))
+        copy = pltpu.make_async_copy(src, slot(dst), fl.at[i])
+        copy.start()
+        copy.wait()
+
+    def whole_f(i):
+        src, dst = wholes[i]
+        for r in (1, 2, 3):
+            arrived(slot(dst), fz_s.at[i, r], fz_r.at[i, r])
+        ref = dst.at[:, c, x, y]
+        go(remote(ref, ref, ff_s.at[i], ff_r.at[i], to_f))
+        go(remote(ref, ref, fg_s.at[i, 0], fg_r.at[i, 0], to_g))
+
+    def whole_g(i):
+        dst = wholes[i][1]
+        ref = dst.at[:, c, xf, yf]
+        arrived(ref, ff_s.at[i], ff_r.at[i])
+        go(remote(ref, ref, fg_s.at[i, 1], fg_r.at[i, 1], to_g))
+
+    def whole_c(i):
+        dst = wholes[i][1]
+        for j in (0, 1):
+            arrived(dst.at[:, c, xg, yg], fg_s.at[i, j], fg_r.at[i, j])
+        ref = dst.at[:, c]
+        go(remote(ref, ref, fc_s.at[i], fc_r.at[i], to_core))
+
+    def whole_end(i):
+        arrived(wholes[i][1].at[:, c], fc_s.at[i], fc_r.at[i])
+
+    def slice_1(i):
+        src, dst = sliced[i]
+        for r in range(1, 8):
+            there = lax.rem(place + r, 8)
+            go(remote(src.at[there], slot(dst), s1_s.at[i, r], s1_r.at[i, r], (there, other)))
+        copy = pltpu.make_async_copy(src.at[place], slot(dst), fl.at[3 + i])
+        copy.start()
+        copy.wait()
+
+    def slice_2(i):
+        dst = sliced[i][1]
+        for r in range(1, 8):
+            arrived(slot(dst), s1_s.at[i, r], s1_r.at[i, r])
+        ref = dst.at[:, c, :, y]
+        go(remote(ref, ref, s2_s.at[i], s2_r.at[i], to_y))
+
+    def slice_3(i):
+        dst = sliced[i][1]
+        arrived(dst.at[:, c, :, y], s2_s.at[i], s2_r.at[i])
+        ref = dst.at[:, c]
+        go(remote(ref, ref, s3_s.at[i], s3_r.at[i], to_core))
+
+    def slice_end(i):
+        arrived(sliced[i][1].at[:, c], s3_s.at[i], s3_r.at[i])
+
+    row16 = iota((ROW, D), 0)
+
+    def top(rows):
+        return jnp.where(row16[:, : rows.shape[1]] < SEGS, rows, 0.0)
+
+    def pack_early():
+        src_q[...] = top(state["q_r"].astype(F32)).astype(BF)
+        hl_f32, a_f32, x_f32 = (top(m.astype(F32)) for m in (state["hl_r"], state["a_r"], x_low))
+        three = hl_f32 + pltpu.roll(a_f32, 4, 0) + pltpu.roll(x_f32, 8, 0)
+        z_rows = dot_plain(state["p_low"], x_ref[...])
+        early = jnp.concatenate([three, z_rows], axis=0).astype(BF)
+        early = dot_plain(early, sel_s[...]).astype(BF)
+        for d in range(8):
+            src_e[d] = early[:, 128 * d : 128 * d + 128]
+
+    def pack_gelu():
+        for d in range(8):
+            packed = jnp.zeros((ROW, 128), F32)
+            for b in range(3):
+                first = 384 * d + 128 * b
+                g = top(state["g_r"][first // D][:, first % D : first % D + 128].astype(F32))
+                packed = packed + (pltpu.roll(g, 4 * b, 0) if b else g)
+            src_g[d] = packed.astype(BF)
 
     after = {
         0: [lambda: small_vectors(), lambda: mix(0, k_s, None, None)],
         1: [lambda: mix(1, v_s, "bv", None)],
         2: [lambda: mix(2, q_s, "bq", scaled), rows_attention, lambda: attend(0, 2)],
-        3: [rows_project, lambda: attend(2, 4)],
+        3: [rows_project, pack_early, lambda: slice_1(0), lambda: attend(2, 4)],
         4: [lambda: rows_up(0), lambda: attend(4, 6)],
         5: [lambda: rows_up(1), project, lambda: up(0)],
         6: [lambda: rows_up(2), lambda: up(1)],
-        7: [lambda: rows_up(3), lambda: up(2)],
-        8: [lambda: rows_down(0), lambda: up(3)],
+        7: [lambda: rows_up(3), pack_gelu, lambda: up(2)],
+        8: [lambda: rows_down(0), lambda: up(3), lambda: slice_2(0)],
         9: [lambda: rows_down(1), lambda: down(0)],
         10: [lambda: rows_down(2), rows_finish],
     }
@@ -628,116 +734,28 @@
             for unit in after[i - 3]:
                 unit()
 
-    def cls_copy(i):
-        return remote(cls_own, cls_all.at[me], cls_sem.at[i], cls_r.at[i], peer_at(i))
-
-    def cls_send(i, carry):
-        cls_copy(i).start()
-        return carry
-
-    lax.fori_loop(1, 32, cls_send, 0)
-
-    xf, yf = x + (1 - c) * (1 - 2 * x), y + c * (1 - 2 * y)
-    xg, yg = x + c * (1 - 2 * x), y + (1 - c) * (1 - 2 * y)
-    to_f, to_g = device(z, xf, yf, c), device(z, xg, yg, c)
-    wholes = ((src_q, fq_ref), (src_u, fu_ref), (src_a, fa_ref))
-    sliced = ((src_e, se_ref), (src_l, sl_ref))
-
-    def slot(ref):
-        return ref.at[tower, c, x, y, zi]
-
-    def whole_z(i):
-        src, dst = wholes[i]
-        for r in (1, 2, 3):
-            go(remote(src, slot(dst), fz_s.at[i, r], fz_r.at[i, r], device(lax.rem(z + r, 4), x, y, c)))
-        copy = pltpu.make_async_copy(src, slot(dst), fl.at[i])
-        copy.start()
-        copy.wait()
-
-    def whole_f(i):
-        src, dst = wholes[i]
-        for r in (1, 2, 3):
-            arrived(slot(dst), fz_s.at[i, r], fz_r.at[i, r])
-        ref = dst.at[:, c, x, y]
-        go(remote(ref, ref, ff_s.at[i], ff_r.at[i], to_f))
-        go(remote(ref, ref, fg_s.at[i, 0], fg_r.at[i, 0], to_g))
-
-    def whole_g(i):
-        dst = wholes[i][1]
-        ref = dst.at[:, c, xf, yf]
-        arrived(ref, ff_s.at[i], ff_r.at[i])
-        go(remote(ref, ref, fg_s.at[i, 1], fg_r.at[i, 1], to_g))
-
-    def whole_c(i):
-        dst = wholes[i][1]
-        for j in (0, 1):
-            arrived(dst.at[:, c, xg, yg], fg_s.at[i, j], fg_r.at[i, j])
-        ref = dst.at[:, c]
-        go(remote(ref, ref, fc_s.at[i], fc_r.at[i], to_core))
-
-    def whole_end(i):
-        arrived(wholes[i][1].at[:, c], fc_s.at[i], fc_r.at[i])
-
-    def slice_1(i):
-        src, dst = sliced[i]
-        for r in range(1, 8):
-            there = lax.rem(place + r, 8)
-            go(remote(src.at[there], slot(dst), s1_s.at[i, r], s1_r.at[i, r], (there, other)))
-        copy = pltpu.make_async_copy(src.at[place], slot(dst), fl.at[3 + i])
-        copy.start()
-        copy.wait()
-
-    def slice_2(i):
-        dst = sliced[i][1]
-        for r in range(1, 8):
-            arrived(slot(dst), s1_s.at[i, r], s1_r.at[i, r])
-        ref = dst.at[:, c, :, y]
-        go(remote(ref, ref, s2_s.at[i], s2_r.at[i], to_y))
-
-    def slice_3(i):
-        dst = sliced[i][1]
-        arrived(dst.at[:, c, :, y], s2_s.at[i], s2_r.at[i])
-        ref = dst.at[:, c]
-        go(remote(ref, ref, s3_s.at[i], s3_r.at[i], to_core))
-
-    def slice_end(i):
-        arrived(sliced[i][1].at[:, c], s3_s.at[i], s3_r.at[i])
-
-    first_rows = row16 < SEGS
-
-    def top(rows):
-        return jnp.where(row16[:, : rows.shape[1]] < SEGS, rows, 0.0)
-
-    q_f32 = top(state["q_r"].astype(F32))
-    src_q[...] = q_f32.astype(BF)
+    go(cls_z(1))
+    go(cls_z(2))
+    go(cls_z(3))
     whole_z(0)
-    hl_f32, a_f32, x_f32 = (top(m.astype(F32)) for m in (state["hl_r"], state["a_r"], x_low))
-    four = hl_f32
-    for r in (4, 8, 12):
-        four = four + pltpu.roll(hl_f32, r, 0)
-    pair = pltpu.roll(a_f32, 4, 0) + pltpu.roll(x_f32, 8, 0)
-    z_rows = dot_plain(state["p_low"], x_ref[...])
-    early = jnp.concatenate([four, pair, z_rows], axis=0).astype(BF)
-    early = dot_plain(early, sel_s[...]).astype(BF)
-    for d in range(8):
-        src_e[d, :80, :] = early[:, 128 * d : 128 * d + 128]
-        for b in range(3):
-            first = 384 * d + 128 * b
-            g = state["g_r"][first // D][:, first % D : first % D + 128]
-            src_e[d, 80 + 16 * b : 96 + 16 * b, :] = top(g.astype(F32)).astype(BF)
-    slice_1(0)
-
+    slice_1(1)
     down(1)
+    for r in (1, 2, 3):
+        cls_z(r).wait_recv()
+    for r in range(1, 8):
+        go(cls_plane(r))
     down(2)
     finish()
 
-    def cls_wait(i, carry):
-        cls_copy(i).wait_recv()
-        return carry
-
-    lax.fori_loop(1, 32, cls_wait, 0)
+    keep_enc = pltpu.make_async_copy(enc_ref, enc_out, done.at[0])
+    keep_enc.start()
+    whole_f(0)
+    slice_3(0)
+    slice_2(1)
+    for r in range(1, 8):
+        cls_plane(r).wait_recv()
     for i in range(32):
-        cls_f[SEGS * i : SEGS * i + SEGS, :] = cls_all[i].astype(F32)
+        cls_f[SEGS * i : SEGS * i + SEGS, :] = cls_all[i // 8, i % 8].astype(F32)
     all_q, all_p = cls_f[:64, :].astype(BF), cls_f[64:, :].astype(BF)
     pair_scale = 2.0 * D ** (-0.5)
     logits = dot_over_columns(all_p, all_q) * pair_scale
@@ -757,7 +775,6 @@
     vec_g2, vec_o2 = total(d_cls * state["unit2"]), total(d_cls)
     dz2 = norm_back(state["unit2"], state["inv2"], state["g2"], d_cls)
     df = dz2.astype(BF)
-    whole_f(0)
     dh = dz2
     du_rows = []
     for j in range(4):
@@ -771,16 +788,13 @@
         packed = packed + pltpu.roll(du_rows[j], 4 * j, 0)
     src_u[...] = packed.astype(BF)
     whole_z(1)
-    slice_2(0)
     whole_g(0)
     for j in range(4):
         dh = dh + dot_over_columns(du_rows[j].astype(BF), wa[4 + j])
     vec_g1, vec_o1 = total(dh * state["unit1"]), total(dh)
     dz1 = norm_back(state["unit1"], state["inv1"], state["g1"], dh)
     db = dz1.astype(BF)
-    whole_f(1)
-    slice_3(0)
-    whole_c(0)
+    slice_3(1)
     da = dot_over_columns(db, wa[3]).astype(BF)
     a_wide = widen(da).astype(BF)
     d_p_rows = dot_over_columns(a_wide, v_s[...])
@@ -790,7 +804,6 @@
     df_f, db_f, da_f, dq_f = (m.astype(F32) for m in (df, db, da, dq))
     src_a[...] = (df_f + pltpu.roll(db_f, 4, 0) + pltpu.roll(dq_f, 8, 0) + pltpu.roll(da_f, 12, 0)).astype(BF)
     whole_z(2)
-    whole_g(1)
     y_rows = dot_plain(ds, x_ref[...]) * scaled
     weight_sum = jnp.sum(state["p_low"].astype(F32), axis=1, keepdims=True)
     vec_bv = total(weight_sum * a_wide.astype(F32))
@@ -801,10 +814,10 @@
     late = dot_plain(late, sel_s[...]).astype(BF)
     for d in range(8):
         src_l[d] = late[:, 128 * d : 128 * d + 128]
-    slice_1(1)
-    whole_f(2)
-    whole_c(1)
-
+
+    slice_1(2)
+    whole_f(1)
+    whole_c(0)
     t_k = dot_over_columns(state["q_wide"], wa[0]).astype(BF)
     t_v = dot_over_columns(a_wide, wa[1]).astype(BF)
     at_rows = dz1 + dot_over_columns(dq, wa[2])
@@ -812,16 +825,22 @@
     rest = (at_rows - high.astype(F32)).astype(BF)
     left = jnp.concatenate([ds, state["p_low"], spot, spot], axis=0)
     right = jnp.concatenate([t_k, t_v, high, rest], axis=0)
-    whole_g(2)
-    slice_2(1)
+    whole_f(2)
+    whole_g(1)
     for n in range(0, D, BLOCK):
         drow_ref[:, n : n + BLOCK] = dot_over_rows(left, right[:, n : n + BLOCK])
+    keep_row = pltpu.make_async_copy(drow_ref, drow_out, done.at[1])
+    keep_row.start()
+    slice_2(2)
+    whole_g(2)
+    whole_c(1)
+    slice_3(2)
     whole_c(2)
-    slice_3(1)
     for i in range(3):
         whole_end(i)
-    for i in range(2):
         slice_end(i)
+    keep_enc.wait()
+    keep_row.wait()
 
     for copy in sent:
         copy.wait_send()
@@ -836,14 +855,22 @@
     for i in range(1, 8):
         sv_copy(i).wait_send()
 
-    def cls_sent(i, carry):
-        cls_copy(i).wait_send()
-        return carry
-
-    lax.fori_loop(1, 32, cls_sent, 0)
-
-
-def grads_kernel(fq_ref, fu_ref, fa_ref, se_ref, sl_ref, mix_ref, proj_ref, up_ref, down_ref, upb_ref, rowb_ref, gain_ref):
+
+def grads_kernel(
+    fq_hbm, fu_hbm, fa_hbm, se_hbm, sg_hbm, sl_hbm, enc_hbm, drow_hbm,
+    enc_out, drow_out, mix_out, proj_out, up_out, down_out, upb_ref, rowb_ref, gain_ref,
+    fq_ref, fu_ref, fa_ref, se_ref, sg_ref, sl_ref, mix_ref, proj_ref, up_ref, down_ref, enc_ref, drow_ref, got, put,
+):
+    def fetch(i, src, dst):
+        copy = pltpu.make_async_copy(src, dst, got.at[i])
+        copy.start()
+        return copy
+
+    order = (
+        (fu_hbm, fu_ref), (se_hbm, se_ref), (fa_hbm, fa_ref), (sg_hbm, sg_ref), (fq_hbm, fq_ref), (sl_hbm, sl_ref),
+        (enc_hbm, enc_ref), (drow_hbm, drow_ref),
+    )
+    in_u, in_e, in_a, in_g, in_q, in_l, keep_e, keep_d = (fetch(i, *pair) for i, pair in enumerate(order))
     place = lax.axis_index("dp")
     kind = iota((256, 128), 0) % ROW
     part = 96
@@ -854,105 +881,145 @@
     take_q = jnp.where(iota((192, 64), 1) == group * ROW + within, 1.0, 0.0).astype(BF)
     take_a = jnp.where(iota((192, 64), 1) == group * ROW + within + 12, 1.0, 0.0).astype(BF)
     kind16, col16 = iota((256, ROW), 0) % ROW, iota((256, ROW), 1)
-    biases = jnp.zeros((128, ROW), F32)
-    gains = jnp.zeros((128, ROW), F32)
-    up_bias = jnp.zeros((384, ROW), F32)
+    again_row, again_col = iota((256, 256), 0), iota((256, 256), 1)
+    again = jnp.where(again_col == again_row // ROW * ROW + again_row % SEGS, 1.0, 0.0).astype(BF)
+    stores = []
+
+    def store(src, dst):
+        copy = pltpu.make_async_copy(src, dst, put.at[len(stores)])
+        copy.start()
+        stores.append(copy)
+
+    def keep(rows, lo, hi):
+        return jnp.where((kind >= lo) & (kind < hi), rows, jnp.zeros((), BF))
+
+    in_u.wait()
+    in_e.wait()
+    three = [se_ref[t, :, 0:16, :].reshape(256, 128) for t in range(2)]
     for t in range(2):
-        def keep(ref_rows, lo, hi):
-            return jnp.where((kind >= lo) & (kind < hi), ref_rows, jnp.zeros((), BF))
-
-        four = se_ref[t, :, 0:16, :].reshape(256, 128)
-        two = se_ref[t, :, 16:32, :].reshape(256, 128)
-        fa, fu = fa_ref[t], fu_ref[t]
-        mix_ref[:, 3 * D * t : 3 * D * t + D] = dot_over_rows(keep(two, 8, 12), fa)[:part]
-        proj_ref[:, D * t : D * t + D] = dot_over_rows(keep(two, 4, 8), fa)[:part]
+        four = dot_plain(again, three[t]).astype(BF)
         for j in range(4):
-            first = FF * t + D * j
-            up_ref[:, first : first + D] = dot_over_rows(keep(four, 4 * j, 4 * j + 4), fu)[:part]
+            cols = slice(FF * t + D * j, FF * t + D * j + D)
+            up_ref[:, cols] = dot_over_rows(keep(four, 4 * j, 4 * j + 4), fu_ref[t])[:part]
+            store(up_ref.at[:, cols], up_out.at[:, cols])
+    up_bias = jnp.zeros((ROW, 384), F32)
+    for t in range(2):
+        mine = fu_ref[t, :, pl.ds(pl.multiple_of(place % 2 * 384, 128), 384)]
+        to_up = jnp.where((kind16 // 4 == place // 2) & (col16 == t), 1.0, 0.0).astype(BF)
+        up_bias = up_bias + dot_over_rows(to_up, mine)
+    upb_ref[...] = up_bias[:2]
+    keep_e.wait()
+    store(enc_ref, enc_out)
+    keep_d.wait()
+    store(drow_ref, drow_out)
+    in_a.wait()
+    in_g.wait()
+    for t in range(2):
+        fa = fa_ref[t]
+        cols = slice(D * t, D * t + D)
+        proj_ref[:, cols] = dot_over_rows(keep(three[t], 4, 8), fa)[:part]
+        store(proj_ref.at[:, cols], proj_out.at[:, cols])
+        first = slice(3 * D * t, 3 * D * t + D)
+        mix_ref[:, first] = dot_over_rows(keep(three[t], 8, 12), fa)[:part]
+        store(mix_ref.at[:, first], mix_out.at[:, first])
+        df = dot_plain(again, fa).astype(BF)
+        g = sg_ref[t].reshape(256, 128)
         for b in range(3):
-            g = se_ref[t, :, 80 + 16 * b : 96 + 16 * b, :].reshape(256, 128)
-            down_ref[128 * b : 128 * b + 128, D * t : D * t + D] = dot_over_rows(g, fa)
-        gk = jnp.zeros((128, D), F32)
+            at = slice(128 * b, 128 * b + 128)
+            down_ref[at, cols] = dot_over_rows(keep(g, 4 * b, 4 * b + 4), df)
+        store(down_ref.at[:, cols], down_out.at[:, cols])
+    for t in range(2):
         gv = jnp.zeros((128, D), F32)
         for s in range(4):
+            a_wide = jnp.where(own_head, dot_plain(take_a, fa_ref[t, 64 * s : 64 * s + 64, :]), 0.0).astype(BF)
+            gv = gv + dot_over_rows(se_ref[t, 4 * s : 4 * s + 4, 16:64, :].reshape(192, 128), a_wide)
+        cols = slice(3 * D * t + 2 * D, 3 * D * t + 3 * D)
+        mix_ref[:, cols] = gv[:part]
+        store(mix_ref.at[:, cols], mix_out.at[:, cols])
+    in_q.wait()
+    in_l.wait()
+    biases = jnp.zeros((ROW, 128), F32)
+    gains = jnp.zeros((ROW, 128), F32)
+    for t in range(2):
+        gk = jnp.zeros((128, D), F32)
+        for s in range(4):
             q_wide = jnp.where(own_head, dot_plain(take_q, fq_ref[t, 64 * s : 64 * s + 64, :]), 0.0).astype(BF)
-            a_wide = jnp.where(own_head, dot_plain(take_a, fa[64 * s : 64 * s + 64, :]), 0.0).astype(BF)
-            y = sl_ref[t, 4 * s : 4 * s + 4, 0:48, :].reshape(192, 128)
-            z = se_ref[t, 4 * s : 4 * s + 4, 32:80, :].reshape(192, 128)
-            gk = gk + dot_over_rows(y, q_wide)
-            gv = gv + dot_over_rows(z, a_wide)
-        mix_ref[:, 3 * D * t + D : 3 * D * t + 2 * D] = gk[:part]
-        mix_ref[:, 3 * D * t + 2 * D : 3 * D * t + 3 * D] = gv[:part]
+            gk = gk + dot_over_rows(sl_ref[t, 4 * s : 4 * s + 4, 0:48, :].reshape(192, 128), q_wide)
+        cols = slice(3 * D * t + D, 3 * D * t + 2 * D)
+        mix_ref[:, cols] = gk[:part]
+        store(mix_ref.at[:, cols], mix_out.at[:, cols])
         vec = sl_ref[t, :, 48:64, :].reshape(256, 128)
         to_bias = jnp.where((kind16 < 6) & (col16 == kind16 + 6 * t), 1.0, 0.0).astype(BF)
         to_gain = jnp.where((kind16 >= 6) & (kind16 < 8) & (col16 == kind16 - 6 + 2 * t), 1.0, 0.0).astype(BF)
-        biases = biases + dot_over_rows(vec, to_bias)
-        gains = gains + dot_over_rows(vec, to_gain)
-        mine = fu_ref[t, :, pl.ds(pl.multiple_of(place % 2 * 384, 128), 384)]
-        to_up = jnp.where((kind16 // 4 == place // 2) & (col16 == t), 1.0, 0.0).astype(BF)
-        up_bias = up_bias + dot_over_rows(mine, to_up)
-    rowb_ref[...] = biases[:part, :12]
-    gain_ref[...] = gains[:part, :4]
-    upb_ref[...] = up_bias[:, :2]
+        biases = biases + dot_over_rows(to_bias, vec)
+        gains = gains + dot_over_rows(to_gain, vec)
+    rowb_ref[...] = biases[:12, :part]
+    gain_ref[...] = gains[:4, :part]
+    for copy in stores:
+        copy.wait()
 
 
 def fast_device(text_rows, text_segments, positives, w_mix, w_proj, w_up, w_down, b_up, b_rows, g_rows):
     sem = pltpu.SemaphoreType.DMA
     vm = pltpu.VMEM
     part = b_rows.shape[0]
-    towers = []
-    for t in range(2):
-        narrow = jnp.concatenate([b_rows[:, 6 * t : 6 * t + 6], g_rows[:, 2 * t : 2 * t + 2]], axis=1).T
-        narrow = jnp.pad(narrow, ((0, 7), (0, 4 * part - part)))
-        towers.append(jnp.concatenate([b_up[:, t][None, :], narrow], axis=0))
-    small = jnp.stack(towers)
     kinds = len(PIECES)
     fulls = jax.ShapeDtypeStruct((2, 2, 2, 2, 2, ROW, D), BF)
     row_len = text_rows.shape[1]
     here, there = pl.BlockSpec(memory_space=vm), pl.BlockSpec(memory_space=pl.ANY)
-    encoded, d_rows, fq, fu, fa, se, sl = pl.pallas_call(
+    slices = lambda r: jax.ShapeDtypeStruct((2, 2, 2, 2, 2, r, 128), BF)
+    encoded, d_rows, fq, fu, fa, se, sg, sl = pl.pallas_call(
         main_kernel,
         out_shape=[
             jax.ShapeDtypeStruct((row_len, D), BF),
             jax.ShapeDtypeStruct((row_len, D), F32),
-            fulls, fulls, fulls,
-            jax.ShapeDtypeStruct((2, 2, 2, 2, 2, 128, 128), BF),
-            jax.ShapeDtypeStruct((2, 2, 2, 2, 2, 64, 128), BF),
+            fulls, fulls, fulls, slices(64), slices(ROW), slices(64),
         ],
-        in_specs=[here] * 4 + [there] * 4,
-        out_specs=[here] * 2 + [there] * 5,
+        in_specs=[here] * 6 + [there] * 4,
+        out_specs=[there] * 2 + [here] * 6,
         scratch_shapes=[
-            vm((8, D, D), BF), vm((3, FF, 256), BF), vm((8, ROW, 384), BF),
+            vm((row_len, D), BF), vm((row_len, D), F32),
+            vm((8, D, D), BF), vm((3, FF, 256), BF),
+            vm((2, ROW, 384), F32), vm((2, ROW, 384), BF), vm((8, ROW, 384), BF),
             vm((row_len, D), BF), vm((row_len, D), BF), vm((row_len, D), BF), vm((row_len, D), BF),
             vm((row_len, row_len), F32), vm((row_len, D), F32), vm((row_len, D), F32), vm((row_len, D), BF),
             vm((4, row_len, D), BF), vm((D, 1024), BF),
-            vm((SEGS, D), BF), vm((32, SEGS, D), BF), vm((128, D), F32),
-            vm((ROW, D), BF), vm((ROW, D), BF), vm((ROW, D), BF), vm((8, 128, 128), BF), vm((8, 64, 128), BF),
+            vm((SEGS, D), BF), vm((4, 8, SEGS, D), BF), vm((128, D), F32),
+            vm((ROW, D), BF), vm((ROW, D), BF), vm((ROW, D), BF),
+            vm((8, 64, 128), BF), vm((8, ROW, 128), BF), vm((8, 64, 128), BF),
             sem((kinds,)), sem((kinds,)), sem((kinds,)), sem((kinds, 3)), sem((kinds, 2)),
             sem((kinds, 4)), sem((kinds, 4)), sem((kinds, 4)), sem((kinds, 4)), sem((kinds,)), sem((kinds,)),
-            sem((8,)), sem((8,)), sem((32,)), sem((32,)),
-            sem((5,)), sem((3, 4)), sem((3, 4)), sem((3,)), sem((3,)), sem((3, 2)), sem((3, 2)), sem((3,)), sem((3,)),
-            sem((2, 8)), sem((2, 8)), sem((2,)), sem((2,)), sem((2,)), sem((2,)),
+            sem((8,)), sem((8,)), sem((4,)), sem((4,)), sem((8,)), sem((8,)), sem((2,)),
+            sem((6,)), sem((3, 4)), sem((3, 4)), sem((3,)), sem((3,)), sem((3, 2)), sem((3, 2)), sem((3,)), sem((3,)),
+            sem((3, 8)), sem((3, 8)), sem((3,)), sem((3,)), sem((3,)), sem((3,)),
         ],
         compiler_params=pltpu.CompilerParams(collective_id=5, has_side_effects=True, vmem_limit_bytes=60 << 20),
         name="main_step",
-    )(text_rows[0], text_segments, positives[None, :], small, w_mix, w_proj, w_up, w_down)
+    )(text_rows[0], text_segments, positives[None, :], b_up.T, b_rows.T, g_rows.T, w_mix, w_proj, w_up, w_down)
     shape = lambda r, n: jax.ShapeDtypeStruct((r, n), F32)
     grads = pl.pallas_call(
         grads_kernel,
         out_shape=[
+            jax.ShapeDtypeStruct((row_len, D), BF), shape(row_len, D),
             shape(part, 6 * D), shape(part, 2 * D), shape(part, 2 * FF), shape(4 * part, 2 * D),
-            shape(4 * part, 2), shape(part, 12), shape(part, 4),
+            shape(2, 4 * part), shape(12, part), shape(4, part),
         ],
-        in_specs=[here] * 5,
-        out_specs=[here] * 7,
+        in_specs=[there] * 8,
+        out_specs=[there] * 6 + [here] * 3,
+        scratch_shapes=[
+            vm((2, 256, D), BF), vm((2, 256, D), BF), vm((2, 256, D), BF),
+            vm((2, 16, 64, 128), BF), vm((2, 16, ROW, 128), BF), vm((2, 16, 64, 128), BF),
+            vm((part, 6 * D), F32), vm((part, 2 * D), F32), vm((part, 2 * FF), F32), vm((4 * part, 2 * D), F32),
+            vm((row_len, D), BF), vm((row_len, D), F32), sem((8,)), sem((20,)),
+        ],
         compiler_params=pltpu.CompilerParams(vmem_limit_bytes=60 << 20),
         name="weight_grads",
     )(
         fq.reshape(2, 256, D), fu.reshape(2, 256, D), fa.reshape(2, 256, D),
-        se.reshape(2, 16, 128, 128), sl.reshape(2, 16, 64, 128),
+        se.reshape(2, 16, 64, 128), sg.reshape(2, 16, ROW, 128), sl.reshape(2, 16, 64, 128), encoded, d_rows,
     )
-    return (encoded[None], d_rows[None], *grads)
+    encoded, d_rows, mix, proj, up, down, up_b, row_b, gain = grads
+    return encoded[None], d_rows[None], mix, proj, up, down, up_b.T, row_b.T, gain.T
 
 
 def solution(mesh):

time: 139 us -> 120 us (0.86)
  Pallas kernels: 128 us -> 119 us
  local copies, waits for them, and re-layouts: 8.97 us -> 0 us
    pallas_call x1, Pallas kernels: 121 us -> 110 us  [fast_device(): pl.pallas_call(main_kernel, out_shape=[jax.ShapeDtypeStruct((row_len, D),...]
    unnamed x9 -> x0, local copies, waits for them, and re-layouts: 6.68 us -> none
    slice x2 -> x0, local copies, waits for them, and re-layouts: 1.53 us -> none  [the longest x1 0.77 us: fast_device(): b_rows[:, 6 * t:6 * t + 6]]
where the time goes in v3:
time: 120 us
  Pallas kernels  119 us (99%)
    pallas_call x1, Pallas kernels, fast_device(): pl.pallas_call(main_kernel, out_shape=[jax.ShapeDtypeStruct((row_len, D),...  110 us
    pallas_call x1, Pallas kernels, fast_device(): pl.pallas_call(grads_kernel, out_shape=[jax.ShapeDtypeStruct((row_len, D)...  9.03 us

profile of v3, /device:TPU:1, one launch (start us, length us, event | category | flops | bytes accessed | tf_op | source)
XLA Modules:
  0.0 119.8 jit_solution(3252942489630961230)
XLA Ops:
  0.6 109.9 %main_step.1 = (bf16[512,768]{1,0:T(8,128)(2,1)}, f32[512,768]{1,0:T(8,128)}, bf16[2,2,2,2,2,16,768]{6,5,4,3,2,1,0:T(8,128)(2,1)}, bf16[2,2,2,2,2,16,768]{6,5,4,...) custom-call(bf16[512,768]{1,0:T(8,128)(2,1)} %bitcast.16, ...), custom_call_target="tpu_custom_call" | custom-call | tf_op jit(solution)/shard_map/main_step/pallas_call | solution.py:971
  110.6 9.0 %weight_grads.1 = (bf16[512,768]{1,0:T(8,128)(2,1)}, f32[512,768]{1,0:T(8,128)}, f32[96,4608]{1,0:T(8,128)}, f32[96,1536]{1,0:T(8,128)}, f32[96,6144]{1,0:T(8,12...) custom-call(bf16[2,256,768]{2,1,0:T(8,128)(2,1)} %bitcast.17, ...), custom_call_target="tpu_custom_call" | custom-call | tf_op jit(solution)/shard_map/weight_grads/pallas_call | solution.py:1000

commit v4 on v3

--- a/solution.py
+++ b/solution.py
@@ -316,9 +316,9 @@
 
 
 def main_kernel(
-    x_ref, seg_ref, pos_ref, bu_ref, br_ref, gr_ref, w_mix, w_proj, w_up, w_down,
+    x_in, seg_in, pos_in, bu_in, br_in, gr_in, w_mix, w_proj, w_up, w_down,
     enc_out, drow_out, fq_ref, fu_ref, fa_ref, se_ref, sg_ref, sl_ref,
-    enc_ref, drow_ref, wa, wd, sv_f, sv_ref, sv_all, q_s, k_s, v_s, a_s, mask_s, b_s, h_s, hl_s, g_s, sel_s,
+    x_ref, seg_ref, pos_ref, bu_ref, br_ref, gr_ref, first, enc_ref, drow_ref, wa, wd, sv_f, sv_ref, sv_all, q_s, k_s, v_s, a_s, mask_s, b_s, h_s, hl_s, g_s, sel_s,
     cls_own, cls_all, cls_f, src_q, src_u, src_a, src_e, src_g, src_l,
     ld, far_s, near_s, z_r, rel_s, x_s, x_r, y_s, y_r, c_s, c_r, sv_sem, sv_r, cz_s, cz_r, cp_s, cp_r, done,
     fl, fz_s, fz_r, ff_s, ff_r, fg_s, fg_r, fc_s, fc_r, s1_s, s1_r, s2_s, s2_r, s3_s, s3_r,
@@ -342,6 +342,11 @@
     to_near, to_far = device(zn, x, y, c), device(z_a, x, y, c)
     to_x, to_y, to_core = device(z, 1 - x, y, c), device(z, x, 1 - y, c), device(z, x, y, 1 - c)
 
+    loads = []
+    pairs = ((bu_in, bu_ref), (br_in, br_ref), (gr_in, gr_ref), (seg_in, seg_ref), (pos_in, pos_ref), (x_in, x_ref))
+    for i, (src, dst) in enumerate(pairs):
+        loads.append(pltpu.make_async_copy(src, dst, first.at[i]))
+        loads[-1].start()
     barrier = pltpu.get_barrier_semaphore()
 
     def peer_at(i):
@@ -447,6 +452,11 @@
         there = lax.rem(place + i, 8)
         return remote(sv_ref.at[there // 4], sv_all.at[place], sv_sem.at[i], sv_r.at[i], (there, other))
 
+    WINDOW = 2
+    for k in range(WINDOW):
+        stage0(k)
+    for copy in loads:
+        copy.wait()
     sv_f[...] = jnp.zeros_like(sv_f)
     for t in range(2):
         sv_f[t, 0:1, :] = bu_ref[...].astype(F32)[t : t + 1]
@@ -454,9 +464,6 @@
         sv_f[t, 7:9, 0:96] = gr_ref[...].astype(F32)[2 * t : 2 * t + 2]
     sv_ref[...] = sv_f[...].astype(BF)
 
-    WINDOW = 2
-    for k in range(WINDOW):
-        stage0(k)
     for i in range(1, 8):
         sv_copy(i).start()
     sv_all[place] = sv_ref[tower]
@@ -510,25 +517,16 @@
             out[:, n : n + BLOCK] = m
 
     def attend(low, high):
-        rows = 256
-        per = row_len // rows
-
-        def body(i, carry):
-            pair, part = i // per, lax.rem(i, per)
-            cols = pl.ds(pl.multiple_of(pair * 128, 128), 128)
-            at = pl.ds(pl.multiple_of(part * rows, rows), rows)
-            qp, kp, vp = q_s[at, cols], k_s[:, cols], v_s[:, cols]
-            left = iota((rows, 128), 1) < HEAD_DIM
+        left = iota((row_len, 128), 1) < HEAD_DIM
+        for pair in range(low, high):
+            cols = slice(128 * pair, 128 * pair + 128)
+            qp, kp, vp = q_s[:, cols], k_s[:, cols], v_s[:, cols]
             found = []
             for keep in (left, jnp.logical_not(left)):
-                s = dot_over_columns(jnp.where(keep, qp, jnp.zeros((), BF)), kp) + mask_s[at, :]
+                s = dot_over_columns(jnp.where(keep, qp, jnp.zeros((), BF)), kp) + mask_s[...]
                 e = jnp.exp(s - jnp.max(s, axis=1, keepdims=True))
-                p = (e * (1.0 / jnp.sum(e, axis=1, keepdims=True))).astype(BF)
-                found.append(dot_plain(p, vp))
-            a_s[at, cols] = jnp.where(left, found[0], found[1]).astype(BF)
-            return carry
-
-        lax.fori_loop(low * per, high * per, body, 0)
+                found.append(dot_plain(e.astype(BF), vp) * (1.0 / jnp.sum(e, axis=1, keepdims=True)))
+            a_s[:, cols] = jnp.where(left, found[0], found[1]).astype(BF)
 
     def project():
         for n in range(0, D, BLOCK):
@@ -538,15 +536,10 @@
                 + state["bo"][:, n : n + BLOCK]
             )
 
-        def body(i, carry):
-            at = pl.ds(pl.multiple_of(i * 128, 128), 128)
-            unit, _ = norm_parts(b_s[at, :])
-            h = unit * state["g1"] + state["o1"]
-            h_s[at, :] = h
-            hl_s[at, :] = h.astype(BF)
-            return carry
-
-        lax.fori_loop(0, row_len // 128, body, 0)
+        unit, _ = norm_parts(b_s[...])
+        h = unit * state["g1"] + state["o1"]
+        h_s[...] = h
+        hl_s[...] = h.astype(BF)
 
     def up(j):
         for n in range(0, D, BLOCK):
@@ -561,13 +554,8 @@
         b_s[:, cols] = total
 
     def finish():
-        def body(i, carry):
-            at = pl.ds(pl.multiple_of(i * 128, 128), 128)
-            unit, _ = norm_parts(b_s[at, :])
-            enc_ref[at, :] = (unit * state["g2"] + state["o2"]).astype(BF)
-            return carry
-
-        lax.fori_loop(0, row_len // 128, body, 0)
+        unit, _ = norm_parts(b_s[...])
+        enc_ref[...] = (unit * state["g2"] + state["o2"]).astype(BF)
 
     def rows_attention():
         q_r = (dot_plain(x_low, wa[2]) + state["bq"]).astype(BF)
@@ -857,29 +845,18 @@
 
 
 def grads_kernel(
-    fq_hbm, fu_hbm, fa_hbm, se_hbm, sg_hbm, sl_hbm, enc_hbm, drow_hbm,
+    fq_ref, fu_ref, fa_ref, se_ref, sg_ref, sl_ref, enc_ref, drow_ref,
     enc_out, drow_out, mix_out, proj_out, up_out, down_out, upb_ref, rowb_ref, gain_ref,
-    fq_ref, fu_ref, fa_ref, se_ref, sg_ref, sl_ref, mix_ref, proj_ref, up_ref, down_ref, enc_ref, drow_ref, got, put,
+    mix_ref, proj_ref, up_ref, down_ref, put,
 ):
-    def fetch(i, src, dst):
-        copy = pltpu.make_async_copy(src, dst, got.at[i])
-        copy.start()
-        return copy
-
-    order = (
-        (fu_hbm, fu_ref), (se_hbm, se_ref), (fa_hbm, fa_ref), (sg_hbm, sg_ref), (fq_hbm, fq_ref), (sl_hbm, sl_ref),
-        (enc_hbm, enc_ref), (drow_hbm, drow_ref),
-    )
-    in_u, in_e, in_a, in_g, in_q, in_l, keep_e, keep_d = (fetch(i, *pair) for i, pair in enumerate(order))
     place = lax.axis_index("dp")
     kind = iota((256, 128), 0) % ROW
     part = 96
-    pick = iota((192, 64), 0)
-    group, within = pick // 48, pick % SEGS
-    head_row, head_col = iota((192, D), 0), iota((192, D), 1)
-    own_head = (head_row % 48) // SEGS == head_col // HEAD_DIM
-    take_q = jnp.where(iota((192, 64), 1) == group * ROW + within, 1.0, 0.0).astype(BF)
-    take_a = jnp.where(iota((192, 64), 1) == group * ROW + within + 12, 1.0, 0.0).astype(BF)
+    wide_row, wide_col = iota((D, 256), 0), iota((D, 256), 1)
+    first_of = wide_row // 48 * ROW + wide_row % SEGS
+    take_q = jnp.where(wide_col == first_of, 1.0, 0.0).astype(BF)
+    take_a = jnp.where(wide_col == first_of + 12, 1.0, 0.0).astype(BF)
+    own_head = (iota((D, D), 0) % 48) // SEGS == iota((D, D), 1) // HEAD_DIM
     kind16, col16 = iota((256, ROW), 0) % ROW, iota((256, ROW), 1)
     again_row, again_col = iota((256, 256), 0), iota((256, 256), 1)
     again = jnp.where(again_col == again_row // ROW * ROW + again_row % SEGS, 1.0, 0.0).astype(BF)
@@ -890,11 +867,12 @@
         copy.start()
         stores.append(copy)
 
+    store(enc_ref, enc_out)
+    store(drow_ref, drow_out)
+
     def keep(rows, lo, hi):
         return jnp.where((kind >= lo) & (kind < hi), rows, jnp.zeros((), BF))
 
-    in_u.wait()
-    in_e.wait()
     three = [se_ref[t, :, 0:16, :].reshape(256, 128) for t in range(2)]
     for t in range(2):
         four = dot_plain(again, three[t]).astype(BF)
@@ -908,12 +886,6 @@
         to_up = jnp.where((kind16 // 4 == place // 2) & (col16 == t), 1.0, 0.0).astype(BF)
         up_bias = up_bias + dot_over_rows(to_up, mine)
     upb_ref[...] = up_bias[:2]
-    keep_e.wait()
-    store(enc_ref, enc_out)
-    keep_d.wait()
-    store(drow_ref, drow_out)
-    in_a.wait()
-    in_g.wait()
     for t in range(2):
         fa = fa_ref[t]
         cols = slice(D * t, D * t + D)
@@ -929,22 +901,16 @@
             down_ref[at, cols] = dot_over_rows(keep(g, 4 * b, 4 * b + 4), df)
         store(down_ref.at[:, cols], down_out.at[:, cols])
     for t in range(2):
-        gv = jnp.zeros((128, D), F32)
-        for s in range(4):
-            a_wide = jnp.where(own_head, dot_plain(take_a, fa_ref[t, 64 * s : 64 * s + 64, :]), 0.0).astype(BF)
-            gv = gv + dot_over_rows(se_ref[t, 4 * s : 4 * s + 4, 16:64, :].reshape(192, 128), a_wide)
+        a_wide = jnp.where(own_head, dot_plain(take_a, fa_ref[t]), 0.0).astype(BF)
+        gv = dot_over_rows(se_ref[t, :, 16:64, :].reshape(D, 128), a_wide)
         cols = slice(3 * D * t + 2 * D, 3 * D * t + 3 * D)
         mix_ref[:, cols] = gv[:part]
         store(mix_ref.at[:, cols], mix_out.at[:, cols])
-    in_q.wait()
-    in_l.wait()
     biases = jnp.zeros((ROW, 128), F32)
     gains = jnp.zeros((ROW, 128), F32)
     for t in range(2):
-        gk = jnp.zeros((128, D), F32)
-        for s in range(4):
-            q_wide = jnp.where(own_head, dot_plain(take_q, fq_ref[t, 64 * s : 64 * s + 64, :]), 0.0).astype(BF)
-            gk = gk + dot_over_rows(sl_ref[t, 4 * s : 4 * s + 4, 0:48, :].reshape(192, 128), q_wide)
+        q_wide = jnp.where(own_head, dot_plain(take_q, fq_ref[t]), 0.0).astype(BF)
+        gk = dot_over_rows(sl_ref[t, :, 0:48, :].reshape(D, 128), q_wide)
         cols = slice(3 * D * t + D, 3 * D * t + 2 * D)
         mix_ref[:, cols] = gk[:part]
         store(mix_ref.at[:, cols], mix_out.at[:, cols])
@@ -975,9 +941,11 @@
             jax.ShapeDtypeStruct((row_len, D), F32),
             fulls, fulls, fulls, slices(64), slices(ROW), slices(64),
         ],
-        in_specs=[here] * 6 + [there] * 4,
+        in_specs=[pl.BlockSpec(memory_space=pltpu.HBM)] * 10,
         out_specs=[there] * 2 + [here] * 6,
         scratch_shapes=[
+            vm((row_len, D), BF), vm((1, row_len), jnp.int32), vm((1, 64), jnp.int32),
+            vm((2, 384), BF), vm((12, 96), BF), vm((4, 96), BF), sem((6,)),
             vm((row_len, D), BF), vm((row_len, D), F32),
             vm((8, D, D), BF), vm((3, FF, 256), BF),
             vm((2, ROW, 384), F32), vm((2, ROW, 384), BF), vm((8, ROW, 384), BF),
@@ -993,9 +961,9 @@
             sem((6,)), sem((3, 4)), sem((3, 4)), sem((3,)), sem((3,)), sem((3, 2)), sem((3, 2)), sem((3,)), sem((3,)),
             sem((3, 8)), sem((3, 8)), sem((3,)), sem((3,)), sem((3,)), sem((3,)),
         ],
-        compiler_params=pltpu.CompilerParams(collective_id=5, has_side_effects=True, vmem_limit_bytes=60 << 20),
+        compiler_params=pltpu.CompilerParams(collective_id=5, has_side_effects=True, vmem_limit_bytes=44 << 20),
         name="main_step",
-    )(text_rows[0], text_segments, positives[None, :], b_up.T, b_rows.T, g_rows.T, w_mix, w_proj, w_up, w_down)
+    )(*(pltpu.with_memory_space_constraint(m, pltpu.HBM) for m in (text_rows[0], text_segments, positives[None, :], b_up.T, b_rows.T, g_rows.T, w_mix, w_proj, w_up, w_down)))
     shape = lambda r, n: jax.ShapeDtypeStruct((r, n), F32)
     grads = pl.pallas_call(
         grads_kernel,
@@ -1004,15 +972,13 @@
             shape(part, 6 * D), shape(part, 2 * D), shape(part, 2 * FF), shape(4 * part, 2 * D),
             shape(2, 4 * part), shape(12, part), shape(4, part),
         ],
-        in_specs=[there] * 8,
+        in_specs=[here] * 8,
         out_specs=[there] * 6 + [here] * 3,
         scratch_shapes=[
-            vm((2, 256, D), BF), vm((2, 256, D), BF), vm((2, 256, D), BF),
-            vm((2, 16, 64, 128), BF), vm((2, 16, ROW, 128), BF), vm((2, 16, 64, 128), BF),
             vm((part, 6 * D), F32), vm((part, 2 * D), F32), vm((part, 2 * FF), F32), vm((4 * part, 2 * D), F32),
-            vm((row_len, D), BF), vm((row_len, D), F32), sem((8,)), sem((20,)),
+            sem((20,)),
         ],
-        compiler_params=pltpu.CompilerParams(vmem_limit_bytes=60 << 20),
+        compiler_params=pltpu.CompilerParams(vmem_limit_bytes=24 << 20),
         name="weight_grads",
     )(
         fq.reshape(2, 256, D), fu.reshape(2, 256, D), fa.reshape(2, 256, D),

time: 120 us -> 112 us (0.933)
  Pallas kernels: 119 us -> 111 us
    pallas_call x1, Pallas kernels: 110 us -> 106 us  [fast_device(): pl.pallas_call(main_kernel, out_shape=[jax.ShapeDtypeStruct((row_len, D),...]
    pallas_call x1, Pallas kernels: 9.03 us -> 5.84 us  [fast_device(): pl.pallas_call(grads_kernel, out_shape=[jax.ShapeDtypeStruct((row_len, D)...]
where the time goes in v4:
time: 112 us
  Pallas kernels  111 us (99%)
    pallas_call x1, Pallas kernels, fast_device(): pl.pallas_call(main_kernel, out_shape=[jax.ShapeDtypeStruct((row_len, D),...  106 us
    pallas_call x1, Pallas kernels, fast_device(): pl.pallas_call(grads_kernel, out_shape=[jax.ShapeDtypeStruct((row_len, D)...  5.84 us

profile of v4, /device:TPU:1, one launch (start us, length us, event | category | flops | bytes accessed | tf_op | source)
XLA Modules:
  0.0 112.3 jit_solution(6750476881237630957)
XLA Ops:
  0.6 105.6 %main_step.1 = (bf16[512,768]{1,0:T(8,128)(2,1)S(1)}, f32[512,768]{1,0:T(8,128)S(1)}, bf16[2,2,2,2,2,16,768]{6,5,4,3,2,1,0:T(8,128)(2,1)S(1)}, bf16[2,2,2,2,2,16...) custom-call(bf16[512,768]{1,0:T(8,128)(2,1)} %bitcast.22, ...), custom_call_target="tpu_custom_call" | custom-call | tf_op jit(solution)/shard_map/main_step/pallas_call | solution.py:937
  106.3 5.8 %weight_grads.1 = (bf16[512,768]{1,0:T(8,128)(2,1)}, f32[512,768]{1,0:T(8,128)}, f32[96,4608]{1,0:T(8,128)}, f32[96,1536]{1,0:T(8,128)}, f32[96,6144]{1,0:T(8,12...) custom-call(bf16[2,256,768]{2,1,0:T(8,128)(2,1)S(1)} %bitcast.16, ...), custom_call_target="tpu_custom_call" | custom-call | tf_op jit(solution)/shard_map/weight_grads/pallas_call | solution.py:968

commit v5 on v4

--- a/solution.py
+++ b/solution.py
@@ -299,6 +299,7 @@
     + [(3, 256 * i, 256) for i in range(3)]
 )
 WIDTHS = (3 * D, D, FF, D)
+THIN = (2, 5, 8)
 ROW = 16
 BLOCK = 256
 
@@ -317,10 +318,10 @@
 
 def main_kernel(
     x_in, seg_in, pos_in, bu_in, br_in, gr_in, w_mix, w_proj, w_up, w_down,
-    enc_out, drow_out, fq_ref, fu_ref, fa_ref, se_ref, sg_ref, sl_ref,
+    enc_out, drow_out, fq_ref, fu_ref, fa_ref, fb_ref, se_ref, sg_ref, sl_ref,
     x_ref, seg_ref, pos_ref, bu_ref, br_ref, gr_ref, first, enc_ref, drow_ref, wa, wd, sv_f, sv_ref, sv_all, q_s, k_s, v_s, a_s, mask_s, b_s, h_s, hl_s, g_s, sel_s,
-    cls_own, cls_all, cls_f, src_q, src_u, src_a, src_e, src_g, src_l,
-    ld, far_s, near_s, z_r, rel_s, x_s, x_r, y_s, y_r, c_s, c_r, sv_sem, sv_r, cz_s, cz_r, cp_s, cp_r, done,
+    cls_own, cls_all, cls_f, src_q, src_u, src_a, src_b, src_e, src_g, src_l,
+    ld, far_s, near_s, z_r, rel_s, x_s, x_r, y_s, y_r, c_s, c_r, o_s, o_r, sv_sem, sv_r, cz_s, cz_r, cp_s, cp_r, done,
     fl, fz_s, fz_r, ff_s, ff_r, fg_s, fg_r, fc_s, fc_r, s1_s, s1_r, s2_s, s2_r, s3_s, s3_r,
 ):
     sources = (w_mix, w_proj, w_up, w_down)
@@ -349,16 +350,14 @@
         loads[-1].start()
     barrier = pltpu.get_barrier_semaphore()
 
-    def peer_at(i):
-        p = lax.rem(me + i, 32)
-        return (p // 4, lax.rem(p, 4))
-
-    def greet(i, carry):
-        pl.semaphore_signal(barrier, inc=1, device_id=peer_at(i), device_id_type=MESH)
-        return carry
-
-    lax.fori_loop(1, 32, greet, 0)
-    pl.semaphore_wait(barrier, 31)
+    greeted = [device(lax.rem(z + r, 4), x, y, c) for r in (1, 2, 3)]
+    greeted += [device(lax.rem(z + r, 4), 1 - x, y, c) for r in (1, 2, 3)]
+    for r in range(1, 8):
+        to = lax.rem(plane + r, 8)
+        greeted.append((z * 2 + to // 4, lax.rem(to, 4)))
+    for peer in greeted:
+        pl.semaphore_signal(barrier, inc=1, device_id=peer, device_id_type=MESH)
+    pl.semaphore_wait(barrier, len(greeted))
 
     def remote(src, dst, s, r, peer):
         return pltpu.make_async_remote_copy(
@@ -368,11 +367,11 @@
     def arrived(ref, s, r):
         remote(ref, ref, s, r, to_x).wait_recv()
 
-    sent = []
+    state_sent = []
 
     def go(copy):
         copy.start()
-        sent.append(copy)
+        state_sent.append(copy)
 
     def dims(k):
         tensor, first, cols = PIECES[k]
@@ -417,15 +416,21 @@
         go(remote(ref, ref, x_s.at[k, 1], x_r.at[k, 1], to_x))
         go(remote(ref, ref, y_s.at[k, 0], y_r.at[k, 0], to_y))
         for j, zz in ((1, z_a), (2, z_b)):
-            whole = full(k, zz, x, None, c)
-            arrived(whole, near_s.at[k], z_r.at[k, j])
+            whole, part = full(k, zz, x, None, c), full(k, zz, x, y, c)
+            passed = part if k in THIN else whole
 
             @pl.when(inner == 1)
             def _():
-                remote(whole, whole, rel_s.at[k, j - 1], z_r.at[k, j], to_near).start()
-
-            ref = full(k, zz, x, y, c)
-            go(remote(ref, ref, x_s.at[k, 1 + j], x_r.at[k, 1 + j], to_x))
+                arrived(whole, near_s.at[k], z_r.at[k, j])
+                remote(passed, passed, rel_s.at[k, j - 1], z_r.at[k, j], to_near).start()
+
+            @pl.when(inner == 0)
+            def _():
+                arrived(passed, near_s.at[k], z_r.at[k, j])
+                if k in THIN:
+                    remote(part, part, o_s.at[k, j - 1], o_r.at[k, j - 1], to_y).start()
+
+            go(remote(part, part, x_s.at[k, 1 + j], x_r.at[k, 1 + j], to_x))
 
     def stage2(k):
         arrived(full(k, z, 1 - x, None, c), x_s.at[k, 0], x_r.at[k, 0])
@@ -438,6 +443,13 @@
         arrived(full(k, zn, x, 1 - y, c), y_s.at[k, 0], y_r.at[k, 0])
         for j in (1, 2, 3):
             arrived(full(k, planes[j], 1 - x, 1 - y, c), y_s.at[k, j], y_r.at[k, j])
+        if k in THIN:
+
+            @pl.when(inner == 0)
+            def _():
+                for j, zz in ((1, z_a), (2, z_b)):
+                    arrived(full(k, zz, x, 1 - y, c), o_s.at[k, j - 1], o_r.at[k, j - 1])
+
         local[k].wait()
         n = dims(k)[3]
         ref = held(k).at[:, pl.ds(pl.multiple_of(c * (n // 2), 128), n // 2)]
@@ -608,7 +620,7 @@
     xf, yf = x + (1 - c) * (1 - 2 * x), y + c * (1 - 2 * y)
     xg, yg = x + c * (1 - 2 * x), y + (1 - c) * (1 - 2 * y)
     to_f, to_g = device(z, xf, yf, c), device(z, xg, yg, c)
-    wholes = ((src_q, fq_ref), (src_u, fu_ref), (src_a, fa_ref))
+    wholes = ((src_q, fq_ref), (src_u, fu_ref), (src_a, fa_ref), (src_b, fb_ref))
     sliced = ((src_e, se_ref), (src_g, sg_ref), (src_l, sl_ref))
 
     def slot(ref):
@@ -651,7 +663,7 @@
         for r in range(1, 8):
             there = lax.rem(place + r, 8)
             go(remote(src.at[there], slot(dst), s1_s.at[i, r], s1_r.at[i, r], (there, other)))
-        copy = pltpu.make_async_copy(src.at[place], slot(dst), fl.at[3 + i])
+        copy = pltpu.make_async_copy(src.at[place], slot(dst), fl.at[4 + i])
         copy.start()
         copy.wait()
 
@@ -677,7 +689,7 @@
         return jnp.where(row16[:, : rows.shape[1]] < SEGS, rows, 0.0)
 
     def pack_early():
-        src_q[...] = top(state["q_r"].astype(F32)).astype(BF)
+        src_q[...] = top(state["q_r"].astype(F32))[:8].astype(BF)
         hl_f32, a_f32, x_f32 = (top(m.astype(F32)) for m in (state["hl_r"], state["a_r"], x_low))
         three = hl_f32 + pltpu.roll(a_f32, 4, 0) + pltpu.roll(x_f32, 8, 0)
         z_rows = dot_plain(state["p_low"], x_ref[...])
@@ -722,6 +734,29 @@
             for unit in after[i - 3]:
                 unit()
 
+    def drain():
+        for copy in gone:
+            copy.wait_send()
+
+        @pl.when(inner == 1)
+        def _():
+            for k in range(kinds):
+                for j, zz in ((1, z_a), (2, z_b)):
+                    ref = full(k, zz, x, y if k in THIN else None, c)
+                    remote(ref, ref, rel_s.at[k, j - 1], z_r.at[k, j], to_near).wait_send()
+
+        @pl.when(inner == 0)
+        def _():
+            for k in THIN:
+                for j, zz in ((1, z_a), (2, z_b)):
+                    ref = full(k, zz, x, y, c)
+                    remote(ref, ref, o_s.at[k, j - 1], o_r.at[k, j - 1], to_y).wait_send()
+
+        for i in range(1, 8):
+            sv_copy(i).wait_send()
+
+    gone = list(state_sent)
+    state_sent.clear()
     go(cls_z(1))
     go(cls_z(2))
     go(cls_z(3))
@@ -783,6 +818,8 @@
     dz1 = norm_back(state["unit1"], state["inv1"], state["g1"], dh)
     db = dz1.astype(BF)
     slice_3(1)
+    src_a[...] = (df.astype(F32) + pltpu.roll(db.astype(F32), 4, 0))[:8].astype(BF)
+    whole_z(2)
     da = dot_over_columns(db, wa[3]).astype(BF)
     a_wide = widen(da).astype(BF)
     d_p_rows = dot_over_columns(a_wide, v_s[...])
@@ -790,8 +827,8 @@
     ds = (p * (d_p_rows - jnp.sum(p * d_p_rows, axis=1, keepdims=True))).astype(BF)
     dq = narrow(dot_plain(ds, k_s[...]) * scaled).astype(BF)
     df_f, db_f, da_f, dq_f = (m.astype(F32) for m in (df, db, da, dq))
-    src_a[...] = (df_f + pltpu.roll(db_f, 4, 0) + pltpu.roll(dq_f, 8, 0) + pltpu.roll(da_f, 12, 0)).astype(BF)
-    whole_z(2)
+    src_b[...] = (dq_f + pltpu.roll(da_f, 4, 0))[:8].astype(BF)
+    whole_z(3)
     y_rows = dot_plain(ds, x_ref[...]) * scaled
     weight_sum = jnp.sum(state["p_low"].astype(F32), axis=1, keepdims=True)
     vec_bv = total(weight_sum * a_wide.astype(F32))
@@ -814,52 +851,48 @@
     left = jnp.concatenate([ds, state["p_low"], spot, spot], axis=0)
     right = jnp.concatenate([t_k, t_v, high, rest], axis=0)
     whole_f(2)
+    drain()
+    whole_f(3)
     whole_g(1)
+    whole_g(2)
     for n in range(0, D, BLOCK):
         drow_ref[:, n : n + BLOCK] = dot_over_rows(left, right[:, n : n + BLOCK])
     keep_row = pltpu.make_async_copy(drow_ref, drow_out, done.at[1])
     keep_row.start()
     slice_2(2)
-    whole_g(2)
+    whole_g(3)
     whole_c(1)
+    whole_c(2)
     slice_3(2)
-    whole_c(2)
+    whole_c(3)
+    for i in range(4):
+        whole_end(i)
     for i in range(3):
-        whole_end(i)
         slice_end(i)
     keep_enc.wait()
     keep_row.wait()
 
-    for copy in sent:
+    for copy in state_sent:
         copy.wait_send()
-    for k in range(kinds):
-
-        @pl.when(inner == 1)
-        def _():
-            for j, zz in ((1, z_a), (2, z_b)):
-                ref = full(k, zz, x, None, c)
-                remote(ref, ref, rel_s.at[k, j - 1], z_r.at[k, j], to_near).wait_send()
-
-    for i in range(1, 8):
-        sv_copy(i).wait_send()
 
 
 def grads_kernel(
-    fq_ref, fu_ref, fa_ref, se_ref, sg_ref, sl_ref, enc_ref, drow_ref,
+    fq_ref, fu_ref, fa_ref, fb_ref, se_ref, sg_ref, sl_ref, enc_ref, drow_ref,
     enc_out, drow_out, mix_out, proj_out, up_out, down_out, upb_ref, rowb_ref, gain_ref,
     mix_ref, proj_ref, up_ref, down_ref, put,
 ):
     place = lax.axis_index("dp")
     kind = iota((256, 128), 0) % ROW
     part = 96
-    wide_row, wide_col = iota((D, 256), 0), iota((D, 256), 1)
-    first_of = wide_row // 48 * ROW + wide_row % SEGS
+    wide_row, wide_col = iota((D, 128), 0), iota((D, 128), 1)
+    first_of = wide_row // 48 * 8 + wide_row % SEGS
     take_q = jnp.where(wide_col == first_of, 1.0, 0.0).astype(BF)
-    take_a = jnp.where(wide_col == first_of + 12, 1.0, 0.0).astype(BF)
+    take_a = jnp.where(wide_col == first_of + SEGS, 1.0, 0.0).astype(BF)
+    kind8 = iota((128, 128), 0) % 8
     own_head = (iota((D, D), 0) % 48) // SEGS == iota((D, D), 1) // HEAD_DIM
     kind16, col16 = iota((256, ROW), 0) % ROW, iota((256, ROW), 1)
-    again_row, again_col = iota((256, 256), 0), iota((256, 256), 1)
-    again = jnp.where(again_col == again_row // ROW * ROW + again_row % SEGS, 1.0, 0.0).astype(BF)
+    again_row, again_col = iota((256, 128), 0), iota((256, 128), 1)
+    again = jnp.where(again_col == again_row // ROW * 8 + again_row % SEGS, 1.0, 0.0).astype(BF)
     stores = []
 
     def store(src, dst):
@@ -873,9 +906,11 @@
     def keep(rows, lo, hi):
         return jnp.where((kind >= lo) & (kind < hi), rows, jnp.zeros((), BF))
 
-    three = [se_ref[t, :, 0:16, :].reshape(256, 128) for t in range(2)]
+    pair = [se_ref[t, :, 0:8, :].reshape(128, 128) for t in range(2)]
+    last = [se_ref[t, :, 8:16, :].reshape(128, 128) for t in range(2)]
+    none = jnp.zeros((), BF)
     for t in range(2):
-        four = dot_plain(again, three[t]).astype(BF)
+        four = dot_plain(again, pair[t]).astype(BF)
         for j in range(4):
             cols = slice(FF * t + D * j, FF * t + D * j + D)
             up_ref[:, cols] = dot_over_rows(keep(four, 4 * j, 4 * j + 4), fu_ref[t])[:part]
@@ -889,10 +924,10 @@
     for t in range(2):
         fa = fa_ref[t]
         cols = slice(D * t, D * t + D)
-        proj_ref[:, cols] = dot_over_rows(keep(three[t], 4, 8), fa)[:part]
+        proj_ref[:, cols] = dot_over_rows(jnp.where(kind8 >= SEGS, pair[t], none), fa)[:part]
         store(proj_ref.at[:, cols], proj_out.at[:, cols])
         first = slice(3 * D * t, 3 * D * t + D)
-        mix_ref[:, first] = dot_over_rows(keep(three[t], 8, 12), fa)[:part]
+        mix_ref[:, first] = dot_over_rows(jnp.where(kind8 < SEGS, last[t], none), fb_ref[t])[:part]
         store(mix_ref.at[:, first], mix_out.at[:, first])
         df = dot_plain(again, fa).astype(BF)
         g = sg_ref[t].reshape(256, 128)
@@ -901,7 +936,7 @@
             down_ref[at, cols] = dot_over_rows(keep(g, 4 * b, 4 * b + 4), df)
         store(down_ref.at[:, cols], down_out.at[:, cols])
     for t in range(2):
-        a_wide = jnp.where(own_head, dot_plain(take_a, fa_ref[t]), 0.0).astype(BF)
+        a_wide = jnp.where(own_head, dot_plain(take_a, fb_ref[t]), 0.0).astype(BF)
         gv = dot_over_rows(se_ref[t, :, 16:64, :].reshape(D, 128), a_wide)
         cols = slice(3 * D * t + 2 * D, 3 * D * t + 3 * D)
         mix_ref[:, cols] = gv[:part]
@@ -930,19 +965,19 @@
     vm = pltpu.VMEM
     part = b_rows.shape[0]
     kinds = len(PIECES)
-    fulls = jax.ShapeDtypeStruct((2, 2, 2, 2, 2, ROW, D), BF)
+    fulls = lambda r: jax.ShapeDtypeStruct((2, 2, 2, 2, 2, r, D), BF)
     row_len = text_rows.shape[1]
     here, there = pl.BlockSpec(memory_space=vm), pl.BlockSpec(memory_space=pl.ANY)
     slices = lambda r: jax.ShapeDtypeStruct((2, 2, 2, 2, 2, r, 128), BF)
-    encoded, d_rows, fq, fu, fa, se, sg, sl = pl.pallas_call(
+    encoded, d_rows, fq, fu, fa, fb, se, sg, sl = pl.pallas_call(
         main_kernel,
         out_shape=[
             jax.ShapeDtypeStruct((row_len, D), BF),
             jax.ShapeDtypeStruct((row_len, D), F32),
-            fulls, fulls, fulls, slices(64), slices(ROW), slices(64),
+            fulls(8), fulls(ROW), fulls(8), fulls(8), slices(64), slices(ROW), slices(64),
         ],
         in_specs=[pl.BlockSpec(memory_space=pltpu.HBM)] * 10,
-        out_specs=[there] * 2 + [here] * 6,
+        out_specs=[there] * 2 + [here] * 7,
         scratch_shapes=[
             vm((row_len, D), BF), vm((1, row_len), jnp.int32), vm((1, 64), jnp.int32),
             vm((2, 384), BF), vm((12, 96), BF), vm((4, 96), BF), sem((6,)),
@@ -953,12 +988,12 @@
             vm((row_len, row_len), F32), vm((row_len, D), F32), vm((row_len, D), F32), vm((row_len, D), BF),
             vm((4, row_len, D), BF), vm((D, 1024), BF),
             vm((SEGS, D), BF), vm((4, 8, SEGS, D), BF), vm((128, D), F32),
-            vm((ROW, D), BF), vm((ROW, D), BF), vm((ROW, D), BF),
+            vm((8, D), BF), vm((ROW, D), BF), vm((8, D), BF), vm((8, D), BF),
             vm((8, 64, 128), BF), vm((8, ROW, 128), BF), vm((8, 64, 128), BF),
             sem((kinds,)), sem((kinds,)), sem((kinds,)), sem((kinds, 3)), sem((kinds, 2)),
             sem((kinds, 4)), sem((kinds, 4)), sem((kinds, 4)), sem((kinds, 4)), sem((kinds,)), sem((kinds,)),
-            sem((8,)), sem((8,)), sem((4,)), sem((4,)), sem((8,)), sem((8,)), sem((2,)),
-            sem((6,)), sem((3, 4)), sem((3, 4)), sem((3,)), sem((3,)), sem((3, 2)), sem((3, 2)), sem((3,)), sem((3,)),
+            sem((kinds, 2)), sem((kinds, 2)), sem((8,)), sem((8,)), sem((4,)), sem((4,)), sem((8,)), sem((8,)), sem((2,)),
+            sem((7,)), sem((4, 4)), sem((4, 4)), sem((4,)), sem((4,)), sem((4, 2)), sem((4, 2)), sem((4,)), sem((4,)),
             sem((3, 8)), sem((3, 8)), sem((3,)), sem((3,)), sem((3,)), sem((3,)),
         ],
         compiler_params=pltpu.CompilerParams(collective_id=5, has_side_effects=True, vmem_limit_bytes=44 << 20),
@@ -972,7 +1007,7 @@
             shape(part, 6 * D), shape(part, 2 * D), shape(part, 2 * FF), shape(4 * part, 2 * D),
             shape(2, 4 * part), shape(12, part), shape(4, part),
         ],
-        in_specs=[here] * 8,
+        in_specs=[here] * 9,
         out_specs=[there] * 6 + [here] * 3,
         scratch_shapes=[
             vm((part, 6 * D), F32), vm((part, 2 * D), F32), vm((part, 2 * FF), F32), vm((4 * part, 2 * D), F32),
@@ -981,7 +1016,7 @@
         compiler_params=pltpu.CompilerParams(vmem_limit_bytes=24 << 20),
         name="weight_grads",
     )(
-        fq.reshape(2, 256, D), fu.reshape(2, 256, D), fa.reshape(2, 256, D),
+        fq.reshape(2, 128, D), fu.reshape(2, 256, D), fa.reshape(2, 128, D), fb.reshape(2, 128, D),
         se.reshape(2, 16, 64, 128), sg.reshape(2, 16, ROW, 128), sl.reshape(2, 16, 64, 128), encoded, d_rows,
     )
     encoded, d_rows, mix, proj, up, down, up_b, row_b, gain = grads

time: 112 us -> 110 us (0.982)
  Pallas kernels: 111 us -> 109 us
    pallas_call x1, Pallas kernels: 106 us -> 103 us  [fast_device(): pl.pallas_call(main_kernel, out_shape=[jax.ShapeDtypeStruct((row_len, D),...]
where the time goes in v5:
time: 110 us
  Pallas kernels  109 us (99%)
    pallas_call x1, Pallas kernels, fast_device(): pl.pallas_call(main_kernel, out_shape=[jax.ShapeDtypeStruct((row_len, D),...  103 us
    pallas_call x1, Pallas kernels, fast_device(): pl.pallas_call(grads_kernel, out_shape=[jax.ShapeDtypeStruct((row_len, D)...  5.69 us

profile of v5, /device:TPU:1, one launch (start us, length us, event | category | flops | bytes accessed | tf_op | source)
XLA Modules:
  0.0 109.9 jit_solution(9998723323397181056)
XLA Ops:
  0.6 103.4 %main_step.1 = (bf16[512,768]{1,0:T(8,128)(2,1)S(1)}, f32[512,768]{1,0:T(8,128)S(1)}, bf16[2,2,2,2,2,8,768]{6,5,4,3,2,1,0:T(8,128)(2,1)S(1)}, bf16[2,2,2,2,2,16,...) custom-call(bf16[512,768]{1,0:T(8,128)(2,1)} %bitcast.24, ...), custom_call_target="tpu_custom_call" | custom-call | tf_op jit(solution)/shard_map/main_step/pallas_call | solution.py:972
  104.0 5.7 %weight_grads.1 = (bf16[512,768]{1,0:T(8,128)(2,1)}, f32[512,768]{1,0:T(8,128)}, f32[96,4608]{1,0:T(8,128)}, f32[96,1536]{1,0:T(8,128)}, f32[96,6144]{1,0:T(8,12...) custom-call(bf16[2,128,768]{2,1,0:T(8,128)(2,1)S(1)} %bitcast.20, ...), custom_call_target="tpu_custom_call" | custom-call | tf_op jit(solution)/shard_map/weight_grads/pallas_call | solution.py:1003

commit v6 on v5

--- a/solution.py
+++ b/solution.py
@@ -403,8 +403,8 @@
     local = []
 
     def stage0(k):
+        go(remote(own(k, tower, y, c), full(k, z, x, y, c), near_s.at[k], z_r.at[k, 0], to_near))
         go(remote(own(k, 1 - tower, None, c), full(k, z, x, None, c), far_s.at[k], z_r.at[k, 2 - inner], to_far))
-        go(remote(own(k, tower, y, c), full(k, z, x, y, c), near_s.at[k], z_r.at[k, 0], to_near))
         go(remote(own(k, tower, None, c), full(k, z, x, None, c), x_s.at[k, 0], x_r.at[k, 0], to_x))
         copy = pltpu.make_async_copy(own(k, tower, None, c), full(k, z, x, None, c), ld.at[k])
         copy.start()

time: 110 us -> 109 us (level)
  no operation moved by 1% of the time
where the time goes in v6:
time: 109 us
  Pallas kernels  108 us (99%)
    pallas_call x1, Pallas kernels, fast_device(): pl.pallas_call(main_kernel, out_shape=[jax.ShapeDtypeStruct((row_len, D),...  102 us
    pallas_call x1, Pallas kernels, fast_device(): pl.pallas_call(grads_kernel, out_shape=[jax.ShapeDtypeStruct((row_len, D)...  5.69 us

profile of v6, /device:TPU:1, one launch (start us, length us, event | category | flops | bytes accessed | tf_op | source)
XLA Modules:
  0.0 108.9 jit_solution(7444899242366132439)
XLA Ops:
  0.6 102.3 %main_step.1 = (bf16[512,768]{1,0:T(8,128)(2,1)S(1)}, f32[512,768]{1,0:T(8,128)S(1)}, bf16[2,2,2,2,2,8,768]{6,5,4,3,2,1,0:T(8,128)(2,1)S(1)}, bf16[2,2,2,2,2,16,...) custom-call(bf16[512,768]{1,0:T(8,128)(2,1)} %bitcast.24, ...), custom_call_target="tpu_custom_call" | custom-call | tf_op jit(solution)/shard_map/main_step/pallas_call | solution.py:972
  103.0 5.7 %weight_grads.1 = (bf16[512,768]{1,0:T(8,128)(2,1)}, f32[512,768]{1,0:T(8,128)}, f32[96,4608]{1,0:T(8,128)}, f32[96,1536]{1,0:T(8,128)}, f32[96,6144]{1,0:T(8,12...) custom-call(bf16[2,128,768]{2,1,0:T(8,128)(2,1)S(1)} %bitcast.20, ...), custom_call_target="tpu_custom_call" | custom-call | tf_op jit(solution)/shard_map/weight_grads/pallas_call | solution.py:1003
